TPU v7x, 32 devices: a whole 2x2x4 slice. The times are simulated.
32 devices in a mesh: row: 8 (over z, y), col: 4 (over x, core).
Axes of the slice: x: 2, y: 2, z: 4, core: 2. Of those that a mesh axis runs over, the one named last changes fastest.
Arguments:
- inputs: bfloat16 [768, 8192], P('row', 'col'), may hold values from -16 to 16
- norm_gain: float32 [8192], P('col'), may hold values from 0.25 to 4
- w_gate: bfloat16 [8192, 28672], P('col', 'row'), may hold values from -0.09375 to 0.09375
- w_up: bfloat16 [8192, 28672], P('col', 'row'), may hold values from -0.09375 to 0.09375
- w_down: bfloat16 [28672, 8192], P('row', 'col'), may hold values from -0.050111483 to 0.050111483
- mask_gate: int32 [128, 448], P('col', 'row'), may hold values 0 or 1
- mask_up: int32 [128, 448], P('col', 'row'), may hold values 0 or 1
- mask_down: int32 [448, 128], P('row', 'col'), may hold values 0 or 1
- grad_out: bfloat16 [768, 8192], P('row', 'col'), may hold values from -5 to 5
Outputs:
- output: bfloat16 [768, 8192], P('row', 'col')
- grad_inputs: bfloat16 [768, 8192], P('row', 'col')
- grad_gain: float32 [8192], P('col')
- grad_w_gate: bfloat16 [8192, 28672], P('col', 'row')
- grad_w_up: bfloat16 [8192, 28672], P('col', 'row')
- grad_w_down: bfloat16 [28672, 8192], P('row', 'col')
All inputs are finite; a program needn't handle non-finite values. No bound on the sum of `mask_gate` or of `mask_up` or of `mask_down` on one device may be relied on, other than what follows from the above.
Results may differ from a plain program's by a relative error of at most 0.02.
Values may be sent and summed in bfloat16 or wider, within the bound.
No kernel may reach another device: no remote copies, remote signals or barrier semaphores. Data moves between devices by JAX's collectives and lax.ppermute only.
A program may use at most 256 MiB of HBM per device.

v0:
```python
import jax
import jax.numpy as jnp
from jax import lax
from jax.sharding import PartitionSpec as P

D = 8192
BLOCK = 64


epsilon = 1e-05


def expand_mask(weight, block_mask):
    mask_rows, mask_cols = block_mask.shape
    blocked = (
        weight.reshape(mask_rows, BLOCK, mask_cols, BLOCK)
        * block_mask.astype(jnp.bfloat16)[:, None, :, None]
    )
    return blocked.reshape(weight.shape)


def contract_rows(left, right):
    return lax.dot_general(
        left, right, (((0,), (0,)), ((), ())), preferred_element_type=jnp.float32
    )


def contract_cols(left, right):
    return lax.dot_general(
        left, right, (((1,), (1,)), ((), ())), preferred_element_type=jnp.float32
    )


def shards(inputs, norm_gain, w_gate, w_up, w_down, mask_gate, mask_up, mask_down, grad_out):
    gate_eff = expand_mask(w_gate, mask_gate)
    up_eff = expand_mask(w_up, mask_up)
    down_eff = expand_mask(w_down, mask_down)
    local_rows = inputs.shape[0]
    inputs_all, grads_all = (
        lax.all_gather(inputs, "row", axis=0, tiled=True),
        lax.all_gather(grad_out, "row", axis=0, tiled=True),
    )
    ff_width = w_gate.shape[1]
    inputs_wide = inputs_all.astype(jnp.float32)
    squares = lax.psum(jnp.sum(inputs_wide * inputs_wide, axis=1, keepdims=True), "col")
    inv_rms = lax.rsqrt(squares / D + epsilon)
    normed = inputs_wide * inv_rms
    hidden_in = (normed * norm_gain).astype(jnp.bfloat16)
    row_block = hidden_in
    projected = lax.psum_scatter(
        jnp.concatenate(
            [
                jnp.dot(row_block, gate_eff, preferred_element_type=jnp.float32),
                jnp.dot(row_block, up_eff, preferred_element_type=jnp.float32),
            ],
            axis=1,
        ).astype(jnp.bfloat16),
        "col",
        scatter_dimension=0,
        tiled=True,
    ).astype(jnp.float32)
    gate_value = projected[:, :ff_width]
    up_value = projected[:, ff_width:]
    sigmoid_gate = jax.nn.sigmoid(gate_value)
    silu_gate = gate_value * sigmoid_gate
    hidden = (silu_gate * up_value).astype(jnp.bfloat16)
    hidden_all = lax.all_gather(hidden, "col", axis=0, tiled=True)
    row_block = hidden_all
    mixed_out = lax.psum_scatter(
        jnp.dot(row_block, down_eff, preferred_element_type=jnp.float32).astype(jnp.bfloat16),
        "row",
        scatter_dimension=0,
        tiled=True,
    ).astype(jnp.float32)
    output = (inputs.astype(jnp.float32) + mixed_out).astype(jnp.bfloat16)
    grad_w_down = expand_mask(contract_rows(hidden_all, grads_all).astype(jnp.bfloat16), mask_down)
    row_block = grads_all
    d_hidden = lax.psum_scatter(
        contract_cols(row_block, down_eff).astype(jnp.bfloat16),
        "col",
        scatter_dimension=0,
        tiled=True,
    ).astype(jnp.float32)
    d_up = (d_hidden * silu_gate).astype(jnp.bfloat16)
    d_gate = (
        d_hidden * up_value * sigmoid_gate * (1.0 + gate_value * (1.0 - sigmoid_gate))
    ).astype(jnp.bfloat16)
    d_gate_all, d_up_all = (
        lax.all_gather(d_gate, "col", axis=0, tiled=True),
        lax.all_gather(d_up, "col", axis=0, tiled=True),
    )
    grad_w_gate = expand_mask(contract_rows(hidden_in, d_gate_all).astype(jnp.bfloat16), mask_gate)
    grad_w_up = expand_mask(contract_rows(hidden_in, d_up_all).astype(jnp.bfloat16), mask_up)
    d_norm_in = lax.psum_scatter(
        (contract_cols(d_gate_all, gate_eff) + contract_cols(d_up_all, up_eff)).astype(
            jnp.bfloat16
        ),
        "row",
        scatter_dimension=0,
        tiled=True,
    ).astype(jnp.float32)
    row_start = lax.axis_index("row") * local_rows
    normed_local = lax.dynamic_slice_in_dim(normed, row_start, local_rows, 0)
    inv_rms_local = lax.dynamic_slice_in_dim(inv_rms, row_start, local_rows, 0)
    gain_part = jnp.sum(d_norm_in * normed_local, axis=0)
    d_normed = d_norm_in * norm_gain
    inner_part = jnp.sum(d_normed * normed_local, axis=1, keepdims=True)
    row_inner = lax.psum(inner_part, "col") / D
    grad_gain = lax.psum(gain_part, "row")
    grad_inputs = (
        grad_out.astype(jnp.float32) + inv_rms_local * (d_normed - normed_local * row_inner)
    ).astype(jnp.bfloat16)
    return (output, grad_inputs, grad_gain, grad_w_gate, grad_w_up, grad_w_down)


def solution(mesh):
    in_specs = (
        P("row", "col"),
        P("col"),
        P("col", "row"),
        P("col", "row"),
        P("row", "col"),
        P("col", "row"),
        P("col", "row"),
        P("row", "col"),
        P("row", "col"),
    )
    out_specs = (
        P("row", "col"),
        P("row", "col"),
        P("col"),
        P("col", "row"),
        P("col", "row"),
        P("row", "col"),
    )
    return jax.shard_map(shards, mesh=mesh, in_specs=in_specs, out_specs=out_specs, check_vma=False)
```

profile of v0, /device:TPU:0, one launch (start us, length us, event | category | flops | bytes accessed | tf_op | source)
XLA Modules:
  0.0 633.5 jit_solution(2924886407965607107)
XLA Ops:
  7.2 0.7 all-gather.6.cloned.1.call-update
  7.9 0.7 all-gather.10.cloned.1.call-update
  8.7 0.7 convert_element_type.77
  9.4 10.0 %mul.142 = bf16[32,64,56,64]{3,2,1,0:T(8,128)(2,1)} broadcast(bf16[32,56]{1,0:T(8,128)(2,1)S(1)} %convert_element_type.77), dimensions={0,2} | broadcast | bytes 14683648 | tf_op jit(solution)/shard_map/mul | solution.py:16
  19.4 36.2 %mul.143 = bf16[2048,3584]{1,0:T(8,128)(2,1)} reshape(bf16[32,64,56,64]{3,2,1,0:T(8,128)(2,1)} %mul.142) | data formatting | bytes 29360128 | tf_op jit(solution)/shard_map/mul | solution.py:16
  55.7 10.1 %mul.139 = bf16[32,64,56,64]{3,2,1,0:T(8,128)(2,1)} broadcast(bf16[32,56]{1,0:T(8,128)(2,1)S(1)} %convert_element_type.76), dimensions={0,2} | broadcast | bytes 14683648 | tf_op jit(solution)/shard_map/mul | solution.py:16
  65.8 36.3 %mul.140 = bf16[2048,3584]{1,0:T(8,128)(2,1)} reshape(bf16[32,64,56,64]{3,2,1,0:T(8,128)(2,1)} %mul.139) | data formatting | bytes 29360128 | tf_op jit(solution)/shard_map/mul | solution.py:16
  102.1 18.6 %mul.144 = bf16[2048,3584]{1,0:T(8,128)(2,1)} multiply(bf16[2048,3584]{1,0:T(8,128)(2,1)} %param.12, bf16[2048,3584]{1,0:T(8,128)(2,1)} %mul.143) | non-fusion elementwise | flops 7340032 | bytes 44040192 | tf_op jit(solution)/shard_map/mul | solution.py:16
  120.7 1.1 copy-done
  121.8 14.7 %mul.141 = bf16[2048,3584]{1,0:T(8,128)(2,1)} multiply(bf16[2048,3584]{1,0:T(8,128)(2,1)} %param.11, bf16[2048,3584]{1,0:T(8,128)(2,1)S(1)} %copy-done) | non-fusion elementwise | flops 7340032 | bytes 44040192 | tf_op jit(solution)/shard_map/mul | solution.py:16
  136.6 2.7 fusion.3
  139.3 8.2 %psum.21 = f32[768,1]{0,1:T(1,128)S(1)} all-reduce(f32[768,1]{0,1:T(1,128)S(1)} %broadcast_in_dim.4), channel_id=1, replica_groups=mesh['row'=8,'col'=4] {'col'}, use_global_device_ids=true, to_apply=%region_1.0 | all-reduce | flops 768 | bytes 6144 | tf_op jit(solution)/shard_map/psum | solution.py:45
  147.5 0.6 fusion.23
  148.1 17.5 %convolution_convert_fusion.4 = bf16[768,3584]{1,0:T(8,128)(2,1)} fusion(bf16[2048,3584]{1,0:T(8,128)(2,1)} %mul.144, f32[2048]{0:T(1024)S(1)} %copy-done.5, f32[768]{0:T(1024)S(1)} %get-tuple-element.8, bf16[768,2048]{1,0:T(8,128)(2,1)} %all-gather.6.cloned.1.call-done), kind=kOutput, calls=%fused_computation.10 | convolution fusion | flops 11283333120 | bytes 23342080 | tf_op jit(solution)/shard_map/dot_general | solution.py:54
  165.6 13.5 %convolution_convert_fusion.5 = bf16[768,3584]{1,0:T(8,128)(2,1)} fusion(bf16[2048,3584]{1,0:T(8,128)(2,1)S(1)} %bitcast.26, f32[2048]{0:T(1024)S(1)} %copy-done.5, f32[768]{0:T(1024)S(1)} %get-tuple-element.8, bf16[768,2048]{1,0:T(8,128)(2,1)S(1)} %copy-done.1), kind=kOutput, calls=%fused_computation.11 | convolution fusion | flops 11283333120 | bytes 23342080 | tf_op jit(solution)/shard_map/dot_general | solution.py:53
  179.1 9.5 %pad_maximum_fusion = bf16[768,7168]{1,0:T(8,128)(2,1)} fusion(bf16[768,3584]{1,0:T(8,128)(2,1)} %convolution_convert_fusion.4, bf16[768,3584]{1,0:T(8,128)(2,1)} %convolution_convert_fusion.5), kind=kLoop, calls=%fused_computation.6 | loop fusion | flops 22020096 | bytes 22020096 | tf_op jit(solution)/shard_map/concatenate | solution.py:51
  188.6 0.2 reduce-scatter.9.cloned.1.call-start
  188.8 0.5 copy-done.8
  189.3 0.1 copy.15
  189.4 14.1 %mul.147 = bf16[56,64,32,64]{3,2,1,0:T(8,128)(2,1)} broadcast(bf16[56,32]{1,0:T(8,128)(2,1)S(1)} %copy.15), dimensions={0,2} | broadcast | bytes 14683648 | tf_op jit(solution)/shard_map/mul | solution.py:16
  203.6 40.8 %mul.148 = bf16[3584,2048]{1,0:T(8,128)(2,1)} reshape(bf16[56,64,32,64]{3,2,1,0:T(8,128)(2,1)} %mul.147) | data formatting | bytes 29360128 | tf_op jit(solution)/shard_map/mul | solution.py:16
  244.4 19.8 %fusion.4 = bf16[768,3584]{1,0:T(8,128)(2,1)} fusion(bf16[768,2048]{1,0:T(8,128)(2,1)} %all-gather.10.cloned.1.call-done, bf16[3584,2048]{1,0:T(8,128)(2,1)} %param.13, bf16[3584,2048]{1,0:T(8,128)(2,1)} %mul.148), kind=kOutput, calls=%fused_computation.15 | convolution fusion | flops 11284381696 | bytes 38010880 | tf_op jit(solution)/shard_map/dot_general | solution.py:29
  264.2 0.0 all-gather.12.cloned.1.call-start
  264.2 12.5 %reduce-scatter.5.cloned.1.call-done = bf16[192,7168]{1,0:T(8,128)(2,1)} async-done(((bf16[768,7168]{1,0:T(8,128)(2,1)}), bf16[192,7168]{1,0:T(8,128)(2,1)}) %reduce-scatter.5.cloned.1.call-update) | async-done | bytes 2752528 | tf_op jit(solution)/shard_map/reduce_scatter | solution.py:50
  276.7 4.8 convert_element_type.78
  281.5 50.6 %reduce-scatter.9.cloned.1.call-done = bf16[192,3584]{1,0:T(8,128)(2,1)} async-done(((bf16[768,3584]{1,0:T(8,128)(2,1)}), bf16[192,3584]{1,0:T(8,128)(2,1)}) %reduce-scatter.9.cloned.1.call-update) | async-done | bytes 1376272 | tf_op jit(solution)/shard_map/reduce_scatter | solution.py:78
  332.1 5.0 fusion.14
  337.2 0.5 all-gather.14.cloned.1.call-update
  337.8 0.7 all-gather.8.cloned.1.call-update
  338.5 40.7 %all-gather.12.cloned.1.call-done = bf16[768,3584]{1,0:T(8,128)(2,1)} async-done(((bf16[192,3584]{1,0:T(8,128)(2,1)}), bf16[768,3584]{1,0:T(8,128)(2,1)}) %all-gather.12.cloned.1.call-update) | async-done | bytes 5505040 | tf_op jit(solution)/shard_map/all_gather | solution.py:89
  379.2 18.3 %fusion.24 = f32[768,2048]{1,0:T(8,128)} fusion(bf16[768,3584]{1,0:T(8,128)(2,1)} %all-gather.12.cloned.1.call-done, bf16[2048,3584]{1,0:T(8,128)(2,1)} %mul.141), kind=kOutput, calls=%fused_computation.43 | convolution fusion | flops 11274289152 | bytes 26476544 | tf_op jit(solution)/shard_map/dot_general | solution.py:29
  397.5 25.1 %all-gather.14.cloned.1.call-done = bf16[768,3584]{1,0:T(8,128)(2,1)} async-done(((bf16[192,3584]{1,0:T(8,128)(2,1)}), bf16[768,3584]{1,0:T(8,128)(2,1)}) %all-gather.14.cloned.1.call-update) | async-done | bytes 5505040 | tf_op jit(solution)/shard_map/all_gather | solution.py:90
  422.6 18.5 %add_convert_fusion = bf16[768,2048]{1,0:T(8,128)(2,1)} fusion(f32[768,2048]{1,0:T(8,128)} %fusion.24, bf16[768,3584]{1,0:T(8,128)(2,1)} %all-gather.14.cloned.1.call-done, bf16[2048,3584]{1,0:T(8,128)(2,1)} %mul.144), kind=kOutput, calls=%fused_computation.13 | convolution fusion | flops 11277434880 | bytes 29622272 | tf_op jit(solution)/shard_map/dot_general | solution.py:29
  441.1 0.3 reduce-scatter.7.cloned.1.call-start
  441.4 0.8 dynamic-slice_bitcast_fusion
  442.1 3.1 convert_multiply_fusion
  445.3 20.8 %all-gather.8.cloned.1.call-done = bf16[768,3584]{1,0:T(8,128)(2,1)} async-done(((bf16[192,3584]{1,0:T(8,128)(2,1)}), bf16[768,3584]{1,0:T(8,128)(2,1)}) %all-gather.8.cloned.1.call-update) | async-done | bytes 5505040 | tf_op jit(solution)/shard_map/all_gather | solution.py:67
  466.0 19.7 %fusion.8 = bf16[768,2048]{1,0:T(8,128)(2,1)} fusion(bf16[768,3584]{1,0:T(8,128)(2,1)} %all-gather.8.cloned.1.call-done, bf16[3584,2048]{1,0:T(8,128)(2,1)} %param.13, bf16[3584,2048]{1,0:T(8,128)(2,1)} %mul.148), kind=kOutput, calls=%fused_computation.21 | convolution fusion | flops 11283202048 | bytes 38010880 | tf_op jit(solution)/shard_map/dot_general | solution.py:70
  485.8 18.6 %fusion = bf16[2048,3584]{1,0:T(8,128)(2,1)} fusion(bf16[2048,3584]{1,0:T(8,128)(2,1)} %mul.140, bf16[768,3584]{1,0:T(8,128)(2,1)} %all-gather.12.cloned.1.call-done, f32[2048]{0:T(1024)S(1)} %copy-done.6, f32[768]{0:T(1024)S(1)} %get-tuple-element.8, bf16[768,2048]{1,0:T(8,128)(2,1)S(1)} %copy-done.2), kind=kOutput, calls=%fused_computation.3 | convolution fusion | flops 11295260672 | bytes 38022144 | tf_op jit(solution)/shard_map/dot_general | solution.py:23
  504.4 18.7 %fusion.1 = bf16[2048,3584]{1,0:T(8,128)(2,1)} fusion(bf16[2048,3584]{1,0:T(8,128)(2,1)} %mul.143, bf16[768,3584]{1,0:T(8,128)(2,1)} %all-gather.14.cloned.1.call-done, f32[2048]{0:T(1024)S(1)} %copy-done.6, f32[768]{0:T(1024)S(1)} %get-tuple-element.8, bf16[768,2048]{1,0:T(8,128)(2,1)S(1)} %copy-done.2), kind=kOutput, calls=%fused_computation.4 | convolution fusion | flops 11295260672 | bytes 38022144 | tf_op jit(solution)/shard_map/dot_general | solution.py:23
  523.1 20.3 %fusion.2 = bf16[3584,2048]{1,0:T(8,128)(2,1)} fusion(bf16[3584,2048]{1,0:T(8,128)(2,1)} %mul.148, bf16[768,3584]{1,0:T(8,128)(2,1)} %all-gather.8.cloned.1.call-done, bf16[768,2048]{1,0:T(8,128)(2,1)} %all-gather.10.cloned.1.call-done), kind=kOutput, calls=%fused_computation.5 | convolution fusion | flops 11288969216 | bytes 38010880 | tf_op jit(solution)/shard_map/dot_general | solution.py:23
  543.4 1.1 reduce-scatter.11.cloned.1.call-done
  544.5 1.5 fusion.22
  546.0 5.8 psum.22
  551.8 22.4 %psum.23 = f32[2048]{0:T(1024)} all-reduce(f32[2048]{0:T(1024)S(1)} %get-tuple-element.6), channel_id=1, replica_groups=mesh['row'=8,'col'=4] {'row'}, use_global_device_ids=true, to_apply=%region_9.0 | all-reduce | flops 2048 | bytes 16384 | tf_op jit(solution)/shard_map/psum | solution.py:109
  574.2 48.2 %reduce-scatter.7.cloned.1.call-done = bf16[96,2048]{1,0:T(8,128)(2,1)} async-done(((bf16[768,2048]{1,0:T(8,128)(2,1)}), bf16[96,2048]{1,0:T(8,128)(2,1)}) %reduce-scatter.7.cloned.1.call-update) | async-done | bytes 393232 | tf_op jit(solution)/shard_map/reduce_scatter | solution.py:69
  622.5 1.8 add_convert_fusion.1
  624.3 2.3 fusion.21
  (42 shorter events, 0.4 us)
Async XLA Ops:
  7.2 129.4 %all-gather.6.cloned.1.call-start = ((), (), s32[]{:S(2)}) async-start(), calls=%async_computation.4 | async-start | bytes 3538944 | tf_op jit(solution)/shard_map/all_gather | solution.py:40
  7.9 236.5 %all-gather.10.cloned.1.call-start = ((), (), s32[]{:S(2)}) async-start(), calls=%async_computation.8 | async-start | bytes 3538944 | tf_op jit(solution)/shard_map/all_gather | solution.py:41
  8.6 268.0 %reduce-scatter.5.cloned.1.call-start = ((), (), s32[]{:S(2)}) async-start(), calls=%async_computation.5 | async-start | bytes 13762560 | tf_op jit(solution)/shard_map/reduce_scatter | solution.py:50
  19.4 36.2 %copy-start.7 = (s32[32,56]{1,0:T(8,128)S(1)}, s32[32,56]{1,0:T(8,128)}, u32[]{:S(2)}) copy-start(s32[32,56]{1,0:T(8,128)} %param.14) | copy-start | bytes 21508
  102.1 19.7 %copy-start = (bf16[2048,3584]{1,0:T(8,128)(2,1)S(1)}, bf16[2048,3584]{1,0:T(8,128)(2,1)}, u32[]{:S(2)}) copy-start(bf16[2048,3584]{1,0:T(8,128)(2,1)} %mul.140) | copy-start | bytes 44040196
  121.8 26.2 %copy-start.5 = (f32[2048]{0:T(1024)S(1)}, f32[2048]{0:T(1024)}, u32[]{:S(2)}) copy-start(f32[2048]{0:T(1024)} %param.10) | copy-start | bytes 24580
  136.6 29.0 %slice-start = ((s8[14680064]{0:T(1024)(128)(4,1)}), s8[2097152]{0:T(1024)(128)(4,1)S(1)}, s32[]{:S(2)}) async-start(s8[14680064]{0:T(1024)(128)(4,1)} %bitcast.25), calls=%async_computation.13 | async-start | bytes 4194304
  148.1 17.5 %slice-start.1 = ((s8[14680064]{0:T(1024)(128)(4,1)}), s8[4194304]{0:T(1024)(128)(4,1)S(1)}, s32[]{:S(2)}) async-start(s8[14680064]{0:T(1024)(128)(4,1)} %bitcast.25), calls=%async_computation.14 | async-start | bytes 8388608
  148.1 17.5 %slice-start.2 = ((s8[14680064]{0:T(1024)(128)(4,1)}), s8[4194304]{0:T(1024)(128)(4,1)S(1)}, s32[]{:S(2)}) async-start(s8[14680064]{0:T(1024)(128)(4,1)} %bitcast.25), calls=%async_computation.15 | async-start | bytes 8388608
  148.1 17.5 %slice-start.3 = ((s8[14680064]{0:T(1024)(128)(4,1)}), s8[4194304]{0:T(1024)(128)(4,1)S(1)}, s32[]{:S(2)}) async-start(s8[14680064]{0:T(1024)(128)(4,1)} %bitcast.25), calls=%async_computation.16 | async-start | bytes 8388608
  148.1 17.5 %copy-start.1 = (bf16[768,2048]{1,0:T(8,128)(2,1)S(1)}, bf16[768,2048]{1,0:T(8,128)(2,1)}, u32[]{:S(2)}) copy-start(bf16[768,2048]{1,0:T(8,128)(2,1)} %all-gather.6.cloned.1.call-done) | copy-start | bytes 9437188
  188.6 0.7 copy-start.8
  188.6 143.5 %reduce-scatter.9.cloned.1.call-start = ((), (), s32[]{:S(2)}) async-start(), calls=%async_computation.9 | async-start | bytes 6881280 | tf_op jit(solution)/shard_map/reduce_scatter | solution.py:78
  264.2 115.1 %all-gather.12.cloned.1.call-start = ((), (), s32[]{:S(2)}) async-start(), calls=%async_computation.10 | async-start | bytes 6881280 | tf_op jit(solution)/shard_map/all_gather | solution.py:89
  337.1 85.4 %all-gather.14.cloned.1.call-start = ((), (), s32[]{:S(2)}) async-start(), calls=%async_computation.11 | async-start | bytes 6881280 | tf_op jit(solution)/shard_map/all_gather | solution.py:90
  337.7 128.3 %all-gather.8.cloned.1.call-start = ((), (), s32[]{:S(2)}) async-start(), calls=%async_computation.6 | async-start | bytes 6881280 | tf_op jit(solution)/shard_map/all_gather | solution.py:67
  338.5 206.0 %reduce-scatter.11.cloned.1.call-start = ((), (), s32[]{:S(2)}) async-start(), calls=%async_computation.12 | async-start | bytes 3538944 | tf_op jit(solution)/shard_map/reduce_scatter | solution.py:94
  397.5 44.7 %copy-start.2 = (bf16[768,2048]{1,0:T(8,128)(2,1)S(1)}, bf16[768,2048]{1,0:T(8,128)(2,1)}, u32[]{:S(2)}) copy-start(bf16[768,2048]{1,0:T(8,128)(2,1)} %all-gather.6.cloned.1.call-done) | copy-start | bytes 9437188
  441.1 181.3 %reduce-scatter.7.cloned.1.call-start = ((), (), s32[]{:S(2)}) async-start(), calls=%async_computation.7 | async-start | bytes 3538944 | tf_op jit(solution)/shard_map/reduce_scatter | solution.py:69
  445.3 40.5 %copy-start.6 = (f32[2048]{0:T(1024)S(1)}, f32[2048]{0:T(1024)}, u32[]{:S(2)}) copy-start(f32[2048]{0:T(1024)} %param.10) | copy-start | bytes 24580
  523.1 99.3 %copy-start.3 = (bf16[96,2048]{1,0:T(8,128)(2,1)S(1)}, bf16[96,2048]{1,0:T(8,128)(2,1)}, u32[]{:S(2)}) copy-start(bf16[96,2048]{1,0:T(8,128)(2,1)} %param.9) | copy-start | bytes 1179652
  523.1 101.2 %copy-start.4 = (bf16[96,2048]{1,0:T(8,128)(2,1)S(1)}, bf16[96,2048]{1,0:T(8,128)(2,1)}, u32[]{:S(2)}) copy-start(bf16[96,2048]{1,0:T(8,128)(2,1)} %param.17) | copy-start | bytes 1179652
Sparse Core Ops, SparseCore 0:
  10.2 62.7 all-gather.5
  75.1 58.7 all-gather.9
  188.7 87.8 reduce-scatter.4
  279.1 53.0 reduce-scatter.8
  337.3 41.8 all-gather.11
  380.6 41.8 all-gather.13
  424.1 41.8 all-gather.7
  469.6 74.8 reduce-scatter.10
  548.1 74.3 reduce-scatter.6
where the time goes:
time: 644 us; the launch traced here: 634 us
  waiting for transfers between devices  202 us (31%)
  matrix products  165 us (26%)
  local copies, waits for them, and re-layouts  150 us (23%)
  other arithmetic  65.4 us (10%)
  blocking collectives  36.4 us (6%)
  between operations  14.4 us (2%)
    mul x6, local copies, waits for them, and re-layouts, expand_mask(): weight.reshape(mask_rows, BLOCK, mask_cols, BLOCK)  148 us
    dot_general x3, matrix products, contract_rows(): lax.dot_general(left, right, (((0,), (0,)), ((), ())), preferred_element_...  57.6 us
    dot_general x3, matrix products, contract_cols(): lax.dot_general(left, right, (((1,), (1,)), ((), ())), preferred_element_...  56.6 us
    reduce_scatter x1, waiting for transfers between devices, shards(): lax.psum_scatter(contract_cols(row_block, down_eff).astype(jnp.bfloat16),...  50.6 us
    reduce_scatter x1, waiting for transfers between devices, shards(): lax.psum_scatter(jnp.dot(row_block, down_eff, preferred_element_type=jnp....  48.2 us
    all_gather x1, waiting for transfers between devices, shards(): lax.all_gather(d_gate, 'col', axis=0, tiled=True)  40.7 us
    mul x2, other arithmetic, expand_mask(): weight.reshape(mask_rows, BLOCK, mask_cols, BLOCK)  33.3 us
    all_gather x1, waiting for transfers between devices, shards(): lax.all_gather(d_up, 'col', axis=0, tiled=True)  25.1 us
  transfers between devices with their start and end apart: 9, of which 7 were waited for; matrix products, arithmetic and copies ran while one was open for 58% of the time, Pallas kernels for 0%

commit v1 on v0

v1 whole, which is shorter than its diff:
```python
import functools

import jax
import jax.numpy as jnp
from jax import lax
from jax.experimental import pallas as pl
from jax.experimental.pallas import tpu as pltpu
from jax.sharding import PartitionSpec as P

BLOCK = 64
CORES = 2
epsilon = 1e-05
bf16 = jnp.bfloat16
f32 = jnp.float32


def tile_of(size, limit):
    best = 128
    for tile in range(128, limit + 1, 128):
        if size % tile == 0:
            best = tile
    return best


def lanes(block_mask):
    rows, cols = block_mask.shape
    wide = jnp.broadcast_to(block_mask.astype(f32)[:, :, None], (rows, cols, BLOCK))
    return lax.optimization_barrier(wide.reshape(rows, cols * BLOCK))


def dot(left, right, left_axis, right_axis):
    return lax.dot_general(
        left, right, (((left_axis,), (right_axis,)), ((), ())), preferred_element_type=f32
    )


def keep_rows(mask_ref, row, cols):
    keep = jnp.broadcast_to(mask_ref[pl.ds(row, 1), :], (16, cols))
    return keep.astype(bf16)[None]


def block_rows(value, keep):
    cols = value.shape[1]
    return (value.reshape(BLOCK // 16, 16, cols) * keep).reshape(BLOCK, cols)


def whole(array):
    return pl.BlockSpec(array.shape, lambda *_: (0,) * array.ndim)


def call(body, grid, scalars, operands, in_specs, out_specs, out_shape, scratch,
         flops, moved, aliases=None):
    return pl.pallas_call(
        body,
        grid_spec=pltpu.PrefetchScalarGridSpec(
            num_scalar_prefetch=1,
            grid=grid,
            in_specs=in_specs,
            out_specs=out_specs,
            scratch_shapes=scratch,
        ),
        out_shape=out_shape,
        input_output_aliases=aliases or {},
        compiler_params=pltpu.CompilerParams(vmem_limit_bytes=60 << 20),
        cost_estimate=pl.CostEstimate(
            flops=int(flops), bytes_accessed=int(moved), transcendentals=0),
    )(scalars, *operands)


class Plan:
    def __init__(self, width):
        self.half = width // CORES
        self.tile = tile_of(self.half, 256)
        self.count = self.half // self.tile
        first = (self.count + 1) // 2
        self.chunks = [(0, first)]
        if self.count > first:
            self.chunks.append((first, self.count - first))


def mask_columns(plan, chunk, scalars, w_gate, w_up, gate_lanes, up_lanes):
    first, steps = chunk
    depth, tile = w_gate.shape[0], plan.tile

    def body(_, g_ref, u_ref, gm_ref, um_ref, out_ref):
        for w_ref, k_ref, lane in ((g_ref, gm_ref, 0), (u_ref, um_ref, tile)):
            for index in range(depth // BLOCK):
                span = pl.ds(index * BLOCK, BLOCK)
                out_ref[span, lane:lane + tile] = block_rows(
                    w_ref[span, :], keep_rows(k_ref, index, tile))

    column = lambda h, j, s: (0, h * plan.count + first + j)
    weight = pl.BlockSpec((depth, tile), column)
    mask = pl.BlockSpec((depth // BLOCK, tile), column)
    return call(
        body, (CORES, steps), scalars, (w_gate, w_up, gate_lanes, up_lanes),
        [weight, weight, mask, mask],
        pl.BlockSpec((depth, 2 * tile), lambda h, j, s: (0, h * steps + j)),
        jax.ShapeDtypeStruct((depth, CORES * steps * 2 * tile), bf16), [],
        0, 8 * CORES * depth * steps * tile)


def mask_rows(plan, chunk, scalars, w_down, down_lanes):
    first, steps = chunk
    depth, tile = w_down.shape[1], plan.tile

    def body(_, w_ref, k_ref, out_ref):
        start = pl.program_id(0) * plan.count + first + pl.program_id(1)
        for index in range(tile // BLOCK):
            span = pl.ds(index * BLOCK, BLOCK)
            keep = keep_rows(k_ref, start * (tile // BLOCK) + index, depth)
            out_ref[span, :] = block_rows(w_ref[span, :], keep)

    return call(
        body, (CORES, steps), scalars, (w_down, down_lanes),
        [pl.BlockSpec((tile, depth), lambda h, j, s: (h * plan.count + first + j, 0)),
         whole(down_lanes)],
        pl.BlockSpec((tile, depth), lambda h, j, s: (h * steps + j, 0)),
        jax.ShapeDtypeStruct((CORES * steps * tile, depth), bf16), [],
        0, 4 * CORES * depth * steps * tile)


def project(side, halves, tokens, weight, added=None):
    rows, depth = tokens.shape
    width = weight.shape[1] // CORES
    tile = tile_of(width, 512)
    steps = width // tile

    def body(_, x_ref, w_ref, *rest):
        value = dot(x_ref[...], w_ref[...], 1, 0)
        if added is not None:
            value += rest[0][...].astype(f32)
        rest[-1][...] = value.astype(bf16)

    out = pl.BlockSpec((rows, tile), lambda i, h: (0, i))
    extra = () if added is None else (added,)
    return call(
        body, (steps,), halves, (tokens, weight, *extra),
        [whole(tokens), pl.BlockSpec((depth, tile), lambda i, h: (0, h[side] * steps + i))]
        + [out] * len(extra),
        out, jax.ShapeDtypeStruct((rows, width), bf16), [],
        2 * rows * depth * width, 2 * depth * width + 2 * rows * depth + 2 * rows * width)


def back_project(side, halves, tokens, weight, added=None):
    rows, depth = tokens.shape
    width = weight.shape[0] // CORES
    tile = tile_of(width, 256)
    steps = width // tile

    def body(_, g_ref, w_ref, *rest):
        value = dot(g_ref[...], w_ref[...], 1, 1)
        if added is not None:
            value += rest[0][...].astype(f32)
        rest[-1][...] = value.astype(bf16)

    out = pl.BlockSpec((rows, tile), lambda i, h: (0, i))
    extra = () if added is None else (added,)
    return call(
        body, (steps,), halves, (tokens, weight, *extra),
        [whole(tokens), pl.BlockSpec((tile, depth), lambda i, h: (h[side] * steps + i, 0))]
        + [out] * len(extra),
        out, jax.ShapeDtypeStruct((rows, width), bf16), [],
        2 * rows * depth * width, 2 * depth * width + 2 * rows * depth + 2 * rows * width)


def activate(plan, scalars, scale, pieces, grad_pieces, start, stop):
    tile = plan.tile
    width = pieces[0][1][0].shape[1] // 2
    with_grad = grad_pieces is not None
    cuts = {start, stop}
    listed = list(pieces) + (list(grad_pieces) if with_grad else [])
    for first, arrays in listed:
        cuts |= {first, first + arrays[0].shape[0]}
    cuts = sorted(cut for cut in cuts if start <= cut <= stop)
    operands, in_specs = [scale], [whole(scale)]
    for first, arrays in pieces:
        operands += arrays
        in_specs += [pl.BlockSpec((a.shape[0], 2 * tile), lambda j, s: (0, j)) for a in arrays]
    for first, arrays in grad_pieces or ():
        operands += arrays
        in_specs += [pl.BlockSpec((a.shape[0], tile), lambda j, s: (0, j)) for a in arrays]
    rows = stop - start
    wide = 2 * tile if with_grad else tile

    def summed(refs, groups, low, high, lane):
        position = 0
        for first, arrays in groups:
            if first <= low and high <= first + arrays[0].shape[0]:
                total = None
                for ref in refs[position:position + len(arrays)]:
                    term = ref[low - first:high - first, lane:lane + tile].astype(f32)
                    total = term if total is None else total + term
                return total
            position += len(arrays)

    def body(_, s_ref, *refs):
        out_ref = refs[-1]
        count = sum(len(arrays) for _, arrays in pieces)
        for low, high in zip(cuts[:-1], cuts[1:]):
            span = slice(low - start, high - start)
            factor = s_ref[low:high, :]
            gate = summed(refs, pieces, low, high, 0) * factor
            up = summed(refs, pieces, low, high, tile) * factor
            sigma = jax.nn.sigmoid(gate)
            if with_grad:
                grad = summed(refs[count:], grad_pieces, low, high, 0)
                d_gate = grad * up * sigma * (1.0 + gate * (1.0 - sigma))
                out_ref[span, :tile] = d_gate.astype(bf16)
                out_ref[span, tile:] = (grad * (gate * sigma)).astype(bf16)
            else:
                out_ref[span, :] = (gate * sigma * up).astype(bf16)

    return call(
        body, (width // tile,), scalars, operands, in_specs,
        pl.BlockSpec((rows, wide), lambda j, s: (0, j)),
        jax.ShapeDtypeStruct((rows, width // tile * wide), bf16), [],
        0, 2 * sum(a.size for a in operands) + 2 * rows * width)


def down_product(halves, hidden, weights):
    rows, depth = hidden[0][0].shape[0], weights[0].shape[1]
    tile = tile_of(depth, 256)
    operands, in_specs = [], []
    for pair, weight in zip(hidden, weights):
        width = weight.shape[0] // CORES
        for side, value in enumerate(pair):
            operands += [value, weight]
            in_specs += [whole(value), pl.BlockSpec(
                (width, tile), lambda i, h, side=side: (h[side], i))]

    def body(_, *refs):
        value = None
        for h_ref, w_ref in zip(refs[:-1:2], refs[1:-1:2]):
            term = dot(h_ref[...], w_ref[...], 1, 0)
            value = term if value is None else value + term
        refs[-1][...] = value.astype(bf16)

    total = sum(weight.size for weight in weights)
    return call(
        body, (depth // tile,), halves, operands, in_specs,
        pl.BlockSpec((rows, tile), lambda i, h: (0, i)),
        jax.ShapeDtypeStruct((rows, depth), bf16), [],
        2 * rows * total, 2 * total + 2 * rows * (total // depth + depth))


def input_cotangent(halves, pair, weight, start, added, dtype):
    rows = pair[0].shape[0]
    depth, width = weight.shape[0], weight.shape[1] // CORES
    tile = tile_of(depth, 256)
    side = [pl.BlockSpec((tile, width), lambda i, h: (i, h[0])),
            pl.BlockSpec((tile, width), lambda i, h: (i, h[1]))]
    extra = () if added is None else (added,)

    def body(_, m_ref, o_ref, wm_ref, wo_ref, *rest):
        value = dot(m_ref[...], wm_ref[...], 1, 1) + dot(o_ref[...], wo_ref[...], 1, 1)
        if added is not None:
            value += rest[0][start:start + rows, :]
        rest[-1][...] = value.astype(dtype)

    return call(
        body, (depth // tile,), halves, (*pair, weight, weight, *extra),
        [whole(pair[0]), whole(pair[1]), *side]
        + [pl.BlockSpec((a.shape[0], tile), lambda i, h: (0, i)) for a in extra],
        pl.BlockSpec((rows, tile), lambda i, h: (0, i)),
        jax.ShapeDtypeStruct((rows, depth), dtype), [],
        2 * rows * weight.size, 2 * weight.size + 4 * rows * width + 4 * rows * depth)


def turn(scalars, scale, pieces):
    rows, depth = scale.shape[0], pieces[0].shape[1]
    tile = tile_of(depth, 256)

    def body(_, s_ref, *refs):
        out_ref, scratch = refs[-2:]
        first = 0
        for ref in refs[:-2]:
            span = slice(first, first + ref.shape[0])
            scratch[span, :] = (ref[...].astype(f32) * s_ref[span, :]).astype(bf16)
            first += ref.shape[0]
        out_ref[...] = scratch[...].T

    return call(
        body, (depth // tile,), scalars, (scale, *pieces),
        [whole(scale)] + [pl.BlockSpec((p.shape[0], tile), lambda i, s: (0, i)) for p in pieces],
        pl.BlockSpec((tile, rows), lambda i, s: (i, 0)),
        jax.ShapeDtypeStruct((depth, rows), bf16), [pltpu.VMEM((rows, tile), bf16)],
        0, 4 * rows * depth)


def gate_up_grads(plan, chunk, halves, turned, mine, other, gate_lanes, up_lanes, earlier,
                  single=None):
    first, steps = chunk
    skipped = 0
    if single is not None:
        first, steps, skipped = first + single, 1, single
    depth, rows = turned.shape
    tile = plan.tile
    n_mine = len(mine)

    def body(_, x_ref, *refs):
        sides = refs[:n_mine], refs[n_mine:2 * n_mine]
        masks = refs[2 * n_mine:2 * n_mine + 2]
        outs, scratch = refs[-3:-1], refs[-1]

        def collect(pieces):
            row = 0
            for ref in pieces:
                scratch[row:row + ref.shape[0], :] = ref[...]
                row += ref.shape[0]

        pl.when(pl.program_id(0) == 0)(lambda: collect(sides[0]))
        pl.when(pl.program_id(0) == 1)(lambda: collect(sides[1]))
        for index in range(2):
            right = scratch[:, index * tile:(index + 1) * tile]
            value = dot(x_ref[...], right, 1, 0).astype(bf16)
            for block in range(depth // BLOCK):
                span = slice(block * BLOCK, (block + 1) * BLOCK)
                outs[index][span, :] = block_rows(
                    value[span, :], keep_rows(masks[index], block, tile))

    column = lambda p, j, h: (0, h[p] * plan.count + first + j)
    in_specs = [whole(turned)]
    in_specs += [pl.BlockSpec((a.shape[0], 2 * tile), lambda p, j, h: (
        0, skipped + jnp.where(p == 0, j, steps - 1))) for a in mine]
    in_specs += [pl.BlockSpec((a.shape[0], 2 * tile), lambda p, j, h: (
        0, skipped + jnp.where(p == 0, 0, j))) for a in other]
    in_specs += [pl.BlockSpec((depth // BLOCK, tile), column)] * 2
    out = pl.BlockSpec((depth, tile), column)
    shape = jax.ShapeDtypeStruct((depth, plan.half * CORES), bf16)
    operands = [turned, *mine, *other, gate_lanes, up_lanes]
    aliases = None
    if earlier is not None:
        aliases = {len(operands) + 1: 0, len(operands) + 2: 1}
        operands += earlier
        in_specs += [pl.BlockSpec(memory_space=pl.ANY)] * 2
    return call(
        body, (CORES, steps), halves, operands, in_specs, [out, out], [shape, shape],
        [pltpu.VMEM((rows, 2 * tile), bf16)],
        8 * rows * depth * steps * tile,
        2 * rows * depth + 8 * rows * steps * tile + 8 * depth * steps * tile, aliases)


def down_grads(plan, halves, hidden, grads, down_lanes):
    rows, depth = hidden[0][0].shape[0], grads[0].shape[1]
    tile = tile_of(depth, 256)
    operands, places = [], []
    for pair, (first, steps) in zip(hidden, plan.chunks):
        for side, value in enumerate(pair):
            operands.append(value)
            places.append((side, first * plan.tile))
    count = len(operands)
    width = plan.half * CORES

    def body(half_ref, *refs):
        turned, right, out_ref = refs[-2], refs[-1], refs[-3]

        @pl.when(pl.program_id(0) == 0)
        def _():
            for ref, (side, first) in zip(refs[:count], places):
                start = pl.multiple_of(half_ref[side] * plan.half + first, 128)
                for lane in range(0, ref.shape[1], plan.tile):
                    turned[pl.ds(start + lane, plan.tile), :] = ref[:, lane:lane + plan.tile].T

        row = 0
        for ref in refs[count:count + len(grads)]:
            right[row:row + ref.shape[0], :] = ref[...]
            row += ref.shape[0]
        k_ref = refs[count + len(grads)]
        piece = plan.tile
        for part in range(width // piece):
            value = dot(turned[part * piece:(part + 1) * piece, :], right[...], 1, 0).astype(bf16)
            for block in range(piece // BLOCK):
                low = part * piece + block * BLOCK
                out_ref[low:low + BLOCK, :] = block_rows(
                    value[block * BLOCK:(block + 1) * BLOCK, :],
                    keep_rows(k_ref, low // BLOCK, tile))

    column = lambda i, h: (0, i)
    return call(
        body, (depth // tile,), halves, (*operands, *grads, down_lanes),
        [whole(value) for value in operands]
        + [pl.BlockSpec((g.shape[0], tile), column) for g in grads]
        + [pl.BlockSpec((down_lanes.shape[0], tile), column)],
        pl.BlockSpec((width, tile), column),
        jax.ShapeDtypeStruct((width, depth), bf16),
        [pltpu.VMEM((width, rows), bf16), pltpu.VMEM((rows, tile), bf16)],
        2 * rows * depth * width, 2 * depth * width + 2 * rows * width + 2 * rows * depth)


def after(value, *others):
    return lax.optimization_barrier((value, *others))[0]


def shards(n_row, n_col, inputs, norm_gain, w_gate, w_up, w_down,
           mask_gate, mask_up, mask_down, grad_out):
    n_chip = n_col // CORES
    local, width = inputs.shape
    features = width * n_col
    plan = Plan(w_gate.shape[1])
    chunks = plan.chunks
    cycle = list(range(0, n_row, 2)) + list(range(n_row - 1, 0, -2))
    ahead = [(cycle[i], cycle[(i + 1) % n_row]) for i in range(n_row)]
    behind = [(b, a) for a, b in ahead]
    swap = [(i, i ^ 1) for i in range(n_col)]
    n_ahead, n_behind = n_row // 2, (n_row - 1) // 2

    def to_partner(value):
        return lax.ppermute(value, "col", swap)

    def from_chips(value):
        return [
            lax.ppermute(value, "col", [(i, (i + CORES * k) % n_col) for i in range(n_col)])
            for k in range(1, n_chip)
        ]

    def total_over_chips(value):
        total = value
        for other in from_chips(value):
            total = total + other
        return total

    offsets = [0]
    for k in range(1, n_ahead + 1):
        offsets.append(-k)
        if k <= n_behind:
            offsets.append(k)
    near, far = offsets[:3], offsets[3:]
    rows_near = local * len(near)
    rows_all = local * len(offsets)

    core = lax.rem(lax.axis_index("col"), CORES).astype(jnp.int32)
    halves = jnp.stack([core, 1 - core])

    inputs_wide = inputs.astype(f32)
    scaled = (inputs_wide * norm_gain).astype(bf16)
    gate_lanes, up_lanes, down_lanes = lanes(mask_gate), lanes(mask_up), lanes(mask_down)

    def ring_step(found, k, *ready):
        found[-k] = lax.ppermute(after(found[1 - k], *ready), "row", ahead)
        if k <= n_behind:
            found[k] = lax.ppermute(after(found[k - 1], *ready), "row", behind)

    def rows_of(found, group):
        return jnp.concatenate([found[offset] for offset in group], axis=0)

    shard = {0: scaled}
    ring_step(shard, 1)
    gu = [mask_columns(plan, chunks[0], halves, w_gate, w_up, gate_lanes, up_lanes)]
    ring_step(shard, 2, gu[0])
    gu.append(mask_columns(plan, chunks[1], after(halves, gu[0]),
                           w_gate, w_up, gate_lanes, up_lanes))
    ring_step(shard, 3, gu[1])
    tokens_near = rows_of(shard, near)
    sent_near = project(1, after(halves, gu[1]), tokens_near, gu[0])
    for k in range(4, n_ahead + 1):
        ring_step(shard, k, sent_near)
    squares = jnp.sum(jnp.square(tokens_near.astype(f32) / norm_gain), axis=1)
    own_near = project(0, halves, tokens_near, gu[0], to_partner(sent_near))
    others_near = from_chips(own_near)

    tokens_far = rows_of(shard, far)
    squares_far = jnp.sum(jnp.square(tokens_far.astype(f32) / norm_gain), axis=1)
    squares = jnp.concatenate([squares, squares_far])
    sent_far = project(1, halves, after(tokens_far, own_near), gu[0])
    grad_shard = {0: after(grad_out, tokens_far)}
    ring_step(grad_shard, 1)
    dn = [mask_rows(plan, chunks[0], after(halves, sent_far), w_down, down_lanes)]
    own_far = project(0, after(halves, dn[0]), tokens_far, gu[0], to_partner(sent_far))
    others_far = from_chips(after(own_far, *others_near))
    ring_step(grad_shard, 2, own_far)
    dn.append(mask_rows(plan, chunks[1], after(halves, own_far), w_down, down_lanes))
    ring_step(grad_shard, 3, dn[1])
    squares = squares + to_partner(after(squares, own_far))
    squares = total_over_chips(squares)
    scale = lax.rsqrt(squares / features + epsilon)[:, None]
    tokens_all = jnp.concatenate([tokens_near, tokens_far], axis=0)
    sent_next = project(1, after(halves, dn[1]), tokens_all, gu[1])
    for k in range(4, n_ahead + 1):
        ring_step(grad_shard, k, sent_next)
    own_next = project(0, halves, tokens_all, gu[1], to_partner(sent_next))
    grads_near, grads_far = rows_of(grad_shard, near), rows_of(grad_shard, far)
    grads_all = jnp.concatenate([grads_near, grads_far], axis=0)
    sent_grad = back_project(1, after(halves, own_next), grads_all, dn[0])
    turned = turn(after(halves, sent_grad), scale, [tokens_near, tokens_far])
    own_grad = back_project(0, after(halves, turned), grads_all, dn[0],
                            to_partner(sent_grad))
    others_grad = from_chips(after(own_grad, *others_far))
    sent_gf = back_project(1, after(halves, own_grad), grads_far, dn[1])
    sent_gn = back_project(1, after(halves, sent_gf), grads_near, dn[1])
    own_gf = back_project(0, after(halves, sent_gn), grads_far, dn[1],
                          to_partner(sent_gf))
    own_gn = back_project(0, after(halves, own_gf), grads_near, dn[1],
                          to_partner(sent_gn))

    pieces0 = [(0, [own_near, *others_near]), (rows_near, [own_far, *others_far])]
    hidden0 = activate(plan, after(halves, own_gn), scale, pieces0, None, 0, rows_all)
    hidden0 = (hidden0, to_partner(hidden0))
    others_next = from_chips(after(own_next, *others_grad))
    cot0 = activate(plan, after(halves, hidden0[0]), scale, pieces0, [(0, [own_grad, *others_grad])],
                    0, rows_all)
    cot0 = (cot0, to_partner(cot0))
    partial = input_cotangent(halves, cot0, gu[0], 0, None, f32)
    grad_gu = gate_up_grads(plan, chunks[0], after(halves, partial), turned,
                            cot0[:1], cot0[1:], gate_lanes, up_lanes, None)

    pieces1 = [(0, [own_next, *others_next])]
    hidden1 = activate(plan, after(halves, grad_gu[0]), scale, pieces1, None, 0, rows_all)
    hidden1 = (hidden1, to_partner(hidden1))
    others_gf = from_chips(after(own_gf, *others_next))
    mixed = down_product(halves, (hidden0, hidden1), dn)

    def scatter(parts):
        back = parts(-n_ahead)
        front = parts(n_behind)
        for k in range(1, n_ahead + 1):
            back = lax.ppermute(back, "row", behind)
            if k < n_ahead:
                back = (back.astype(f32) + parts(k - n_ahead).astype(f32)).astype(bf16)
            if k <= n_behind:
                front = lax.ppermute(front, "row", ahead)
                if k < n_behind:
                    front = (front.astype(f32) + parts(n_behind - k).astype(f32)).astype(bf16)
        return back.astype(f32) + front.astype(f32) + parts(0).astype(f32)

    def part_of(value, group):
        return {offset: lax.slice_in_dim(value, i * local, (i + 1) * local, axis=0)
                for i, offset in enumerate(group)}

    parts = part_of(mixed, offsets)
    output = (inputs_wide + scatter(lambda offset: parts[offset])).astype(bf16)
    grad_w_down = down_grads(plan, after(halves, mixed), (hidden0, hidden1),
                             (grads_near, grads_far), down_lanes)

    others_gn = from_chips(after(own_gn, *others_gf))
    cot_far = activate(plan, after(halves, grad_w_down), scale, pieces1,
                       [(rows_near, [own_gf, *others_gf])], rows_near, rows_all)
    cot_far = (cot_far, to_partner(cot_far))
    norm_far = input_cotangent(halves, cot_far, gu[1], rows_near, partial, bf16)
    cot_near = activate(plan, after(halves, norm_far), scale, pieces1,
                        [(0, [own_gn, *others_gn])], 0, rows_near)
    cot_near = (cot_near, to_partner(cot_near))
    norm_near = input_cotangent(halves, cot_near, gu[1], 0, partial, bf16)
    norms = {**part_of(norm_far, far), **part_of(norm_near, near)}
    d_norm_in = scatter(lambda offset: norms[offset])
    ready = norm_near
    for index in range(chunks[1][1]):
        grad_gu = gate_up_grads(
            plan, chunks[1], after(halves, ready), turned,
            (cot_near[0], cot_far[0]), (cot_near[1], cot_far[1]), gate_lanes, up_lanes, grad_gu,
            index)
        ready = grad_gu[0]
    grad_w_gate, grad_w_up = grad_gu

    inv_local = scale[:local]
    normed = inputs_wide * inv_local
    d_normed = d_norm_in * norm_gain
    inner = jnp.sum(d_normed * normed, axis=1)
    inner = total_over_chips(inner + to_partner(inner)) / features
    gain_part = jnp.sum(d_norm_in * normed, axis=0)
    step = 1
    while step < n_row:
        gain_part = gain_part + lax.ppermute(
            gain_part, "row", [(i, i ^ step) for i in range(n_row)])
        step *= 2
    grad_inputs = (
        grad_out.astype(f32) + inv_local * (d_normed - normed * inner[:, None])
    ).astype(bf16)
    return (output, grad_inputs, gain_part, grad_w_gate, grad_w_up, grad_w_down)


def solution(mesh):
    in_specs = (
        P("row", "col"),
        P("col"),
        P("col", "row"),
        P("col", "row"),
        P("row", "col"),
        P("col", "row"),
        P("col", "row"),
        P("row", "col"),
        P("row", "col"),
    )
    out_specs = (
        P("row", "col"),
        P("row", "col"),
        P("col"),
        P("col", "row"),
        P("col", "row"),
        P("row", "col"),
    )
    body = functools.partial(shards, mesh.shape["row"], mesh.shape["col"])

    return jax.shard_map(
        body, mesh=mesh, in_specs=in_specs, out_specs=out_specs, check_vma=False)
```

time: 644 us -> 490 us (0.76); the launches traced: 634 us -> 487 us
  Pallas kernels: 0 us -> 306 us
  matrix products: 165 us -> 0 us
  waiting for transfers between devices: 202 us -> 78.4 us
  local copies, waits for them, and re-layouts: 150 us -> 37.7 us
  other arithmetic: 65.4 us -> 20.9 us
  starting transfers between devices: 0.74 us -> 43.2 us
  blocking collectives: 36.4 us -> 0 us
  between operations: 14.4 us -> 0.88 us
    pallas_call x0 -> x31, Pallas kernels: none -> 306 us  [call(): pl.pallas_call(body, grid_spec=pltpu.PrefetchScalarGridSpec(num_scalar_pr...]
    dot_general x9 -> x0, matrix products: 165 us -> none  [the longest x3 57.6 us: contract_rows(): lax.dot_general(left, right, (((0,), (0,)), ((), ())), preferred_element_...]
    mul x7 -> x0, local copies, waits for them, and re-layouts: 148 us -> none  [the longest x6 148 us: expand_mask(): weight.reshape(mask_rows, BLOCK, mask_cols, BLOCK)]
    reduce_scatter x4 -> x0, waiting for transfers between devices: 112 us -> none  [the longest x1 50.6 us: shards(): lax.psum_scatter(contract_cols(row_block, down_eff).astype(jnp.bfloat16),...]
    all_gather x5 -> x0, waiting for transfers between devices: 86.5 us -> none  [the longest x1 40.7 us: shards(): lax.all_gather(d_gate, 'col', axis=0, tiled=True)]
    ppermute x0 -> x52, waiting for transfers between devices: none -> 78.4 us  [the longest x8 30.7 us: ring_step(): found[-k] = lax.ppermute(after(found[1 - k], *ready), 'row', ahead)]
    ppermute x0 -> x52, starting transfers between devices: none -> 43.2 us  [the longest x8 15.2 us: ring_step(): found[-k] = lax.ppermute(after(found[1 - k], *ready), 'row', ahead)]
    mul x4 -> x0, other arithmetic: 36.5 us -> none  [the longest x2 33.3 us: expand_mask(): weight.reshape(mask_rows, BLOCK, mask_cols, BLOCK)]
  transfers between devices with their start and end apart: 9 -> 52, of which waited for: 7 -> 16; matrix products, arithmetic and copies ran while one was open for 58% -> 10% of each run, Pallas kernels for 0% -> 58%
where the time goes in v1:
time: 490 us; the launch traced here: 487 us
  Pallas kernels  306 us (62%)
  waiting for transfers between devices  78.4 us (16%)
  starting transfers between devices  43.2 us (9%)
  local copies, waits for them, and re-layouts  37.7 us (8%)
  other arithmetic  20.9 us (4%)
    pallas_call x31, Pallas kernels, call(): pl.pallas_call(body, grid_spec=pltpu.PrefetchScalarGridSpec(num_scalar_pr...  306 us
    ppermute x8, waiting for transfers between devices, ring_step(): found[-k] = lax.ppermute(after(found[1 - k], *ready), 'row', ahead)  30.7 us
    unnamed x62, local copies, waits for them, and re-layouts  21.8 us
    ppermute x8, waiting for transfers between devices, scatter(): back = lax.ppermute(back, 'row', behind)  17.8 us
    ppermute x8, starting transfers between devices, ring_step(): found[-k] = lax.ppermute(after(found[1 - k], *ready), 'row', ahead)  15.2 us
    ppermute x8, waiting for transfers between devices, from_chips(): lax.ppermute(value, 'col', [(i, (i + CORES * k) % n_col) for i in range(n...  15 us
    ppermute x13, waiting for transfers between devices, to_partner(): return lax.ppermute(value, 'col', swap)  12.8 us
    convert_element_type x6, other arithmetic, scatter(): back = (back.astype(f32) + parts(k - n_ahead).astype(f32)).astype(bf16)  11 us
  transfers between devices with their start and end apart: 52, of which 16 were waited for; matrix products, arithmetic and copies ran while one was open for 10% of the time, Pallas kernels for 58%

profile of v1, /device:TPU:0, one launch (start us, length us, event | category | flops | bytes accessed | tf_op | source)
XLA Modules:
  0.0 487.3 jit_solution(7887869141163182516)
XLA Ops:
  2.5 3.1 collective-permute-start
  13.7 14.6 %shard_map.136.w_ref.wm_ref.wo_ref = bf16[2048,4096]{1,0:T(8,128)(2,1)} custom-call(s32[2]{0:T(128)} %pad_add_fusion._.half_ref, bf16[2048,3584]{1,0:T(8,128)(2,1)} %g_ref.3, bf16[2048,3584]{1,0:T(8,128)(2,1)} %u_ref.3, f32[32,3584]{1,0:T(8,128)} %reshape.28.gm_ref.refs_2_.refs_4_, f32[32,3584]{1,0:T(8,128)} %reshape.29.um_ref.refs_3_.refs_5_), custom_call_target="tpu_custom_call" | custom-call | bytes 33554432 | tf_op jit(solution)/shard_map/pallas_call | solution.py:53
  28.4 11.4 %shard_map.137.w_ref.wm_ref.wo_ref = bf16[2048,3072]{1,0:T(8,128)(2,1)} custom-call(s32[2]{0:T(128)} %pad_add_fusion._.half_ref, bf16[2048,3584]{1,0:T(8,128)(2,1)} %g_ref.3, bf16[2048,3584]{1,0:T(8,128)(2,1)} %u_ref.3, f32[32,3584]{1,0:T(8,128)} %reshape.28.gm_ref.refs_2_.refs_4_, f32[32,3584]{1,0:T(8,128)} %reshape.29.um_ref.refs_3_.refs_5_), custom_call_target="tpu_custom_call" | custom-call | bytes 25165824 | tf_op jit(solution)/shard_map/pallas_call | solution.py:53
  44.3 7.5 %shard_map.138 = bf16[288,2048]{1,0:T(8,128)(2,1)} custom-call(s32[2]{0:T(128)} %pad_add_fusion._.half_ref, bf16[288,2048]{1,0:T(8,128)(2,1)} %get-tuple-element.107.x_ref.refs_0_, bf16[2048,4096]{1,0:T(8,128)(2,1)} %shard_map.136.w_ref.wm_ref.wo_ref), custom_call_target="tpu_custom_call" | custom-call | flops 2415919104 | bytes 10747904 | tf_op jit(solution)/shard_map/pallas_call | solution.py:53
  60.2 4.9 collective-permute-done.4
  69.5 7.7 %shard_map.139.refs_0_ = bf16[288,2048]{1,0:T(8,128)(2,1)} custom-call(s32[2]{0:T(128)} %pad_add_fusion._.half_ref, bf16[288,2048]{1,0:T(8,128)(2,1)} %get-tuple-element.107.x_ref.refs_0_, bf16[2048,4096]{1,0:T(8,128)(2,1)} %shard_map.136.w_ref.wm_ref.wo_ref, bf16[288,2048]{1,0:T(8,128)(2,1)} %collective-permute-done.7.rest_0_), custom_call_target="tpu_custom_call" | custom-call | flops 2415919104 | bytes 10747904 | tf_op jit(solution)/shard_map/pallas_call | solution.py:53
  79.4 9.3 %shard_map.140 = bf16[480,2048]{1,0:T(8,128)(2,1)} custom-call(s32[2]{0:T(128)} %pad_add_fusion._.half_ref, bf16[480,2048]{1,0:T(8,128)(2,1)} %copy-done.1, bf16[2048,4096]{1,0:T(8,128)(2,1)} %shard_map.136.w_ref.wm_ref.wo_ref), custom_call_target="tpu_custom_call" | custom-call | flops 4026531840 | bytes 12320768 | tf_op jit(solution)/shard_map/pallas_call | solution.py:53
  91.7 9.8 %shard_map.141.w_ref.refs_1_.refs_3_ = bf16[2048,2048]{1,0:T(8,128)(2,1)} custom-call(s32[2]{0:T(128)} %pad_add_fusion._.half_ref, bf16[3584,2048]{1,0:T(8,128)(2,1)} %w_ref.3, f32[56,2048]{1,0:T(8,128)} %reshape.30.k_ref.refs_6_), custom_call_target="tpu_custom_call" | custom-call | bytes 16777216 | tf_op jit(solution)/shard_map/pallas_call | solution.py:53
  101.5 9.5 %shard_map.142.refs_2_ = bf16[480,2048]{1,0:T(8,128)(2,1)} custom-call(s32[2]{0:T(128)} %pad_add_fusion._.half_ref, bf16[480,2048]{1,0:T(8,128)(2,1)} %copy-done.1, bf16[2048,4096]{1,0:T(8,128)(2,1)} %shard_map.136.w_ref.wm_ref.wo_ref, bf16[480,2048]{1,0:T(8,128)(2,1)} %collective-permute-done.8.rest_0_), custom_call_target="tpu_custom_call" | custom-call | flops 4026531840 | bytes 12320768 | tf_op jit(solution)/shard_map/pallas_call | solution.py:53
  111.0 7.7 %shard_map.143.w_ref.refs_5_.refs_7_ = bf16[1536,2048]{1,0:T(8,128)(2,1)} custom-call(s32[2]{0:T(128)} %pad_add_fusion._.half_ref, bf16[3584,2048]{1,0:T(8,128)(2,1)} %w_ref.3, f32[56,2048]{1,0:T(8,128)} %reshape.30.k_ref.refs_6_), custom_call_target="tpu_custom_call" | custom-call | bytes 12582912 | tf_op jit(solution)/shard_map/pallas_call | solution.py:53
  118.7 9.7 %shard_map.144 = bf16[768,1536]{1,0:T(8,128)(2,1)} custom-call(s32[2]{0:T(128)} %pad_add_fusion._.half_ref, bf16[768,2048]{1,0:T(8,128)(2,1)} %get-tuple-element.141.x_ref, bf16[2048,3072]{1,0:T(8,128)(2,1)} %shard_map.137.w_ref.wm_ref.wo_ref), custom_call_target="tpu_custom_call" | custom-call | flops 4831838208 | bytes 11796480 | tf_op jit(solution)/shard_map/pallas_call | solution.py:53
  131.4 8.5 %collective-permute-done.10 = bf16[96,2048]{1,0:T(8,128)(2,1)S(1)} collective-permute-done((bf16[96,2048]{1,0:T(8,128)(2,1)S(1)}, bf16[96,2048]{1,0:T(8,128)(2,1)S(1)}, u32[]{:S(2)}, u32[]{:S(2)}) %collective-permute-start.10) | collective-permute-done | bytes 393248 | tf_op jit(solution)/shard_map/ppermute | solution.py:440
  144.2 6.2 %collective-permute-done.12 = bf16[96,2048]{1,0:T(8,128)(2,1)S(1)} collective-permute-done((bf16[96,2048]{1,0:T(8,128)(2,1)S(1)}, bf16[96,2048]{1,0:T(8,128)(2,1)S(1)}, u32[]{:S(2)}, u32[]{:S(2)}) %collective-permute-start.12) | collective-permute-done | bytes 393248 | tf_op jit(solution)/shard_map/ppermute | solution.py:440
  154.3 5.7 %collective-permute-done.14 = bf16[96,2048]{1,0:T(8,128)(2,1)S(1)} collective-permute-done((bf16[96,2048]{1,0:T(8,128)(2,1)S(1)}, bf16[96,2048]{1,0:T(8,128)(2,1)S(1)}, u32[]{:S(2)}, u32[]{:S(2)}) %collective-permute-start.14) | collective-permute-done | bytes 393248 | tf_op jit(solution)/shard_map/ppermute | solution.py:440
  163.6 5.4 %collective-permute-done.16 = bf16[96,2048]{1,0:T(8,128)(2,1)S(1)} collective-permute-done((bf16[96,2048]{1,0:T(8,128)(2,1)S(1)}, bf16[96,2048]{1,0:T(8,128)(2,1)S(1)}, u32[]{:S(2)}, u32[]{:S(2)}) %collective-permute-start.16) | collective-permute-done | bytes 393248 | tf_op jit(solution)/shard_map/ppermute | solution.py:440
  170.0 10.2 %shard_map.145.refs_0_ = bf16[768,1536]{1,0:T(8,128)(2,1)} custom-call(s32[2]{0:T(128)} %pad_add_fusion._.half_ref, bf16[768,2048]{1,0:T(8,128)(2,1)} %get-tuple-element.141.x_ref, bf16[2048,3072]{1,0:T(8,128)(2,1)} %shard_map.137.w_ref.wm_ref.wo_ref, bf16[768,1536]{1,0:T(8,128)(2,1)} %collective-permute-done.9.rest_0_), custom_call_target="tpu_custom_call" | custom-call | flops 4831838208 | bytes 11796480 | tf_op jit(solution)/shard_map/pallas_call | solution.py:53
  180.2 8.3 %shard_map.146 = bf16[768,1024]{1,0:T(8,128)(2,1)} custom-call(s32[2]{0:T(128)} %pad_add_fusion._.half_ref, bf16[768,2048]{1,0:T(8,128)(2,1)} %get-tuple-element.131.g_ref, bf16[2048,2048]{1,0:T(8,128)(2,1)} %shard_map.141.w_ref.refs_1_.refs_3_), custom_call_target="tpu_custom_call" | custom-call | flops 3221225472 | bytes 8912896 | tf_op jit(solution)/shard_map/pallas_call | solution.py:53
  189.7 2.6 collective-permute-done.17
  192.9 3.1 collective-permute-done.18
  196.9 8.1 %shard_map.147.x_ref = bf16[2048,768]{1,0:T(8,128)(2,1)} custom-call(s32[2]{0:T(128)} %pad_add_fusion._.half_ref, f32[768,1]{1,0:T(8,128)} %broadcast_in_dim.12.s_ref, bf16[288,2048]{1,0:T(8,128)(2,1)} %get-tuple-element.107.x_ref.refs_0_, bf16[480,2048]{1,0:T(8,128)(2,1)} %copy-done.1), custom_call_target="tpu_custom_call" | custom-call | bytes 6291456 | tf_op jit(solution)/shard_map/pallas_call | solution.py:53
  205.0 8.4 %shard_map.148.refs_4_ = bf16[768,1024]{1,0:T(8,128)(2,1)} custom-call(s32[2]{0:T(128)} %pad_add_fusion._.half_ref, bf16[768,2048]{1,0:T(8,128)(2,1)} %get-tuple-element.131.g_ref, bf16[2048,2048]{1,0:T(8,128)(2,1)} %shard_map.141.w_ref.refs_1_.refs_3_, bf16[768,1024]{1,0:T(8,128)(2,1)} %collective-permute-done.19.rest_0_), custom_call_target="tpu_custom_call" | custom-call | flops 3221225472 | bytes 8912896 | tf_op jit(solution)/shard_map/pallas_call | solution.py:53
  213.9 6.0 %shard_map.149 = bf16[480,768]{1,0:T(8,128)(2,1)} custom-call(s32[2]{0:T(128)} %pad_add_fusion._.half_ref, bf16[480,2048]{1,0:T(8,128)(2,1)} %get-tuple-element.130.g_ref.refs_5_, bf16[1536,2048]{1,0:T(8,128)(2,1)} %shard_map.143.w_ref.refs_5_.refs_7_), custom_call_target="tpu_custom_call" | custom-call | flops 1509949440 | bytes 5849088 | tf_op jit(solution)/shard_map/pallas_call | solution.py:53
  220.0 5.3 %shard_map.150 = bf16[288,768]{1,0:T(8,128)(2,1)} custom-call(s32[2]{0:T(128)} %pad_add_fusion._.half_ref, bf16[288,2048]{1,0:T(8,128)(2,1)} %copy-done.10, bf16[1536,2048]{1,0:T(8,128)(2,1)} %shard_map.143.w_ref.refs_5_.refs_7_), custom_call_target="tpu_custom_call" | custom-call | flops 905969664 | bytes 4767744 | tf_op jit(solution)/shard_map/pallas_call | solution.py:53
  226.6 6.1 %shard_map.151.refs_2_ = bf16[480,768]{1,0:T(8,128)(2,1)} custom-call(s32[2]{0:T(128)} %pad_add_fusion._.half_ref, bf16[480,2048]{1,0:T(8,128)(2,1)} %get-tuple-element.130.g_ref.refs_5_, bf16[1536,2048]{1,0:T(8,128)(2,1)} %shard_map.143.w_ref.refs_5_.refs_7_, bf16[480,768]{1,0:T(8,128)(2,1)} %copy-done.18), custom_call_target="tpu_custom_call" | custom-call | flops 1509949440 | bytes 5849088 | tf_op jit(solution)/shard_map/pallas_call | solution.py:53
  233.5 5.3 %shard_map.152.refs_2_ = bf16[288,768]{1,0:T(8,128)(2,1)} custom-call(s32[2]{0:T(128)} %pad_add_fusion._.half_ref, bf16[288,2048]{1,0:T(8,128)(2,1)} %copy-done.10, bf16[1536,2048]{1,0:T(8,128)(2,1)} %shard_map.143.w_ref.refs_5_.refs_7_, bf16[288,768]{1,0:T(8,128)(2,1)} %copy-done.20), custom_call_target="tpu_custom_call" | custom-call | flops 905969664 | bytes 4767744 | tf_op jit(solution)/shard_map/pallas_call | solution.py:53
  238.8 6.0 %shard_map.153.refs_0_ = bf16[768,1024]{1,0:T(8,128)(2,1)} custom-call(s32[2]{0:T(128)} %pad_add_fusion._.half_ref, f32[768,1]{1,0:T(8,128)} %broadcast_in_dim.12.s_ref, bf16[288,2048]{1,0:T(8,128)(2,1)} %shard_map.139.refs_0_, bf16[288,2048]{1,0:T(8,128)(2,1)} %collective-permute-done.22.refs_1_, bf16[480,2048]{1,0:T(8,128)(2,1)} %shard_map.142.refs_2_, ...), custom_call_target="tpu_custom_call" | custom-call | bytes 7865856 | tf_op jit(solution)/shard_map/pallas_call | solution.py:53
  244.8 4.1 collective-permute-done.25.refs_5_
  250.1 7.8 %shard_map.154.m_ref.refs_0_ = bf16[768,2048]{1,0:T(8,128)(2,1)} custom-call(s32[2]{0:T(128)} %pad_add_fusion._.half_ref, f32[768,1]{1,0:T(8,128)} %broadcast_in_dim.12.s_ref, bf16[288,2048]{1,0:T(8,128)(2,1)} %shard_map.139.refs_0_, bf16[288,2048]{1,0:T(8,128)(2,1)} %collective-permute-done.22.refs_1_, bf16[480,2048]{1,0:T(8,128)(2,1)} %shard_map.142.refs_2_, ...), custom_call_target="tpu_custom_call" | custom-call | bytes 11011584 | tf_op jit(solution)/shard_map/pallas_call | solution.py:53
  258.9 5.0 %collective-permute-done.26.o_ref.refs_1_ = bf16[768,2048]{1,0:T(8,128)(2,1)} collective-permute-done((bf16[768,2048]{1,0:T(8,128)(2,1)}, bf16[768,2048]{1,0:T(8,128)(2,1)}, u32[]{:S(2)}, u32[]{:S(2)}) %collective-permute-start.26) | collective-permute-done | bytes 3145760 | tf_op jit(solution)/shard_map/ppermute | solution.py:409
  263.9 20.0 %shard_map.155.rest_0_ = f32[768,2048]{1,0:T(8,128)} custom-call(s32[2]{0:T(128)} %pad_add_fusion._.half_ref, bf16[768,2048]{1,0:T(8,128)(2,1)} %shard_map.154.m_ref.refs_0_, bf16[768,2048]{1,0:T(8,128)(2,1)} %collective-permute-done.26.o_ref.refs_1_, bf16[2048,4096]{1,0:T(8,128)(2,1)} %shard_map.136.w_ref.wm_ref.wo_ref, ...), custom_call_target="tpu_custom_call" | custom-call | flops 12884901888 | bytes 29360128 | tf_op jit(solution)/shard_map/pallas_call | solution.py:53
  283.9 20.1 %shard_map.156 = (bf16[2048,3584]{1,0:T(8,128)(2,1)}, bf16[2048,3584]{1,0:T(8,128)(2,1)}) custom-call(s32[2]{0:T(128)} %pad_add_fusion._.half_ref, bf16[2048,768]{1,0:T(8,128)(2,1)} %shard_map.147.x_ref, bf16[768,2048]{1,0:T(8,128)(2,1)} %shard_map.154.m_ref.refs_0_, bf16[768,2048]{1,0:T(8,128)(2,1)} %collective-permute-done.26.o_ref.refs_1_, ...), custom_call_target="tpu_custom_call" | custom-call | flops 12884901888 | bytes 26214400 | tf_op jit(solution)/shard_map/pallas_call | solution.py:53
  304.0 7.8 %collective-permute-done.27.refs_1_ = bf16[768,1536]{1,0:T(8,128)(2,1)} collective-permute-done((bf16[768,1536]{1,0:T(8,128)(2,1)S(1)}, bf16[768,1536]{1,0:T(8,128)(2,1)}, u32[]{:S(2)}, u32[]{:S(2)}) %collective-permute-start.27) | collective-permute-done | bytes 2359328 | tf_op jit(solution)/shard_map/ppermute | solution.py:413
  311.7 5.3 %shard_map.157.refs_4_.refs_2_ = bf16[768,768]{1,0:T(8,128)(2,1)} custom-call(s32[2]{0:T(128)} %pad_add_fusion._.half_ref, f32[768,1]{1,0:T(8,128)} %broadcast_in_dim.12.s_ref, bf16[768,1536]{1,0:T(8,128)(2,1)} %shard_map.145.refs_0_, bf16[768,1536]{1,0:T(8,128)(2,1)} %collective-permute-done.27.refs_1_), custom_call_target="tpu_custom_call" | custom-call | bytes 5899776 | tf_op jit(solution)/shard_map/pallas_call | solution.py:53
  321.1 18.0 %shard_map.158 = bf16[768,2048]{1,0:T(8,128)(2,1)} custom-call(s32[2]{0:T(128)} %pad_add_fusion._.half_ref, bf16[768,1024]{1,0:T(8,128)(2,1)} %shard_map.153.refs_0_, bf16[2048,2048]{1,0:T(8,128)(2,1)} %shard_map.141.w_ref.refs_1_.refs_3_, bf16[768,1024]{1,0:T(8,128)(2,1)} %collective-permute-done.24.refs_2_.refs_1_, ...), custom_call_target="tpu_custom_call" | custom-call | flops 11274289152 | bytes 23330816 | tf_op jit(solution)/shard_map/pallas_call | solution.py:53
  339.1 19.6 %shard_map.159 = bf16[3584,2048]{1,0:T(8,128)(2,1)} custom-call(s32[2]{0:T(128)} %pad_add_fusion._.half_ref, bf16[768,1024]{1,0:T(8,128)(2,1)} %shard_map.153.refs_0_, bf16[768,1024]{1,0:T(8,128)(2,1)} %collective-permute-done.24.refs_2_.refs_1_, bf16[768,768]{1,0:T(8,128)(2,1)} %shard_map.157.refs_4_.refs_2_, bf16[768,768]{1,0:T(8,128)(2,1)} %copy-done.24, ...), custom_call_target="tpu_custom_call" | custom-call | flops 11274289152 | bytes 23330816 | tf_op jit(solution)/shard_map/pallas_call | solution.py:53
  359.6 6.2 %shard_map.160.m_ref.refs_1_ = bf16[480,1536]{1,0:T(8,128)(2,1)} custom-call(s32[2]{0:T(128)} %pad_add_fusion._.half_ref, f32[768,1]{1,0:T(8,128)} %broadcast_in_dim.12.s_ref, bf16[768,1536]{1,0:T(8,128)(2,1)} %shard_map.145.refs_0_, bf16[768,1536]{1,0:T(8,128)(2,1)} %collective-permute-done.27.refs_1_, bf16[480,768]{1,0:T(8,128)(2,1)} %shard_map.151.refs_2_, ...), custom_call_target="tpu_custom_call" | custom-call | bytes 6931968 | tf_op jit(solution)/shard_map/pallas_call | solution.py:53
  366.5 2.8 collective-permute-done.37.o_ref.refs_3_
  370.4 14.6 %shard_map.161 = bf16[480,2048]{1,0:T(8,128)(2,1)} custom-call(s32[2]{0:T(128)} %pad_add_fusion._.half_ref, bf16[480,1536]{1,0:T(8,128)(2,1)} %shard_map.160.m_ref.refs_1_, bf16[480,1536]{1,0:T(8,128)(2,1)} %copy-done.3, bf16[2048,3072]{1,0:T(8,128)(2,1)} %shard_map.137.w_ref.wm_ref.wo_ref, bf16[2048,3072]{1,0:T(8,128)(2,1)} %shard_map.137.w_ref.wm_ref.wo_ref, ...), custom_call_target="tpu_custom_call" | custom-call | flops 6039797760 | bytes 19464192 | tf_op jit(solution)/shard_map/pallas_call | solution.py:53
  393.1 6.0 %collective-permute-done.38 = bf16[96,2048]{1,0:T(8,128)(2,1)S(1)} collective-permute-done((bf16[96,2048]{1,0:T(8,128)(2,1)S(1)}, bf16[96,2048]{1,0:T(8,128)(2,1)S(1)}, u32[]{:S(2)}, u32[]{:S(2)}) %collective-permute-start.38) | collective-permute-done | bytes 393248 | tf_op jit(solution)/shard_map/ppermute | solution.py:517
  400.4 7.1 %collective-permute-done.29 = bf16[96,2048]{1,0:T(8,128)(2,1)S(1)} collective-permute-done((bf16[96,2048]{1,0:T(8,128)(2,1)S(1)}, bf16[96,2048]{1,0:T(8,128)(2,1)S(1)}, u32[]{:S(2)}, u32[]{:S(2)}) %collective-permute-start.29) | collective-permute-done | bytes 393248 | tf_op jit(solution)/shard_map/ppermute | solution.py:517
  410.6 5.6 %shard_map.162.m_ref.refs_0_ = bf16[288,1536]{1,0:T(8,128)(2,1)} custom-call(s32[2]{0:T(128)} %pad_add_fusion._.half_ref, f32[768,1]{1,0:T(8,128)} %broadcast_in_dim.12.s_ref, bf16[768,1536]{1,0:T(8,128)(2,1)} %shard_map.145.refs_0_, bf16[768,1536]{1,0:T(8,128)(2,1)} %collective-permute-done.27.refs_1_, bf16[288,768]{1,0:T(8,128)(2,1)} %shard_map.152.refs_2_, ...), custom_call_target="tpu_custom_call" | custom-call | bytes 6047232 | tf_op jit(solution)/shard_map/pallas_call | solution.py:53
  419.8 4.7 collective-permute-done.30
  429.8 12.7 %shard_map.163 = bf16[288,2048]{1,0:T(8,128)(2,1)} custom-call(s32[2]{0:T(128)} %pad_add_fusion._.half_ref, bf16[288,1536]{1,0:T(8,128)(2,1)} %shard_map.162.m_ref.refs_0_, bf16[288,1536]{1,0:T(8,128)(2,1)} %copy-done.6, bf16[2048,3072]{1,0:T(8,128)(2,1)} %shard_map.137.w_ref.wm_ref.wo_ref, bf16[2048,3072]{1,0:T(8,128)(2,1)} %shard_map.137.w_ref.wm_ref.wo_ref, ...), custom_call_target="tpu_custom_call" | custom-call | flops 3623878656 | bytes 16711680 | tf_op jit(solution)/shard_map/pallas_call | solution.py:53
  451.1 8.6 %shard_map.164 = (bf16[2048,3584]{1,0:T(8,128)(2,1)}, bf16[2048,3584]{1,0:T(8,128)(2,1)}) custom-call(s32[2]{0:T(128)} %pad_add_fusion._.half_ref, bf16[2048,768]{1,0:T(8,128)(2,1)} %shard_map.147.x_ref, bf16[288,1536]{1,0:T(8,128)(2,1)} %shard_map.162.m_ref.refs_0_, ...), custom_call_target="tpu_custom_call", output_to_operand_aliasing={{0}: (8, {}), {1}: (9, {})} | custom-call | flops 3221225472 | bytes 8912896 | tf_op jit(solution)/shard_map/pallas_call | solution.py:53
  460.3 8.2 %shard_map.165 = (bf16[2048,3584]{1,0:T(8,128)(2,1)}, bf16[2048,3584]{1,0:T(8,128)(2,1)}) custom-call(s32[2]{0:T(128)} %pad_add_fusion._.half_ref, bf16[2048,768]{1,0:T(8,128)(2,1)} %shard_map.147.x_ref, bf16[288,1536]{1,0:T(8,128)(2,1)} %shard_map.162.m_ref.refs_0_, ...), custom_call_target="tpu_custom_call", output_to_operand_aliasing={{0}: (8, {}), {1}: (9, {})} | custom-call | flops 3221225472 | bytes 8912896 | tf_op jit(solution)/shard_map/pallas_call | solution.py:53
  469.5 8.4 %shard_map.166 = (bf16[2048,3584]{1,0:T(8,128)(2,1)}, bf16[2048,3584]{1,0:T(8,128)(2,1)}) custom-call(s32[2]{0:T(128)} %pad_add_fusion._.half_ref, bf16[2048,768]{1,0:T(8,128)(2,1)} %shard_map.147.x_ref, bf16[288,1536]{1,0:T(8,128)(2,1)} %shard_map.162.m_ref.refs_0_, ...), custom_call_target="tpu_custom_call", output_to_operand_aliasing={{0}: (8, {}), {1}: (9, {})} | custom-call | flops 3221225472 | bytes 8912896 | tf_op jit(solution)/shard_map/pallas_call | solution.py:53
  481.6 2.6 collective-permute-start.51
  484.2 2.5 fusion.7
  (186 shorter events, 98.3 us)
Async XLA Ops:
  2.5 37.3 %collective-permute-start = (bf16[96,2048]{1,0:T(8,128)(2,1)}, bf16[96,2048]{1,0:T(8,128)(2,1)}, u32[]{:S(2)}, u32[]{:S(2)}) collective-permute-start(bf16[96,2048]{1,0:T(8,128)(2,1)} %get-tuple-element.109), channel_id=1, source_target_pairs={{0,8},{8,16},{16,24},{24,28},{28,20},{20,12},{12,4},{4,0},{1,9},{9... | collective-permute-start | bytes 1179656 | tf_op jit(solution)/shard_map/ppermute | solution.py:440
  5.5 36.3 %collective-permute-start.1 = (bf16[96,2048]{1,0:T(8,128)(2,1)}, bf16[96,2048]{1,0:T(8,128)(2,1)S(1)}, u32[]{:S(2)}, u32[]{:S(2)}) collective-permute-start(bf16[96,2048]{1,0:T(8,128)(2,1)} %get-tuple-element.109), channel_id=1, source_target_pairs={{8,0},{16,8},{24,16},{28,24},{20,28},{12,20},{4,12},{0,4},{9,1},{1... | collective-permute-start | bytes 1179656 | tf_op jit(solution)/shard_map/ppermute | solution.py:442
  39.8 13.1 %collective-permute-start.2 = (bf16[96,2048]{1,0:T(8,128)(2,1)}, bf16[96,2048]{1,0:T(8,128)(2,1)}, u32[]{:S(2)}, u32[]{:S(2)}) collective-permute-start(bf16[96,2048]{1,0:T(8,128)(2,1)} %collective-permute-done), channel_id=1, source_target_pairs={{0,8},{8,16},{16,24},{24,28},{28,20},{20,12},{12,4},{4,0},{1,9},{9... | collective-permute-start | bytes 1179656 | tf_op jit(solution)/shard_map/ppermute | solution.py:440
  41.8 13.1 %collective-permute-start.3 = (bf16[96,2048]{1,0:T(8,128)(2,1)S(1)}, bf16[96,2048]{1,0:T(8,128)(2,1)}, u32[]{:S(2)}, u32[]{:S(2)}) collective-permute-start(bf16[96,2048]{1,0:T(8,128)(2,1)S(1)} %collective-permute-done.1), channel_id=1, source_target_pairs={{8,0},{16,8},{24,16},{28,24},{20,28},{12,20},{4,12},{0,4},{9,1},{1... | collective-permute-start | bytes 1179656 | tf_op jit(solution)/shard_map/ppermute | solution.py:442
  51.8 17.7 %collective-permute-start.7 = (bf16[288,2048]{1,0:T(8,128)(2,1)}, bf16[288,2048]{1,0:T(8,128)(2,1)}, u32[]{:S(2)}, u32[]{:S(2)}) collective-permute-start(bf16[288,2048]{1,0:T(8,128)(2,1)} %shard_map.138), channel_id=1, source_target_pairs={{0,1},{1,0},{2,3},{3,2},{4,5},{5,4},{6,7},{7,6},{8,9},{9,8},{10,11... | collective-permute-start | bytes 3538952 | tf_op jit(solution)/shard_map/ppermute | solution.py:409
  52.9 12.1 %collective-permute-start.4 = (bf16[96,2048]{1,0:T(8,128)(2,1)}, bf16[96,2048]{1,0:T(8,128)(2,1)}, u32[]{:S(2)}, u32[]{:S(2)}) collective-permute-start(bf16[96,2048]{1,0:T(8,128)(2,1)} %collective-permute-done.2), channel_id=1, source_target_pairs={{0,8},{8,16},{16,24},{24,28},{28,20},{20,12},{12,4},{4,0},{1,9},{9... | collective-permute-start | bytes 1179656 | tf_op jit(solution)/shard_map/ppermute | solution.py:440
  55.0 13.7 %collective-permute-start.5 = (bf16[96,2048]{1,0:T(8,128)(2,1)}, bf16[96,2048]{1,0:T(8,128)(2,1)S(1)}, u32[]{:S(2)}, u32[]{:S(2)}) collective-permute-start(bf16[96,2048]{1,0:T(8,128)(2,1)} %collective-permute-done.3), channel_id=1, source_target_pairs={{8,0},{16,8},{24,16},{28,24},{20,28},{12,20},{4,12},{0,4},{9,1},{1... | collective-permute-start | bytes 1179656 | tf_op jit(solution)/shard_map/ppermute | solution.py:442
  65.0 12.2 %collective-permute-start.6 = (bf16[96,2048]{1,0:T(8,128)(2,1)}, bf16[96,2048]{1,0:T(8,128)(2,1)S(1)}, u32[]{:S(2)}, u32[]{:S(2)}) collective-permute-start(bf16[96,2048]{1,0:T(8,128)(2,1)} %collective-permute-done.4), channel_id=1, source_target_pairs={{0,8},{8,16},{16,24},{24,28},{28,20},{20,12},{12,4},{4,0},{1,9},{9... | collective-permute-start | bytes 1179656 | tf_op jit(solution)/shard_map/ppermute | solution.py:440
  88.7 12.8 %collective-permute-start.8 = (bf16[480,2048]{1,0:T(8,128)(2,1)}, bf16[480,2048]{1,0:T(8,128)(2,1)}, u32[]{:S(2)}, u32[]{:S(2)}) collective-permute-start(bf16[480,2048]{1,0:T(8,128)(2,1)} %shard_map.140), channel_id=1, source_target_pairs={{0,1},{1,0},{2,3},{3,2},{4,5},{5,4},{6,7},{7,6},{8,9},{9,8},{10,11... | collective-permute-start | bytes 5898248 | tf_op jit(solution)/shard_map/ppermute | solution.py:409
  90.2 53.4 %collective-permute-start.22 = (bf16[288,2048]{1,0:T(8,128)(2,1)S(1)}, bf16[288,2048]{1,0:T(8,128)(2,1)}, u32[]{:S(2)}, u32[]{:S(2)}) collective-permute-start(bf16[288,2048]{1,0:T(8,128)(2,1)S(1)} %copy-done.7), channel_id=1, source_target_pairs={{0,2},{1,3},{2,0},{3,1},{4,6},{5,7},{6,4},{7,5},{8,10},{9,11},{10,... | collective-permute-start | bytes 3538952 | tf_op jit(solution)/shard_map/ppermute | solution.py:413
  128.4 41.6 %collective-permute-start.9 = (bf16[768,1536]{1,0:T(8,128)(2,1)}, bf16[768,1536]{1,0:T(8,128)(2,1)}, u32[]{:S(2)}, u32[]{:S(2)}) collective-permute-start(bf16[768,1536]{1,0:T(8,128)(2,1)} %shard_map.144), channel_id=1, source_target_pairs={{0,1},{1,0},{2,3},{3,2},{4,5},{5,4},{6,7},{7,6},{8,9},{9,8},{10,11... | collective-permute-start | bytes 7077896 | tf_op jit(solution)/shard_map/ppermute | solution.py:409
  128.6 11.3 %collective-permute-start.10 = (bf16[96,2048]{1,0:T(8,128)(2,1)S(1)}, bf16[96,2048]{1,0:T(8,128)(2,1)S(1)}, u32[]{:S(2)}, u32[]{:S(2)}) collective-permute-start(bf16[96,2048]{1,0:T(8,128)(2,1)S(1)} %copy-done.15), channel_id=1, source_target_pairs={{0,8},{8,16},{16,24},{24,28},{28,20},{20,12},{12,4},{4,0},{1,9},{9... | collective-permute-start | bytes 1179656 | tf_op jit(solution)/shard_map/ppermute | solution.py:440
  130.2 11.3 %collective-permute-start.11 = (bf16[96,2048]{1,0:T(8,128)(2,1)S(1)}, bf16[96,2048]{1,0:T(8,128)(2,1)S(1)}, u32[]{:S(2)}, u32[]{:S(2)}) collective-permute-start(bf16[96,2048]{1,0:T(8,128)(2,1)S(1)} %copy-done.15), channel_id=1, source_target_pairs={{8,0},{16,8},{24,16},{28,24},{20,28},{12,20},{4,12},{0,4},{9,1},{1... | collective-permute-start | bytes 1179656 | tf_op jit(solution)/shard_map/ppermute | solution.py:442
  139.9 10.4 %collective-permute-start.12 = (bf16[96,2048]{1,0:T(8,128)(2,1)S(1)}, bf16[96,2048]{1,0:T(8,128)(2,1)S(1)}, u32[]{:S(2)}, u32[]{:S(2)}) collective-permute-start(bf16[96,2048]{1,0:T(8,128)(2,1)S(1)} %collective-permute-done.10), channel_id=1, source_target_pairs={{0,8},{8,16},{16,24},{24,28},{28,20},{20,12},{12,4},{4,0},{1,9},{9... | collective-permute-start | bytes 1179656 | tf_op jit(solution)/shard_map/ppermute | solution.py:440
  141.5 10.4 %collective-permute-start.13 = (bf16[96,2048]{1,0:T(8,128)(2,1)S(1)}, bf16[96,2048]{1,0:T(8,128)(2,1)S(1)}, u32[]{:S(2)}, u32[]{:S(2)}) collective-permute-start(bf16[96,2048]{1,0:T(8,128)(2,1)S(1)} %collective-permute-done.11), channel_id=1, source_target_pairs={{8,0},{16,8},{24,16},{28,24},{20,28},{12,20},{4,12},{0,4},{9,1},{1... | collective-permute-start | bytes 1179656 | tf_op jit(solution)/shard_map/ppermute | solution.py:442
  143.6 69.8 %collective-permute-start.23 = (bf16[480,2048]{1,0:T(8,128)(2,1)S(1)}, bf16[480,2048]{1,0:T(8,128)(2,1)}, u32[]{:S(2)}, u32[]{:S(2)}) collective-permute-start(bf16[480,2048]{1,0:T(8,128)(2,1)S(1)} %copy-done.4), channel_id=1, source_target_pairs={{0,2},{1,3},{2,0},{3,1},{4,6},{5,7},{6,4},{7,5},{8,10},{9,11},{10,... | collective-permute-start | bytes 5898248 | tf_op jit(solution)/shard_map/ppermute | solution.py:413
  150.4 9.7 %collective-permute-start.14 = (bf16[96,2048]{1,0:T(8,128)(2,1)S(1)}, bf16[96,2048]{1,0:T(8,128)(2,1)S(1)}, u32[]{:S(2)}, u32[]{:S(2)}) collective-permute-start(bf16[96,2048]{1,0:T(8,128)(2,1)S(1)} %collective-permute-done.12), channel_id=1, source_target_pairs={{0,8},{8,16},{16,24},{24,28},{28,20},{20,12},{12,4},{4,0},{1,9},{9... | collective-permute-start | bytes 1179656 | tf_op jit(solution)/shard_map/ppermute | solution.py:440
  151.9 10.7 %collective-permute-start.15 = (bf16[96,2048]{1,0:T(8,128)(2,1)S(1)}, bf16[96,2048]{1,0:T(8,128)(2,1)S(1)}, u32[]{:S(2)}, u32[]{:S(2)}) collective-permute-start(bf16[96,2048]{1,0:T(8,128)(2,1)S(1)} %collective-permute-done.13), channel_id=1, source_target_pairs={{8,0},{16,8},{24,16},{28,24},{20,28},{12,20},{4,12},{0,4},{9,1},{1... | collective-permute-start | bytes 1179656 | tf_op jit(solution)/shard_map/ppermute | solution.py:442
  160.1 8.9 %collective-permute-start.16 = (bf16[96,2048]{1,0:T(8,128)(2,1)S(1)}, bf16[96,2048]{1,0:T(8,128)(2,1)S(1)}, u32[]{:S(2)}, u32[]{:S(2)}) collective-permute-start(bf16[96,2048]{1,0:T(8,128)(2,1)S(1)} %collective-permute-done.14), channel_id=1, source_target_pairs={{0,8},{8,16},{16,24},{24,28},{28,20},{20,12},{12,4},{4,0},{1,9},{9... | collective-permute-start | bytes 1179656 | tf_op jit(solution)/shard_map/ppermute | solution.py:440
  188.5 16.5 %collective-permute-start.19 = (bf16[768,1024]{1,0:T(8,128)(2,1)}, bf16[768,1024]{1,0:T(8,128)(2,1)}, u32[]{:S(2)}, u32[]{:S(2)}) collective-permute-start(bf16[768,1024]{1,0:T(8,128)(2,1)} %shard_map.146), channel_id=1, source_target_pairs={{0,1},{1,0},{2,3},{3,2},{4,5},{5,4},{6,7},{7,6},{8,9},{9,8},{10,11... | collective-permute-start | bytes 4718600 | tf_op jit(solution)/shard_map/ppermute | solution.py:409
  213.4 35.5 %collective-permute-start.25 = (bf16[768,1024]{1,0:T(8,128)(2,1)}, bf16[768,1024]{1,0:T(8,128)(2,1)S(1)}, u32[]{:S(2)}, u32[]{:S(2)}) collective-permute-start(bf16[768,1024]{1,0:T(8,128)(2,1)} %shard_map.148.refs_4_), channel_id=1, source_target_pairs={{0,2},{1,3},{2,0},{3,1},{4,6},{5,7},{6,4},{7,5},{8,10},{9,11},{10,... | collective-permute-start | bytes 4718600 | tf_op jit(solution)/shard_map/ppermute | solution.py:413
  219.9 5.8 %collective-permute-start.20 = (bf16[480,768]{1,0:T(8,128)(2,1)}, bf16[480,768]{1,0:T(8,128)(2,1)S(1)}, u32[]{:S(2)}, u32[]{:S(2)}) collective-permute-start(bf16[480,768]{1,0:T(8,128)(2,1)} %shard_map.149), channel_id=1, source_target_pairs={{0,1},{1,0},{2,3},{3,2},{4,5},{5,4},{6,7},{7,6},{8,9},{9,8},{10,11... | collective-permute-start | bytes 2211848 | tf_op jit(solution)/shard_map/ppermute | solution.py:409
  225.2 7.5 %collective-permute-start.21 = (bf16[288,768]{1,0:T(8,128)(2,1)}, bf16[288,768]{1,0:T(8,128)(2,1)S(1)}, u32[]{:S(2)}, u32[]{:S(2)}) collective-permute-start(bf16[288,768]{1,0:T(8,128)(2,1)} %shard_map.150), channel_id=1, source_target_pairs={{0,1},{1,0},{2,3},{3,2},{4,5},{5,4},{6,7},{7,6},{8,9},{9,8},{10,11... | collective-permute-start | bytes 1327112 | tf_op jit(solution)/shard_map/ppermute | solution.py:409
  257.9 6.0 %collective-permute-start.26 = (bf16[768,2048]{1,0:T(8,128)(2,1)}, bf16[768,2048]{1,0:T(8,128)(2,1)}, u32[]{:S(2)}, u32[]{:S(2)}) collective-permute-start(bf16[768,2048]{1,0:T(8,128)(2,1)} %shard_map.154.m_ref.refs_0_), channel_id=1, source_target_pairs={{0,1},{1,0},{2,3},{3,2},{4,5},{5,4},{6,7},{7,6},{8,9},{9,8},{10,11... | collective-permute-start | bytes 9437192 | tf_op jit(solution)/shard_map/ppermute | solution.py:409
  257.9 59.8 %collective-permute-start.24 = (bf16[768,1024]{1,0:T(8,128)(2,1)}, bf16[768,1024]{1,0:T(8,128)(2,1)}, u32[]{:S(2)}, u32[]{:S(2)}) collective-permute-start(bf16[768,1024]{1,0:T(8,128)(2,1)} %shard_map.153.refs_0_), channel_id=1, source_target_pairs={{0,1},{1,0},{2,3},{3,2},{4,5},{5,4},{6,7},{7,6},{8,9},{9,8},{10,11... | collective-permute-start | bytes 4718600 | tf_op jit(solution)/shard_map/ppermute | solution.py:409
  258.4 53.3 %collective-permute-start.27 = (bf16[768,1536]{1,0:T(8,128)(2,1)S(1)}, bf16[768,1536]{1,0:T(8,128)(2,1)}, u32[]{:S(2)}, u32[]{:S(2)}) collective-permute-start(bf16[768,1536]{1,0:T(8,128)(2,1)S(1)} %copy-done), channel_id=1, source_target_pairs={{0,2},{1,3},{2,0},{3,1},{4,6},{5,7},{6,4},{7,5},{8,10},{9,11},{10,... | collective-permute-start | bytes 7077896 | tf_op jit(solution)/shard_map/ppermute | solution.py:413
  317.1 41.6 %collective-permute-start.36 = (bf16[480,768]{1,0:T(8,128)(2,1)S(1)}, bf16[480,768]{1,0:T(8,128)(2,1)S(1)}, u32[]{:S(2)}, u32[]{:S(2)}) collective-permute-start(bf16[480,768]{1,0:T(8,128)(2,1)S(1)} %copy-done.12), channel_id=1, source_target_pairs={{0,2},{1,3},{2,0},{3,1},{4,6},{5,7},{6,4},{7,5},{8,10},{9,11},{10,... | collective-permute-start | bytes 2211848 | tf_op jit(solution)/shard_map/ppermute | solution.py:413
  366.0 43.9 %collective-permute-start.41 = (bf16[288,768]{1,0:T(8,128)(2,1)S(1)}, bf16[288,768]{1,0:T(8,128)(2,1)S(1)}, u32[]{:S(2)}, u32[]{:S(2)}) collective-permute-start(bf16[288,768]{1,0:T(8,128)(2,1)S(1)} %copy-done.13), channel_id=1, source_target_pairs={{0,2},{1,3},{2,0},{3,1},{4,6},{5,7},{6,4},{7,5},{8,10},{9,11},{10,... | collective-permute-start | bytes 1327112 | tf_op jit(solution)/shard_map/ppermute | solution.py:413
  387.1 12.0 %collective-permute-start.38 = (bf16[96,2048]{1,0:T(8,128)(2,1)S(1)}, bf16[96,2048]{1,0:T(8,128)(2,1)S(1)}, u32[]{:S(2)}, u32[]{:S(2)}) collective-permute-start(bf16[96,2048]{1,0:T(8,128)(2,1)S(1)} %get-tuple-element.118), channel_id=1, source_target_pairs={{8,0},{16,8},{24,16},{28,24},{20,28},{12,20},{4,12},{0,4},{9,1},{1... | collective-permute-start | bytes 1179656 | tf_op jit(solution)/shard_map/ppermute | solution.py:517
  389.5 18.0 %collective-permute-start.29 = (bf16[96,2048]{1,0:T(8,128)(2,1)S(1)}, bf16[96,2048]{1,0:T(8,128)(2,1)S(1)}, u32[]{:S(2)}, u32[]{:S(2)}) collective-permute-start(bf16[96,2048]{1,0:T(8,128)(2,1)S(1)} %get-tuple-element.114), channel_id=1, source_target_pairs={{8,0},{16,8},{24,16},{28,24},{20,28},{12,20},{4,12},{0,4},{9,1},{1... | collective-permute-start | bytes 1179656 | tf_op jit(solution)/shard_map/ppermute | solution.py:517
  391.0 28.7 %collective-permute-start.33 = (bf16[96,2048]{1,0:T(8,128)(2,1)}, bf16[96,2048]{1,0:T(8,128)(2,1)}, u32[]{:S(2)}, u32[]{:S(2)}) collective-permute-start(bf16[96,2048]{1,0:T(8,128)(2,1)} %get-tuple-element.115), channel_id=1, source_target_pairs={{0,8},{8,16},{16,24},{24,28},{28,20},{20,12},{12,4},{4,0},{1,9},{9... | collective-permute-start | bytes 1179656 | tf_op jit(solution)/shard_map/ppermute | solution.py:521
  391.5 24.7 %collective-permute-start.44 = (bf16[96,2048]{1,0:T(8,128)(2,1)}, bf16[96,2048]{1,0:T(8,128)(2,1)}, u32[]{:S(2)}, u32[]{:S(2)}) collective-permute-start(bf16[96,2048]{1,0:T(8,128)(2,1)} %get-tuple-element.119), channel_id=1, source_target_pairs={{0,8},{8,16},{16,24},{24,28},{28,20},{20,12},{12,4},{4,0},{1,9},{9... | collective-permute-start | bytes 1179656 | tf_op jit(solution)/shard_map/ppermute | solution.py:521
  400.0 16.3 %collective-permute-start.39 = (bf16[96,2048]{1,0:T(8,128)(2,1)}, bf16[96,2048]{1,0:T(8,128)(2,1)}, u32[]{:S(2)}, u32[]{:S(2)}) collective-permute-start(bf16[96,2048]{1,0:T(8,128)(2,1)} %add_convert_fusion.4), channel_id=1, source_target_pairs={{8,0},{16,8},{24,16},{28,24},{20,28},{12,20},{4,12},{0,4},{9,1},{1... | collective-permute-start | bytes 1179656 | tf_op jit(solution)/shard_map/ppermute | solution.py:517
  409.4 15.1 %collective-permute-start.30 = (bf16[96,2048]{1,0:T(8,128)(2,1)}, bf16[96,2048]{1,0:T(8,128)(2,1)}, u32[]{:S(2)}, u32[]{:S(2)}) collective-permute-start(bf16[96,2048]{1,0:T(8,128)(2,1)} %add_convert_fusion.9), channel_id=1, source_target_pairs={{8,0},{16,8},{24,16},{28,24},{20,28},{12,20},{4,12},{0,4},{9,1},{1... | collective-permute-start | bytes 1179656 | tf_op jit(solution)/shard_map/ppermute | solution.py:517
  416.3 12.6 %collective-permute-start.42 = (bf16[288,1536]{1,0:T(8,128)(2,1)}, bf16[288,1536]{1,0:T(8,128)(2,1)S(1)}, u32[]{:S(2)}, u32[]{:S(2)}) collective-permute-start(bf16[288,1536]{1,0:T(8,128)(2,1)} %shard_map.162.m_ref.refs_0_), channel_id=1, source_target_pairs={{0,1},{1,0},{2,3},{3,2},{4,5},{5,4},{6,7},{7,6},{8,9},{9,8},{10,11... | collective-permute-start | bytes 2654216 | tf_op jit(solution)/shard_map/ppermute | solution.py:409
  417.7 24.9 %collective-permute-start.40 = (bf16[96,2048]{1,0:T(8,128)(2,1)S(1)}, bf16[96,2048]{1,0:T(8,128)(2,1)S(1)}, u32[]{:S(2)}, u32[]{:S(2)}) collective-permute-start(bf16[96,2048]{1,0:T(8,128)(2,1)S(1)} %get-tuple-element.116), channel_id=1, source_target_pairs={{8,0},{16,8},{24,16},{28,24},{20,28},{12,20},{4,12},{0,4},{9,1},{1... | collective-permute-start | bytes 1179656 | tf_op jit(solution)/shard_map/ppermute | solution.py:517
  419.2 23.3 %collective-permute-start.45 = (bf16[96,2048]{1,0:T(8,128)(2,1)S(1)}, bf16[96,2048]{1,0:T(8,128)(2,1)S(1)}, u32[]{:S(2)}, u32[]{:S(2)}) collective-permute-start(bf16[96,2048]{1,0:T(8,128)(2,1)S(1)} %get-tuple-element.117), channel_id=1, source_target_pairs={{0,8},{8,16},{16,24},{24,28},{28,20},{20,12},{12,4},{4,0},{1,9},{9... | collective-permute-start | bytes 1179656 | tf_op jit(solution)/shard_map/ppermute | solution.py:521
  426.9 20.0 %collective-permute-start.31 = (bf16[96,2048]{1,0:T(8,128)(2,1)}, bf16[96,2048]{1,0:T(8,128)(2,1)S(1)}, u32[]{:S(2)}, u32[]{:S(2)}) collective-permute-start(bf16[96,2048]{1,0:T(8,128)(2,1)} %get-tuple-element.112), channel_id=1, source_target_pairs={{8,0},{16,8},{24,16},{28,24},{20,28},{12,20},{4,12},{0,4},{9,1},{1... | collective-permute-start | bytes 1179656 | tf_op jit(solution)/shard_map/ppermute | solution.py:517
  427.3 19.5 %collective-permute-start.34 = (bf16[96,2048]{1,0:T(8,128)(2,1)S(1)}, bf16[96,2048]{1,0:T(8,128)(2,1)}, u32[]{:S(2)}, u32[]{:S(2)}) collective-permute-start(bf16[96,2048]{1,0:T(8,128)(2,1)S(1)} %get-tuple-element.113), channel_id=1, source_target_pairs={{0,8},{8,16},{16,24},{24,28},{28,20},{20,12},{12,4},{4,0},{1,9},{9... | collective-permute-start | bytes 1179656 | tf_op jit(solution)/shard_map/ppermute | solution.py:521
  444.8 15.0 %collective-permute-start.46 = (bf16[96,2048]{1,0:T(8,128)(2,1)}, bf16[96,2048]{1,0:T(8,128)(2,1)S(1)}, u32[]{:S(2)}, u32[]{:S(2)}) collective-permute-start(bf16[96,2048]{1,0:T(8,128)(2,1)} %get-tuple-element.121), channel_id=1, source_target_pairs={{0,8},{8,16},{16,24},{24,28},{28,20},{20,12},{12,4},{4,0},{1,9},{9... | collective-permute-start | bytes 1179656 | tf_op jit(solution)/shard_map/ppermute | solution.py:521
  446.4 13.4 %collective-permute-start.43 = (bf16[96,2048]{1,0:T(8,128)(2,1)}, bf16[96,2048]{1,0:T(8,128)(2,1)S(1)}, u32[]{:S(2)}, u32[]{:S(2)}) collective-permute-start(bf16[96,2048]{1,0:T(8,128)(2,1)} %get-tuple-element.120), channel_id=1, source_target_pairs={{8,0},{16,8},{24,16},{28,24},{20,28},{12,20},{4,12},{0,4},{9,1},{1... | collective-permute-start | bytes 1179656 | tf_op jit(solution)/shard_map/ppermute | solution.py:517
  449.1 35.1 %collective-permute-start.35 = (bf16[96,2048]{1,0:T(8,128)(2,1)}, bf16[96,2048]{1,0:T(8,128)(2,1)S(1)}, u32[]{:S(2)}, u32[]{:S(2)}) collective-permute-start(bf16[96,2048]{1,0:T(8,128)(2,1)} %get-tuple-element.111), channel_id=1, source_target_pairs={{0,8},{8,16},{16,24},{24,28},{28,20},{20,12},{12,4},{4,0},{1,9},{9... | collective-permute-start | bytes 1179656 | tf_op jit(solution)/shard_map/ppermute | solution.py:521
  450.7 33.5 %collective-permute-start.32 = (bf16[96,2048]{1,0:T(8,128)(2,1)S(1)}, bf16[96,2048]{1,0:T(8,128)(2,1)S(1)}, u32[]{:S(2)}, u32[]{:S(2)}) collective-permute-start(bf16[96,2048]{1,0:T(8,128)(2,1)S(1)} %get-tuple-element.110), channel_id=1, source_target_pairs={{8,0},{16,8},{24,16},{28,24},{20,28},{12,20},{4,12},{0,4},{9,1},{1... | collective-permute-start | bytes 1179656 | tf_op jit(solution)/shard_map/ppermute | solution.py:517
  460.2 8.8 %collective-permute-start.47 = (f32[96]{0:T(128)S(1)}, f32[96]{0:T(128)S(1)}, u32[]{:S(2)}, u32[]{:S(2)}) collective-permute-start(f32[96]{0:T(128)S(1)} %get-tuple-element.105), channel_id=1, source_target_pairs={{0,1},{1,0},{2,3},{3,2},{4,5},{5,4},{6,7},{7,6},{8,9},{9,8},{10,11... | collective-permute-start | bytes 1160 | tf_op jit(solution)/shard_map/ppermute | solution.py:409
  468.5 9.3 %collective-permute-start.49 = (f32[2048]{0:T(1024)S(1)}, f32[2048]{0:T(1024)S(1)}, u32[]{:S(2)}, u32[]{:S(2)}) collective-permute-start(f32[2048]{0:T(1024)S(1)} %get-tuple-element.104), channel_id=1, source_target_pairs={{0,4},{4,0},{8,12},{12,8},{16,20},{20,16},{24,28},{28,24},{1,5},{5... | collective-permute-start | bytes 24584 | tf_op jit(solution)/shard_map/ppermute | solution.py:563
  469.0 10.5 %collective-permute-start.48 = (f32[96]{0:T(128)S(1)}, f32[96]{0:T(128)S(1)}, u32[]{:S(2)}, u32[]{:S(2)}) collective-permute-start(f32[96]{0:T(128)S(1)} %add.94), channel_id=1, source_target_pairs={{0,2},{1,3},{2,0},{3,1},{4,6},{5,7},{6,4},{7,5},{8,10},{9,11},{10,... | collective-permute-start | bytes 1160 | tf_op jit(solution)/shard_map/ppermute | solution.py:413
  477.9 3.7 collective-permute-start.50
  481.6 5.1 %collective-permute-start.51 = (f32[2048]{0:T(1024)S(1)}, f32[2048]{0:T(1024)S(1)}, u32[]{:S(2)}, u32[]{:S(2)}) collective-permute-start(f32[2048]{0:T(1024)S(1)} %add.98), channel_id=1, source_target_pairs={{0,16},{4,20},{8,24},{12,28},{16,0},{20,4},{24,8},{28,12},{1,17},{... | collective-permute-start | bytes 24584 | tf_op jit(solution)/shard_map/ppermute | solution.py:563
  (29 other events, 191.0 us)

commit v2 on v1

--- a/solution.py
+++ b/solution.py
@@ -78,28 +78,6 @@
             self.chunks.append((first, self.count - first))
 
 
-def mask_columns(plan, chunk, scalars, w_gate, w_up, gate_lanes, up_lanes):
-    first, steps = chunk
-    depth, tile = w_gate.shape[0], plan.tile
-
-    def body(_, g_ref, u_ref, gm_ref, um_ref, out_ref):
-        for w_ref, k_ref, lane in ((g_ref, gm_ref, 0), (u_ref, um_ref, tile)):
-            for index in range(depth // BLOCK):
-                span = pl.ds(index * BLOCK, BLOCK)
-                out_ref[span, lane:lane + tile] = block_rows(
-                    w_ref[span, :], keep_rows(k_ref, index, tile))
-
-    column = lambda h, j, s: (0, h * plan.count + first + j)
-    weight = pl.BlockSpec((depth, tile), column)
-    mask = pl.BlockSpec((depth // BLOCK, tile), column)
-    return call(
-        body, (CORES, steps), scalars, (w_gate, w_up, gate_lanes, up_lanes),
-        [weight, weight, mask, mask],
-        pl.BlockSpec((depth, 2 * tile), lambda h, j, s: (0, h * steps + j)),
-        jax.ShapeDtypeStruct((depth, CORES * steps * 2 * tile), bf16), [],
-        0, 8 * CORES * depth * steps * tile)
-
-
 def mask_rows(plan, chunk, scalars, w_down, down_lanes):
     first, steps = chunk
     depth, tile = w_down.shape[1], plan.tile
@@ -120,102 +98,137 @@
         0, 4 * CORES * depth * steps * tile)
 
 
-def project(side, halves, tokens, weight, added=None):
-    rows, depth = tokens.shape
-    width = weight.shape[1] // CORES
-    tile = tile_of(width, 512)
-    steps = width // tile
-
-    def body(_, x_ref, w_ref, *rest):
-        value = dot(x_ref[...], w_ref[...], 1, 0)
-        if added is not None:
-            value += rest[0][...].astype(f32)
-        rest[-1][...] = value.astype(bf16)
-
-    out = pl.BlockSpec((rows, tile), lambda i, h: (0, i))
-    extra = () if added is None else (added,)
-    return call(
-        body, (steps,), halves, (tokens, weight, *extra),
-        [whole(tokens), pl.BlockSpec((depth, tile), lambda i, h: (0, h[side] * steps + i))]
-        + [out] * len(extra),
-        out, jax.ShapeDtypeStruct((rows, width), bf16), [],
-        2 * rows * depth * width, 2 * depth * width + 2 * rows * depth + 2 * rows * width)
+def gathered(shards, scratch):
+    @pl.when(pl.program_id(0) == 0)
+    def _():
+        row = 0
+        for ref in shards:
+            scratch[row:row + ref.shape[0], :] = ref[...]
+            row += ref.shape[0]
+
+
+def project(side, plan, chunk, halves, tokens, weights, added=None, inverse_gain=None):
+    first, steps = chunk
+    local, depth = tokens[0].shape
+    rows, tile, count = local * len(tokens), plan.tile, len(tokens)
+
+    def body(_, *refs):
+        scratch = refs[-1]
+        g_ref, u_ref, gm_ref, um_ref = refs[count:count + 4]
+        rest = refs[count + 4:-1]
+        gathered(refs[:count], scratch)
+        if inverse_gain is not None:
+            gain_ref, out_ref, kept_ref, sum_ref = rest
+
+            @pl.when(pl.program_id(0) == 0)
+            def _():
+                for row in range(0, rows, local):
+                    value = scratch[row:row + local, :].astype(f32) * gain_ref[...]
+                    sum_ref[row:row + local, :] = jnp.sum(value * value, axis=1, keepdims=True)
+        else:
+            out_ref, kept_ref = rest[-2:]
+        for w_ref, k_ref, lane in ((g_ref, gm_ref, 0), (u_ref, um_ref, tile)):
+            for index in range(depth // BLOCK):
+                span = pl.ds(index * BLOCK, BLOCK)
+                kept_ref[span, lane:lane + tile] = block_rows(
+                    w_ref[span, :], keep_rows(k_ref, index, tile))
+            value = dot(scratch[...], kept_ref[:, lane:lane + tile], 1, 0)
+            if added is not None:
+                value += rest[0][:, lane:lane + tile].astype(f32)
+            out_ref[:, lane:lane + tile] = value.astype(bf16)
+
+    column = lambda j, h: (0, h[side] * plan.count + first + j)
+    weight = pl.BlockSpec((depth, tile), column)
+    mask = pl.BlockSpec((depth // BLOCK, tile), column)
+    out = pl.BlockSpec((rows, 2 * tile), lambda j, h: (0, j))
+    kept = pl.BlockSpec((depth, 2 * tile), lambda j, h: (0, j))
+    width = 2 * steps * tile
+    extra, extra_specs = [], []
+    out_specs = [out, kept]
+    shapes = [jax.ShapeDtypeStruct((rows, width), bf16),
+              jax.ShapeDtypeStruct((depth, width), bf16)]
+    if added is not None:
+        extra, extra_specs = [added], [out]
+    if inverse_gain is not None:
+        extra, extra_specs = [inverse_gain], [whole(inverse_gain)]
+        out_specs.append(pl.BlockSpec((rows, 1), lambda j, h: (0, 0)))
+        shapes.append(jax.ShapeDtypeStruct((rows, 1), f32))
+    return call(
+        body, (steps,), halves, (*tokens, *weights, *extra),
+        [whole(value) for value in tokens] + [weight, weight, mask, mask] + extra_specs,
+        out_specs, shapes, [pltpu.VMEM((rows, depth), bf16)],
+        2 * rows * depth * width, 4 * depth * width + 2 * rows * depth + 4 * rows * width)
 
 
 def back_project(side, halves, tokens, weight, added=None):
-    rows, depth = tokens.shape
+    local, depth = tokens[0].shape
+    rows, count = local * len(tokens), len(tokens)
     width = weight.shape[0] // CORES
     tile = tile_of(width, 256)
     steps = width // tile
 
-    def body(_, g_ref, w_ref, *rest):
-        value = dot(g_ref[...], w_ref[...], 1, 1)
+    def body(_, *refs):
+        scratch, out_ref, w_ref = refs[-1], refs[-2], refs[count]
+        gathered(refs[:count], scratch)
+        value = dot(scratch[...], w_ref[...], 1, 1)
         if added is not None:
-            value += rest[0][...].astype(f32)
-        rest[-1][...] = value.astype(bf16)
+            value += refs[count + 1][...].astype(f32)
+        out_ref[...] = value.astype(bf16)
 
     out = pl.BlockSpec((rows, tile), lambda i, h: (0, i))
     extra = () if added is None else (added,)
     return call(
-        body, (steps,), halves, (tokens, weight, *extra),
-        [whole(tokens), pl.BlockSpec((tile, depth), lambda i, h: (h[side] * steps + i, 0))]
+        body, (steps,), halves, (*tokens, weight, *extra),
+        [whole(value) for value in tokens]
+        + [pl.BlockSpec((tile, depth), lambda i, h: (h[side] * steps + i, 0))]
         + [out] * len(extra),
-        out, jax.ShapeDtypeStruct((rows, width), bf16), [],
+        out, jax.ShapeDtypeStruct((rows, width), bf16), [pltpu.VMEM((rows, depth), bf16)],
         2 * rows * depth * width, 2 * depth * width + 2 * rows * depth + 2 * rows * width)
 
 
-def activate(plan, scalars, scale, pieces, grad_pieces, start, stop):
+def activate(plan, scalars, scale, pair, grads, with_hidden):
+    rows, width = pair[0].shape
     tile = plan.tile
-    width = pieces[0][1][0].shape[1] // 2
-    with_grad = grad_pieces is not None
-    cuts = {start, stop}
-    listed = list(pieces) + (list(grad_pieces) if with_grad else [])
-    for first, arrays in listed:
-        cuts |= {first, first + arrays[0].shape[0]}
-    cuts = sorted(cut for cut in cuts if start <= cut <= stop)
-    operands, in_specs = [scale], [whole(scale)]
-    for first, arrays in pieces:
-        operands += arrays
-        in_specs += [pl.BlockSpec((a.shape[0], 2 * tile), lambda j, s: (0, j)) for a in arrays]
-    for first, arrays in grad_pieces or ():
-        operands += arrays
-        in_specs += [pl.BlockSpec((a.shape[0], tile), lambda j, s: (0, j)) for a in arrays]
-    rows = stop - start
-    wide = 2 * tile if with_grad else tile
-
-    def summed(refs, groups, low, high, lane):
-        position = 0
-        for first, arrays in groups:
-            if first <= low and high <= first + arrays[0].shape[0]:
-                total = None
-                for ref in refs[position:position + len(arrays)]:
-                    term = ref[low - first:high - first, lane:lane + tile].astype(f32)
-                    total = term if total is None else total + term
-                return total
-            position += len(arrays)
+    count = len(pair)
+    operands = [scale, *pair, *(grads or ())]
+    in_specs = [whole(scale)]
+    in_specs += [pl.BlockSpec((rows, 2 * tile), lambda j, s: (0, j)) for _ in pair]
+    in_specs += [pl.BlockSpec((rows, tile), lambda j, s: (0, j)) for _ in grads or ()]
+    out_specs, shapes = [], []
+    if grads:
+        out_specs.append(pl.BlockSpec((rows, 2 * tile), lambda j, s: (0, j)))
+        shapes.append(jax.ShapeDtypeStruct((rows, width), bf16))
+    if with_hidden:
+        out_specs.append(pl.BlockSpec((rows, tile), lambda j, s: (0, j)))
+        shapes.append(jax.ShapeDtypeStruct((rows, width // 2), bf16))
+
+    def summed(refs, low, high, lane):
+        total = None
+        for ref in refs:
+            term = ref[low:high, lane:lane + tile].astype(f32)
+            total = term if total is None else total + term
+        return total
 
     def body(_, s_ref, *refs):
-        out_ref = refs[-1]
-        count = sum(len(arrays) for _, arrays in pieces)
-        for low, high in zip(cuts[:-1], cuts[1:]):
-            span = slice(low - start, high - start)
+        outs = refs[len(operands) - 1:]
+        for low in range(0, rows, 96 if rows % 96 == 0 else 16):
+            high = low + (96 if rows % 96 == 0 else 16)
             factor = s_ref[low:high, :]
-            gate = summed(refs, pieces, low, high, 0) * factor
-            up = summed(refs, pieces, low, high, tile) * factor
+            gate = summed(refs[:count], low, high, 0) * factor
+            up = summed(refs[:count], low, high, tile) * factor
             sigma = jax.nn.sigmoid(gate)
-            if with_grad:
-                grad = summed(refs[count:], grad_pieces, low, high, 0)
+            silu = gate * sigma
+            if grads:
+                grad = summed(refs[count:len(operands) - 1], low, high, 0)
                 d_gate = grad * up * sigma * (1.0 + gate * (1.0 - sigma))
-                out_ref[span, :tile] = d_gate.astype(bf16)
-                out_ref[span, tile:] = (grad * (gate * sigma)).astype(bf16)
-            else:
-                out_ref[span, :] = (gate * sigma * up).astype(bf16)
-
-    return call(
-        body, (width // tile,), scalars, operands, in_specs,
-        pl.BlockSpec((rows, wide), lambda j, s: (0, j)),
-        jax.ShapeDtypeStruct((rows, width // tile * wide), bf16), [],
-        0, 2 * sum(a.size for a in operands) + 2 * rows * width)
+                outs[0][low:high, :tile] = d_gate.astype(bf16)
+                outs[0][low:high, tile:] = (grad * silu).astype(bf16)
+            if with_hidden:
+                outs[-1][low:high, :] = (silu * up).astype(bf16)
+
+    return call(
+        body, (width // 2 // tile,), scalars, operands, in_specs,
+        out_specs, shapes, [], 0, 2 * sum(a.size for a in operands) + 3 * rows * width)
 
 
 def down_product(halves, hidden, weights):
@@ -244,27 +257,26 @@
         2 * rows * total, 2 * total + 2 * rows * (total // depth + depth))
 
 
-def input_cotangent(halves, pair, weight, start, added, dtype):
+def input_cotangent(scalars, pair, weights, added, dtype):
     rows = pair[0].shape[0]
-    depth, width = weight.shape[0], weight.shape[1] // CORES
+    depth, width = weights[0].shape
     tile = tile_of(depth, 256)
-    side = [pl.BlockSpec((tile, width), lambda i, h: (i, h[0])),
-            pl.BlockSpec((tile, width), lambda i, h: (i, h[1]))]
+    side = pl.BlockSpec((tile, width), lambda i, h: (i, 0))
     extra = () if added is None else (added,)
 
     def body(_, m_ref, o_ref, wm_ref, wo_ref, *rest):
         value = dot(m_ref[...], wm_ref[...], 1, 1) + dot(o_ref[...], wo_ref[...], 1, 1)
         if added is not None:
-            value += rest[0][start:start + rows, :]
+            value += rest[0][...]
         rest[-1][...] = value.astype(dtype)
 
     return call(
-        body, (depth // tile,), halves, (*pair, weight, weight, *extra),
-        [whole(pair[0]), whole(pair[1]), *side]
+        body, (depth // tile,), scalars, (*pair, *weights, *extra),
+        [whole(pair[0]), whole(pair[1]), side, side]
         + [pl.BlockSpec((a.shape[0], tile), lambda i, h: (0, i)) for a in extra],
         pl.BlockSpec((rows, tile), lambda i, h: (0, i)),
         jax.ShapeDtypeStruct((rows, depth), dtype), [],
-        2 * rows * weight.size, 2 * weight.size + 4 * rows * width + 4 * rows * depth)
+        4 * rows * depth * width, 4 * depth * width + 4 * rows * width + 4 * rows * depth)
 
 
 def turn(scalars, scale, pieces):
@@ -425,89 +437,76 @@
         offsets.append(-k)
         if k <= n_behind:
             offsets.append(k)
-    near, far = offsets[:3], offsets[3:]
-    rows_near = local * len(near)
-    rows_all = local * len(offsets)
 
     core = lax.rem(lax.axis_index("col"), CORES).astype(jnp.int32)
     halves = jnp.stack([core, 1 - core])
 
     inputs_wide = inputs.astype(f32)
     scaled = (inputs_wide * norm_gain).astype(bf16)
-    gate_lanes, up_lanes, down_lanes = lanes(mask_gate), lanes(mask_up), lanes(mask_down)
 
     def ring_step(found, k, *ready):
         found[-k] = lax.ppermute(after(found[1 - k], *ready), "row", ahead)
         if k <= n_behind:
             found[k] = lax.ppermute(after(found[k - 1], *ready), "row", behind)
 
-    def rows_of(found, group):
-        return jnp.concatenate([found[offset] for offset in group], axis=0)
-
     shard = {0: scaled}
     ring_step(shard, 1)
-    gu = [mask_columns(plan, chunks[0], halves, w_gate, w_up, gate_lanes, up_lanes)]
-    ring_step(shard, 2, gu[0])
-    gu.append(mask_columns(plan, chunks[1], after(halves, gu[0]),
-                           w_gate, w_up, gate_lanes, up_lanes))
-    ring_step(shard, 3, gu[1])
-    tokens_near = rows_of(shard, near)
-    sent_near = project(1, after(halves, gu[1]), tokens_near, gu[0])
+    down_lanes = lanes(mask_down)
+    dn = [mask_rows(plan, chunks[0], halves, w_down, down_lanes)]
+    ring_step(shard, 2, dn[0])
+    dn.append(mask_rows(plan, chunks[1], after(halves, dn[0]), w_down, down_lanes))
+    ring_step(shard, 3, dn[1])
+    gate_lanes = lanes(after(mask_gate, dn[1]))
+    up_lanes = lanes(after(mask_up, dn[1]))
     for k in range(4, n_ahead + 1):
-        ring_step(shard, k, sent_near)
-    squares = jnp.sum(jnp.square(tokens_near.astype(f32) / norm_gain), axis=1)
-    own_near = project(0, halves, tokens_near, gu[0], to_partner(sent_near))
-    others_near = from_chips(own_near)
-
-    tokens_far = rows_of(shard, far)
-    squares_far = jnp.sum(jnp.square(tokens_far.astype(f32) / norm_gain), axis=1)
-    squares = jnp.concatenate([squares, squares_far])
-    sent_far = project(1, halves, after(tokens_far, own_near), gu[0])
-    grad_shard = {0: after(grad_out, tokens_far)}
+        ring_step(shard, k, gate_lanes, up_lanes)
+    tokens = [shard[offset] for offset in offsets]
+    weights = (w_gate, w_up, gate_lanes, up_lanes)
+
+    sent0, kept0_o, squares = project(
+        1, plan, chunks[0], halves, tokens, weights,
+        inverse_gain=(1.0 / norm_gain)[None])
+    grad_shard = {0: after(grad_out, *tokens)}
     ring_step(grad_shard, 1)
-    dn = [mask_rows(plan, chunks[0], after(halves, sent_far), w_down, down_lanes)]
-    own_far = project(0, after(halves, dn[0]), tokens_far, gu[0], to_partner(sent_far))
-    others_far = from_chips(after(own_far, *others_near))
-    ring_step(grad_shard, 2, own_far)
-    dn.append(mask_rows(plan, chunks[1], after(halves, own_far), w_down, down_lanes))
-    ring_step(grad_shard, 3, dn[1])
-    squares = squares + to_partner(after(squares, own_far))
-    squares = total_over_chips(squares)
+    squares = squares[:, 0]
+    squares = squares + to_partner(squares)
+    got0 = to_partner(sent0)
+    own0, kept0_m = project(
+        0, plan, chunks[0], after(halves, sent0), tokens, weights, got0)
+    others = from_chips(squares)
+    for other in others:
+        squares = squares + other
     scale = lax.rsqrt(squares / features + epsilon)[:, None]
-    tokens_all = jnp.concatenate([tokens_near, tokens_far], axis=0)
-    sent_next = project(1, after(halves, dn[1]), tokens_all, gu[1])
+    others0 = from_chips(after(own0, *others))
+
+    ring_step(grad_shard, 2, own0)
+    sent1, kept1_o = project(1, plan, chunks[1], after(halves, own0), tokens, weights)
+    ring_step(grad_shard, 3, sent1)
+    turned = turn(after(halves, sent1), scale, tokens)
     for k in range(4, n_ahead + 1):
-        ring_step(grad_shard, k, sent_next)
-    own_next = project(0, halves, tokens_all, gu[1], to_partner(sent_next))
-    grads_near, grads_far = rows_of(grad_shard, near), rows_of(grad_shard, far)
-    grads_all = jnp.concatenate([grads_near, grads_far], axis=0)
-    sent_grad = back_project(1, after(halves, own_next), grads_all, dn[0])
-    turned = turn(after(halves, sent_grad), scale, [tokens_near, tokens_far])
-    own_grad = back_project(0, after(halves, turned), grads_all, dn[0],
-                            to_partner(sent_grad))
-    others_grad = from_chips(after(own_grad, *others_far))
-    sent_gf = back_project(1, after(halves, own_grad), grads_far, dn[1])
-    sent_gn = back_project(1, after(halves, sent_gf), grads_near, dn[1])
-    own_gf = back_project(0, after(halves, sent_gn), grads_far, dn[1],
-                          to_partner(sent_gf))
-    own_gn = back_project(0, after(halves, own_gf), grads_near, dn[1],
-                          to_partner(sent_gn))
-
-    pieces0 = [(0, [own_near, *others_near]), (rows_near, [own_far, *others_far])]
-    hidden0 = activate(plan, after(halves, own_gn), scale, pieces0, None, 0, rows_all)
+        ring_step(grad_shard, k, turned)
+    own1, kept1_m = project(
+        0, plan, chunks[1], after(halves, turned), tokens, weights, to_partner(sent1))
+    grads = [grad_shard[offset] for offset in offsets]
+    sent_b0 = back_project(1, after(halves, own1), grads, dn[0])
+    sent_b1 = back_project(1, after(halves, sent_b0), grads, dn[1])
+    got_b1 = to_partner(sent_b1)
+    own_b0 = back_project(0, after(halves, sent_b1), grads, dn[0], to_partner(sent_b0))
+    others_b0 = from_chips(after(own_b0, *others0))
+    own_b1 = back_project(0, after(halves, own_b0), grads, dn[1], got_b1)
+    others1 = from_chips(after(own1, *others_b0))
+    cot0, hidden0 = activate(plan, after(halves, own_b1), scale, [own0, *others0],
+                             [own_b0, *others_b0], True)
+    cot0 = (cot0, to_partner(cot0))
     hidden0 = (hidden0, to_partner(hidden0))
-    others_next = from_chips(after(own_next, *others_grad))
-    cot0 = activate(plan, after(halves, hidden0[0]), scale, pieces0, [(0, [own_grad, *others_grad])],
-                    0, rows_all)
-    cot0 = (cot0, to_partner(cot0))
-    partial = input_cotangent(halves, cot0, gu[0], 0, None, f32)
+    partial = input_cotangent(halves, cot0, (kept0_m, kept0_o), None, f32)
     grad_gu = gate_up_grads(plan, chunks[0], after(halves, partial), turned,
                             cot0[:1], cot0[1:], gate_lanes, up_lanes, None)
 
-    pieces1 = [(0, [own_next, *others_next])]
-    hidden1 = activate(plan, after(halves, grad_gu[0]), scale, pieces1, None, 0, rows_all)
+    others_b1 = from_chips(after(own_b1, *others1))
+    hidden1, = activate(plan, after(halves, grad_gu[0]), scale, [own1, *others1],
+                        None, True)
     hidden1 = (hidden1, to_partner(hidden1))
-    others_gf = from_chips(after(own_gf, *others_next))
     mixed = down_product(halves, (hidden0, hidden1), dn)
 
     def scatter(parts):
@@ -523,32 +522,24 @@
                     front = (front.astype(f32) + parts(n_behind - k).astype(f32)).astype(bf16)
         return back.astype(f32) + front.astype(f32) + parts(0).astype(f32)
 
-    def part_of(value, group):
-        return {offset: lax.slice_in_dim(value, i * local, (i + 1) * local, axis=0)
-                for i, offset in enumerate(group)}
-
-    parts = part_of(mixed, offsets)
-    output = (inputs_wide + scatter(lambda offset: parts[offset])).astype(bf16)
-    grad_w_down = down_grads(plan, after(halves, mixed), (hidden0, hidden1),
-                             (grads_near, grads_far), down_lanes)
-
-    others_gn = from_chips(after(own_gn, *others_gf))
-    cot_far = activate(plan, after(halves, grad_w_down), scale, pieces1,
-                       [(rows_near, [own_gf, *others_gf])], rows_near, rows_all)
-    cot_far = (cot_far, to_partner(cot_far))
-    norm_far = input_cotangent(halves, cot_far, gu[1], rows_near, partial, bf16)
-    cot_near = activate(plan, after(halves, norm_far), scale, pieces1,
-                        [(0, [own_gn, *others_gn])], 0, rows_near)
-    cot_near = (cot_near, to_partner(cot_near))
-    norm_near = input_cotangent(halves, cot_near, gu[1], 0, partial, bf16)
-    norms = {**part_of(norm_far, far), **part_of(norm_near, near)}
-    d_norm_in = scatter(lambda offset: norms[offset])
-    ready = norm_near
+    def part_of(value):
+        parts = {offset: lax.slice_in_dim(value, i * local, (i + 1) * local, axis=0)
+                 for i, offset in enumerate(offsets)}
+        return lambda offset: parts[offset]
+
+    output = (inputs_wide + scatter(part_of(mixed))).astype(bf16)
+    cot1, = activate(plan, after(halves, mixed), scale, [own1, *others1],
+                     [own_b1, *others_b1], False)
+    cot1 = (cot1, to_partner(cot1))
+    norm_all = input_cotangent(halves, cot1, (kept1_m, kept1_o), partial, bf16)
+    d_norm_in = scatter(part_of(norm_all))
+    grad_w_down = down_grads(plan, after(halves, norm_all), (hidden0, hidden1),
+                             grads, down_lanes)
+    ready = grad_w_down
     for index in range(chunks[1][1]):
         grad_gu = gate_up_grads(
             plan, chunks[1], after(halves, ready), turned,
-            (cot_near[0], cot_far[0]), (cot_near[1], cot_far[1]), gate_lanes, up_lanes, grad_gu,
-            index)
+            cot1[:1], cot1[1:], gate_lanes, up_lanes, grad_gu, index)
         ready = grad_gu[0]
     grad_w_gate, grad_w_up = grad_gu
 
@@ -556,7 +547,8 @@
     normed = inputs_wide * inv_local
     d_normed = d_norm_in * norm_gain
     inner = jnp.sum(d_normed * normed, axis=1)
-    inner = total_over_chips(inner + to_partner(inner)) / features
+    inner = inner + to_partner(inner)
+    inner = total_over_chips(inner) / features
     gain_part = jnp.sum(d_norm_in * normed, axis=0)
     step = 1
     while step < n_row:

time: 490 us -> 455 us (0.929)
  Pallas kernels: 306 us -> 247 us
  waiting for transfers between devices: 78.4 us -> 126 us
  local copies, waits for them, and re-layouts: 37.7 us -> 19.1 us
  other arithmetic: 20.9 us -> 15.7 us
    pallas_call x31 -> x22, Pallas kernels: 306 us -> 247 us  [call(): pl.pallas_call(body, grid_spec=pltpu.PrefetchScalarGridSpec(num_scalar_pr...]
    ppermute x8 -> x6, waiting for transfers between devices: 15 us -> 53.1 us  [from_chips(): lax.ppermute(value, 'col', [(i, (i + CORES * k) % n_col) for i in range(n...]
    ppermute x8, waiting for transfers between devices: 30.7 us -> 12.8 us  [ring_step(): found[-k] = lax.ppermute(after(found[1 - k], *ready), 'row', ahead)]
    ppermute x8, waiting for transfers between devices: 17.8 us -> 29.9 us  [scatter(): back = lax.ppermute(back, 'row', behind)]
    ppermute x6, waiting for transfers between devices: 0.02 us -> 11.3 us  [ring_step(): found[k] = lax.ppermute(after(found[k - 1], *ready), 'row', behind)]
    unnamed x62 -> x66, local copies, waits for them, and re-layouts: 21.8 us -> 10.7 us
    ppermute x13 -> x10, waiting for transfers between devices: 12.8 us -> 16.3 us  [to_partner(): return lax.ppermute(value, 'col', swap)]
  transfers between devices with their start and end apart: 52 -> 47, of which waited for: 16 -> 24; matrix products, arithmetic and copies ran while one was open for 10% -> 5% of each run, Pallas kernels for 58% -> 43%
where the time goes in v2:
time: 455 us; the launch traced here: 453 us
  Pallas kernels  247 us (54%)
  waiting for transfers between devices  126 us (28%)
  starting transfers between devices  44.4 us (10%)
  local copies, waits for them, and re-layouts  19.1 us (4%)
  other arithmetic  15.7 us (3%)
    pallas_call x22, Pallas kernels, call(): pl.pallas_call(body, grid_spec=pltpu.PrefetchScalarGridSpec(num_scalar_pr...  247 us
    ppermute x6, waiting for transfers between devices, from_chips(): lax.ppermute(value, 'col', [(i, (i + CORES * k) % n_col) for i in range(n...  53.1 us
    ppermute x8, waiting for transfers between devices, scatter(): back = lax.ppermute(back, 'row', behind)  29.9 us
    ppermute x10, waiting for transfers between devices, to_partner(): return lax.ppermute(value, 'col', swap)  16.3 us
    ppermute x8, starting transfers between devices, ring_step(): found[-k] = lax.ppermute(after(found[1 - k], *ready), 'row', ahead)  14.3 us
    ppermute x8, waiting for transfers between devices, ring_step(): found[-k] = lax.ppermute(after(found[1 - k], *ready), 'row', ahead)  12.8 us
    ppermute x6, waiting for transfers between devices, ring_step(): found[k] = lax.ppermute(after(found[k - 1], *ready), 'row', behind)  11.3 us
    unnamed x66, local copies, waits for them, and re-layouts  10.7 us
  transfers between devices with their start and end apart: 47, of which 24 were waited for; matrix products, arithmetic and copies ran while one was open for 5% of the time, Pallas kernels for 43%

profile of v2, /device:TPU:0, one launch (start us, length us, event | category | flops | bytes accessed | tf_op | source)
XLA Modules:
  0.0 452.8 jit_solution(15501228727009259284)
XLA Ops:
  1.7 3.1 collective-permute-start
  7.6 9.9 %shard_map.136.refs_8_.refs_1_.refs_3_ = bf16[2048,2048]{1,0:T(8,128)(2,1)} custom-call(s32[2]{0:T(128)} %pad_add_fusion._.half_ref, bf16[3584,2048]{1,0:T(8,128)(2,1)} %w_ref.3, f32[56,2048]{1,0:T(8,128)} %reshape.28.k_ref.refs_12_), custom_call_target="tpu_custom_call" | custom-call | bytes 16777216 | tf_op jit(solution)/shard_map/pallas_call | solution.py:53
  17.5 2.1 collective-permute-start.2
  19.6 7.7 %shard_map.137.refs_8_.refs_5_.refs_7_ = bf16[1536,2048]{1,0:T(8,128)(2,1)} custom-call(s32[2]{0:T(128)} %pad_add_fusion._.half_ref, bf16[3584,2048]{1,0:T(8,128)(2,1)} %w_ref.3, f32[56,2048]{1,0:T(8,128)} %reshape.28.k_ref.refs_12_), custom_call_target="tpu_custom_call" | custom-call | bytes 12582912 | tf_op jit(solution)/shard_map/pallas_call | solution.py:53
  28.2 1.7 collective-permute-start.4
  32.6 4.8 %collective-permute-done.3.refs_4_ = bf16[96,2048]{1,0:T(8,128)(2,1)S(1)} collective-permute-done((bf16[96,2048]{1,0:T(8,128)(2,1)S(1)}, bf16[96,2048]{1,0:T(8,128)(2,1)S(1)}, u32[]{:S(2)}, u32[]{:S(2)}) %collective-permute-start.3) | collective-permute-done | bytes 393248 | tf_op jit(solution)/shard_map/ppermute | solution.py:450
  40.0 6.5 %collective-permute-done.5.refs_6_ = bf16[96,2048]{1,0:T(8,128)(2,1)S(1)} collective-permute-done((bf16[96,2048]{1,0:T(8,128)(2,1)S(1)}, bf16[96,2048]{1,0:T(8,128)(2,1)S(1)}, u32[]{:S(2)}, u32[]{:S(2)}) %collective-permute-start.5) | collective-permute-done | bytes 393248 | tf_op jit(solution)/shard_map/ppermute | solution.py:450
  47.6 13.4 %shard_map.138 = (bf16[768,2048]{1,0:T(8,128)(2,1)}, bf16[2048,2048]{1,0:T(8,128)(2,1)}, f32[768,1]{1,0:T(8,128)}) custom-call(s32[2]{0:T(128)} %pad_add_fusion._.half_ref, bf16[96,2048]{1,0:T(8,128)(2,1)} %copy-done.1, bf16[96,2048]{1,0:T(8,128)(2,1)} %copy-done.2, bf16[96,2048]{1,0:T(8,128)(2,1)} %copy-done.3, bf16[96,2048]{1,0:T(8,128)(2,1)} %copy-done.4, ...), custom_call_target="tpu_custom_call" | custom-call | flops 6442450944 | bytes 26214400 | tf_op jit(solution)/shard_map/pallas_call | solution.py:53
  61.1 5.9 %collective-permute-done.7.refs_12_ = bf16[768,2048]{1,0:T(8,128)(2,1)S(1)} collective-permute-done((bf16[768,2048]{1,0:T(8,128)(2,1)}, bf16[768,2048]{1,0:T(8,128)(2,1)S(1)}, u32[]{:S(2)}, u32[]{:S(2)}) %collective-permute-start.7) | collective-permute-done | bytes 3145760 | tf_op jit(solution)/shard_map/ppermute | solution.py:421
  66.9 1.7 copy-done.22
  68.6 13.3 %shard_map.139 = (bf16[768,2048]{1,0:T(8,128)(2,1)}, bf16[2048,2048]{1,0:T(8,128)(2,1)}) custom-call(s32[2]{0:T(128)} %pad_add_fusion._.half_ref, bf16[96,2048]{1,0:T(8,128)(2,1)} %copy-done.1, bf16[96,2048]{1,0:T(8,128)(2,1)} %copy-done.2, bf16[96,2048]{1,0:T(8,128)(2,1)} %copy-done.3, bf16[96,2048]{1,0:T(8,128)(2,1)} %copy-done.4, ...), custom_call_target="tpu_custom_call" | custom-call | flops 6442450944 | bytes 26214400 | tf_op jit(solution)/shard_map/pallas_call | solution.py:53
  81.9 10.8 %shard_map.140 = (bf16[768,1536]{1,0:T(8,128)(2,1)}, bf16[2048,1536]{1,0:T(8,128)(2,1)}) custom-call(s32[2]{0:T(128)} %pad_add_fusion._.half_ref, bf16[96,2048]{1,0:T(8,128)(2,1)} %copy-done.1, bf16[96,2048]{1,0:T(8,128)(2,1)} %copy-done.2, bf16[96,2048]{1,0:T(8,128)(2,1)} %copy-done.3, bf16[96,2048]{1,0:T(8,128)(2,1)} %copy-done.4, ...), custom_call_target="tpu_custom_call" | custom-call | flops 4831838208 | bytes 20447232 | tf_op jit(solution)/shard_map/pallas_call | solution.py:53
  94.9 9.4 %collective-permute-done.11.refs_1_.refs_5_ = bf16[96,2048]{1,0:T(8,128)(2,1)S(1)} collective-permute-done((bf16[96,2048]{1,0:T(8,128)(2,1)S(1)}, bf16[96,2048]{1,0:T(8,128)(2,1)S(1)}, u32[]{:S(2)}, u32[]{:S(2)}) %collective-permute-start.11) | collective-permute-done | bytes 393248 | tf_op jit(solution)/shard_map/ppermute | solution.py:448
  108.6 2.1 collective-permute-done.9
  112.7 2.1 collective-permute-done.13.refs_3_.refs_7_
  117.2 7.9 %shard_map.141.x_ref = bf16[2048,768]{1,0:T(8,128)(2,1)} custom-call(s32[2]{0:T(128)} %pad_add_fusion._.half_ref, f32[768,1]{1,0:T(8,128)} %broadcast_in_dim.15.s_ref, bf16[96,2048]{1,0:T(8,128)(2,1)} %copy-done.1, bf16[96,2048]{1,0:T(8,128)(2,1)} %copy-done.2, bf16[96,2048]{1,0:T(8,128)(2,1)} %copy-done.3, bf16[96,2048]{1,0:T(8,128)(2,1)} %copy-done.4, ...), custom_call_target="tpu_custom_call" | custom-call | bytes 6291456 | tf_op jit(solution)/shard_map/pallas_call | solution.py:53
  127.2 11.4 %shard_map.142 = (bf16[768,1536]{1,0:T(8,128)(2,1)}, bf16[2048,1536]{1,0:T(8,128)(2,1)}) custom-call(s32[2]{0:T(128)} %pad_add_fusion._.half_ref, bf16[96,2048]{1,0:T(8,128)(2,1)} %copy-done.1, bf16[96,2048]{1,0:T(8,128)(2,1)} %copy-done.2, bf16[96,2048]{1,0:T(8,128)(2,1)} %copy-done.3, bf16[96,2048]{1,0:T(8,128)(2,1)} %copy-done.4, ...), custom_call_target="tpu_custom_call" | custom-call | flops 4831838208 | bytes 20447232 | tf_op jit(solution)/shard_map/pallas_call | solution.py:53
  140.1 8.3 %shard_map.143 = bf16[768,1024]{1,0:T(8,128)(2,1)} custom-call(s32[2]{0:T(128)} %pad_add_fusion._.half_ref, bf16[96,2048]{1,0:T(8,128)(2,1)} %refs_4_, bf16[96,2048]{1,0:T(8,128)(2,1)} %copy-done.12, bf16[96,2048]{1,0:T(8,128)(2,1)} %copy-done.13, bf16[96,2048]{1,0:T(8,128)(2,1)} %copy-done.14, bf16[96,2048]{1,0:T(8,128)(2,1)} %copy-done.15, ...), custom_call_target="tpu_custom_call" | custom-call | flops 3221225472 | bytes 8912896 | tf_op jit(solution)/shard_map/pallas_call | solution.py:53
  148.5 7.2 %shard_map.144 = bf16[768,768]{1,0:T(8,128)(2,1)} custom-call(s32[2]{0:T(128)} %pad_add_fusion._.half_ref, bf16[96,2048]{1,0:T(8,128)(2,1)} %refs_4_, bf16[96,2048]{1,0:T(8,128)(2,1)} %copy-done.12, bf16[96,2048]{1,0:T(8,128)(2,1)} %copy-done.13, bf16[96,2048]{1,0:T(8,128)(2,1)} %copy-done.14, bf16[96,2048]{1,0:T(8,128)(2,1)} %copy-done.15, ...), custom_call_target="tpu_custom_call" | custom-call | flops 2415919104 | bytes 7471104 | tf_op jit(solution)/shard_map/pallas_call | solution.py:53
  156.8 8.6 %shard_map.145.refs_2_ = bf16[768,1024]{1,0:T(8,128)(2,1)} custom-call(s32[2]{0:T(128)} %pad_add_fusion._.half_ref, bf16[96,2048]{1,0:T(8,128)(2,1)} %refs_4_, bf16[96,2048]{1,0:T(8,128)(2,1)} %copy-done.12, bf16[96,2048]{1,0:T(8,128)(2,1)} %copy-done.13, bf16[96,2048]{1,0:T(8,128)(2,1)} %copy-done.14, bf16[96,2048]{1,0:T(8,128)(2,1)} %copy-done.15, ...), custom_call_target="tpu_custom_call" | custom-call | flops 3221225472 | bytes 8912896 | tf_op jit(solution)/shard_map/pallas_call | solution.py:53
  165.4 14.9 %collective-permute-done.20.refs_1_ = bf16[768,2048]{1,0:T(8,128)(2,1)} collective-permute-done((bf16[768,2048]{1,0:T(8,128)(2,1)}, bf16[768,2048]{1,0:T(8,128)(2,1)}, u32[]{:S(2)}, u32[]{:S(2)}) %collective-permute-start.20) | collective-permute-done | bytes 3145760 | tf_op jit(solution)/shard_map/ppermute | solution.py:425
  181.8 3.1 collective-permute-done.19.refs_9_
  185.9 7.4 %shard_map.146.refs_2_ = bf16[768,768]{1,0:T(8,128)(2,1)} custom-call(s32[2]{0:T(128)} %pad_add_fusion._.half_ref, bf16[96,2048]{1,0:T(8,128)(2,1)} %refs_4_, bf16[96,2048]{1,0:T(8,128)(2,1)} %copy-done.12, bf16[96,2048]{1,0:T(8,128)(2,1)} %copy-done.13, bf16[96,2048]{1,0:T(8,128)(2,1)} %copy-done.14, bf16[96,2048]{1,0:T(8,128)(2,1)} %copy-done.15, ...), custom_call_target="tpu_custom_call" | custom-call | flops 2415919104 | bytes 7471104 | tf_op jit(solution)/shard_map/pallas_call | solution.py:53
  193.4 21.9 %collective-permute-done.21.refs_3_ = bf16[768,1024]{1,0:T(8,128)(2,1)S(1)} collective-permute-done((bf16[768,1024]{1,0:T(8,128)(2,1)}, bf16[768,1024]{1,0:T(8,128)(2,1)S(1)}, u32[]{:S(2)}, u32[]{:S(2)}) %collective-permute-start.21) | collective-permute-done | bytes 1572896 | tf_op jit(solution)/shard_map/ppermute | solution.py:425
  216.4 8.5 %shard_map.147 = (bf16[768,2048]{1,0:T(8,128)(2,1)}, bf16[768,1024]{1,0:T(8,128)(2,1)}) custom-call(s32[2]{0:T(128)} %pad_add_fusion._.half_ref, f32[768,1]{1,0:T(8,128)} %broadcast_in_dim.15.s_ref, bf16[768,2048]{1,0:T(8,128)(2,1)} %get-tuple-element.87.refs_0_, bf16[768,2048]{1,0:T(8,128)(2,1)} %collective-permute-done.20.refs_1_, ...), custom_call_target="tpu_custom_call" | custom-call | bytes 14157312 | tf_op jit(solution)/shard_map/pallas_call | solution.py:53
  227.0 4.0 collective-permute-done.23.o_ref.refs_1_
  231.0 19.9 %shard_map.148.rest_0_ = f32[768,2048]{1,0:T(8,128)} custom-call(s32[2]{0:T(128)} %pad_add_fusion._.half_ref, bf16[768,2048]{1,0:T(8,128)(2,1)} %get-tuple-element.90.m_ref.refs_0_, bf16[768,2048]{1,0:T(8,128)(2,1)} %collective-permute-done.23.o_ref.refs_1_, bf16[2048,2048]{1,0:T(8,128)(2,1)} %get-tuple-element.91.wm_ref, ...), custom_call_target="tpu_custom_call" | custom-call | flops 12884901888 | bytes 29360128 | tf_op jit(solution)/shard_map/pallas_call | solution.py:53
  250.9 20.1 %shard_map.149 = (bf16[2048,3584]{1,0:T(8,128)(2,1)}, bf16[2048,3584]{1,0:T(8,128)(2,1)}) custom-call(s32[2]{0:T(128)} %pad_add_fusion._.half_ref, bf16[2048,768]{1,0:T(8,128)(2,1)} %shard_map.141.x_ref, bf16[768,2048]{1,0:T(8,128)(2,1)} %get-tuple-element.90.m_ref.refs_0_, bf16[768,2048]{1,0:T(8,128)(2,1)} %collective-permute-done.23.o_ref.refs_1_, ...), custom_call_target="tpu_custom_call" | custom-call | flops 12884901888 | bytes 26214400 | tf_op jit(solution)/shard_map/pallas_call | solution.py:53
  271.0 7.8 %collective-permute-done.24.refs_1_ = bf16[768,1536]{1,0:T(8,128)(2,1)} collective-permute-done((bf16[768,1536]{1,0:T(8,128)(2,1)S(1)}, bf16[768,1536]{1,0:T(8,128)(2,1)}, u32[]{:S(2)}, u32[]{:S(2)}) %collective-permute-start.24) | collective-permute-done | bytes 2359328 | tf_op jit(solution)/shard_map/ppermute | solution.py:425
  278.8 5.3 %shard_map.150.refs_4_.refs_2_ = bf16[768,768]{1,0:T(8,128)(2,1)} custom-call(s32[2]{0:T(128)} %pad_add_fusion._.half_ref, f32[768,1]{1,0:T(8,128)} %broadcast_in_dim.15.s_ref, bf16[768,1536]{1,0:T(8,128)(2,1)} %get-tuple-element.96.refs_0_, bf16[768,1536]{1,0:T(8,128)(2,1)} %collective-permute-done.24.refs_1_), custom_call_target="tpu_custom_call" | custom-call | bytes 8259072 | tf_op jit(solution)/shard_map/pallas_call | solution.py:53
  288.2 18.0 %shard_map.151 = bf16[768,2048]{1,0:T(8,128)(2,1)} custom-call(s32[2]{0:T(128)} %pad_add_fusion._.half_ref, bf16[768,1024]{1,0:T(8,128)(2,1)} %get-tuple-element.89.refs_0_, bf16[2048,2048]{1,0:T(8,128)(2,1)} %shard_map.136.refs_8_.refs_1_.refs_3_, bf16[768,1024]{1,0:T(8,128)(2,1)} %collective-permute-done.22.refs_2_.refs_1_, ...), custom_call_target="tpu_custom_call" | custom-call | flops 11274289152 | bytes 23330816 | tf_op jit(solution)/shard_map/pallas_call | solution.py:53
  306.2 6.3 %collective-permute-done.33.refs_3_ = bf16[768,768]{1,0:T(8,128)(2,1)S(1)} collective-permute-done((bf16[768,768]{1,0:T(8,128)(2,1)S(1)}, bf16[768,768]{1,0:T(8,128)(2,1)S(1)}, u32[]{:S(2)}, u32[]{:S(2)}) %collective-permute-start.33) | collective-permute-done | bytes 1179680 | tf_op jit(solution)/shard_map/ppermute | solution.py:425
  313.6 7.4 %shard_map.152.m_ref.refs_0_ = bf16[768,1536]{1,0:T(8,128)(2,1)} custom-call(s32[2]{0:T(128)} %pad_add_fusion._.half_ref, f32[768,1]{1,0:T(8,128)} %broadcast_in_dim.15.s_ref, bf16[768,1536]{1,0:T(8,128)(2,1)} %get-tuple-element.96.refs_0_, bf16[768,1536]{1,0:T(8,128)(2,1)} %collective-permute-done.24.refs_1_, bf16[768,768]{1,0:T(8,128)(2,1)} %shard_map.146.refs_2_, ...), custom_call_target="tpu_custom_call" | custom-call | bytes 10618368 | tf_op jit(solution)/shard_map/pallas_call | solution.py:53
  321.0 1.9 fusion.12
  327.2 17.3 %shard_map.153 = bf16[768,2048]{1,0:T(8,128)(2,1)} custom-call(s32[2]{0:T(128)} %pad_add_fusion._.half_ref, bf16[768,1536]{1,0:T(8,128)(2,1)} %shard_map.152.m_ref.refs_0_, bf16[768,1536]{1,0:T(8,128)(2,1)} %copy-done, bf16[2048,1536]{1,0:T(8,128)(2,1)} %get-tuple-element.99.wm_ref, bf16[2048,1536]{1,0:T(8,128)(2,1)} %get-tuple-element.100.wo_ref, ...), custom_call_target="tpu_custom_call" | custom-call | flops 9663676416 | bytes 23592960 | tf_op jit(solution)/shard_map/pallas_call | solution.py:53
  349.8 8.1 %collective-permute-done.35 = bf16[96,2048]{1,0:T(8,128)(2,1)S(1)} collective-permute-done((bf16[96,2048]{1,0:T(8,128)(2,1)S(1)}, bf16[96,2048]{1,0:T(8,128)(2,1)S(1)}, u32[]{:S(2)}, u32[]{:S(2)}) %collective-permute-start.35) | collective-permute-done | bytes 393248 | tf_op jit(solution)/shard_map/ppermute | solution.py:516
  359.6 6.7 %collective-permute-done.27 = bf16[96,2048]{1,0:T(8,128)(2,1)S(1)} collective-permute-done((bf16[96,2048]{1,0:T(8,128)(2,1)S(1)}, bf16[96,2048]{1,0:T(8,128)(2,1)S(1)}, u32[]{:S(2)}, u32[]{:S(2)}) %collective-permute-start.27) | collective-permute-done | bytes 393248 | tf_op jit(solution)/shard_map/ppermute | solution.py:516
  369.8 5.0 %collective-permute-done.36 = bf16[96,2048]{1,0:T(8,128)(2,1)S(1)} collective-permute-done((bf16[96,2048]{1,0:T(8,128)(2,1)S(1)}, bf16[96,2048]{1,0:T(8,128)(2,1)S(1)}, u32[]{:S(2)}, u32[]{:S(2)}) %collective-permute-start.36) | collective-permute-done | bytes 393248 | tf_op jit(solution)/shard_map/ppermute | solution.py:516
  377.1 6.1 %collective-permute-done.28 = bf16[96,2048]{1,0:T(8,128)(2,1)S(1)} collective-permute-done((bf16[96,2048]{1,0:T(8,128)(2,1)S(1)}, bf16[96,2048]{1,0:T(8,128)(2,1)S(1)}, u32[]{:S(2)}, u32[]{:S(2)}) %collective-permute-start.28) | collective-permute-done | bytes 393248 | tf_op jit(solution)/shard_map/ppermute | solution.py:516
  383.2 2.3 add_convert_fusion.7
  387.5 4.1 collective-permute-done.37
  394.8 19.5 %shard_map.154 = bf16[3584,2048]{1,0:T(8,128)(2,1)} custom-call(s32[2]{0:T(128)} %pad_add_fusion._.half_ref, bf16[768,1024]{1,0:T(8,128)(2,1)} %get-tuple-element.89.refs_0_, bf16[768,1024]{1,0:T(8,128)(2,1)} %collective-permute-done.22.refs_2_.refs_1_, bf16[768,768]{1,0:T(8,128)(2,1)} %shard_map.150.refs_4_.refs_2_, bf16[768,768]{1,0:T(8,128)(2,1)} %copy-done.32, ...), custom_call_target="tpu_custom_call" | custom-call | flops 11274289152 | bytes 23330816 | tf_op jit(solution)/shard_map/pallas_call | solution.py:53
  414.3 8.4 %shard_map.155 = (bf16[2048,3584]{1,0:T(8,128)(2,1)}, bf16[2048,3584]{1,0:T(8,128)(2,1)}) custom-call(s32[2]{0:T(128)} %pad_add_fusion._.half_ref, bf16[2048,768]{1,0:T(8,128)(2,1)} %shard_map.141.x_ref, bf16[768,1536]{1,0:T(8,128)(2,1)} %shard_map.152.m_ref.refs_0_, bf16[768,1536]{1,0:T(8,128)(2,1)} %copy-done, ...), custom_call_target="tpu_custom_call", output_to_operand_aliasing={{0}: (6, {}), {1}: (7, {})} | custom-call | flops 3221225472 | bytes 8912896 | tf_op jit(solution)/shard_map/pallas_call | solution.py:53
  424.3 8.2 %shard_map.156 = (bf16[2048,3584]{1,0:T(8,128)(2,1)}, bf16[2048,3584]{1,0:T(8,128)(2,1)}) custom-call(s32[2]{0:T(128)} %pad_add_fusion._.half_ref, bf16[2048,768]{1,0:T(8,128)(2,1)} %shard_map.141.x_ref, bf16[768,1536]{1,0:T(8,128)(2,1)} %shard_map.152.m_ref.refs_0_, bf16[768,1536]{1,0:T(8,128)(2,1)} %copy-done, ...), custom_call_target="tpu_custom_call", output_to_operand_aliasing={{0}: (6, {}), {1}: (7, {})} | custom-call | flops 3221225472 | bytes 8912896 | tf_op jit(solution)/shard_map/pallas_call | solution.py:53
  434.6 8.4 %shard_map.157 = (bf16[2048,3584]{1,0:T(8,128)(2,1)}, bf16[2048,3584]{1,0:T(8,128)(2,1)}) custom-call(s32[2]{0:T(128)} %pad_add_fusion._.half_ref, bf16[2048,768]{1,0:T(8,128)(2,1)} %shard_map.141.x_ref, bf16[768,1536]{1,0:T(8,128)(2,1)} %shard_map.152.m_ref.refs_0_, bf16[768,1536]{1,0:T(8,128)(2,1)} %copy-done, ...), custom_call_target="tpu_custom_call", output_to_operand_aliasing={{0}: (6, {}), {1}: (7, {})} | custom-call | flops 3221225472 | bytes 8912896 | tf_op jit(solution)/shard_map/pallas_call | solution.py:53
  444.6 2.1 collective-permute-done.45
  446.7 2.6 collective-permute-start.46
  449.2 3.0 fusion.7
  (167 shorter events, 65.6 us)
Async XLA Ops:
  1.7 15.8 %collective-permute-start = (bf16[96,2048]{1,0:T(8,128)(2,1)S(1)}, bf16[96,2048]{1,0:T(8,128)(2,1)S(1)}, u32[]{:S(2)}, u32[]{:S(2)}) collective-permute-start(bf16[96,2048]{1,0:T(8,128)(2,1)S(1)} %fusion.9.refs_0_), channel_id=1, source_target_pairs={{0,8},{8,16},{16,24},{24,28},{28,20},{20,12},{12,4},{4,0},{1,9},{9... | collective-permute-start | bytes 1179656 | tf_op jit(solution)/shard_map/ppermute | solution.py:448
  4.8 22.5 %collective-permute-start.1 = (bf16[96,2048]{1,0:T(8,128)(2,1)S(1)}, bf16[96,2048]{1,0:T(8,128)(2,1)S(1)}, u32[]{:S(2)}, u32[]{:S(2)}) collective-permute-start(bf16[96,2048]{1,0:T(8,128)(2,1)S(1)} %fusion.9.refs_0_), channel_id=1, source_target_pairs={{8,0},{16,8},{24,16},{28,24},{20,28},{12,20},{4,12},{0,4},{9,1},{1... | collective-permute-start | bytes 1179656 | tf_op jit(solution)/shard_map/ppermute | solution.py:450
  17.5 10.6 %collective-permute-start.2 = (bf16[96,2048]{1,0:T(8,128)(2,1)S(1)}, bf16[96,2048]{1,0:T(8,128)(2,1)S(1)}, u32[]{:S(2)}, u32[]{:S(2)}) collective-permute-start(bf16[96,2048]{1,0:T(8,128)(2,1)S(1)} %collective-permute-done.refs_1_), channel_id=1, source_target_pairs={{0,8},{8,16},{16,24},{24,28},{28,20},{20,12},{12,4},{4,0},{1,9},{9... | collective-permute-start | bytes 1179656 | tf_op jit(solution)/shard_map/ppermute | solution.py:448
  27.3 10.1 %collective-permute-start.3 = (bf16[96,2048]{1,0:T(8,128)(2,1)S(1)}, bf16[96,2048]{1,0:T(8,128)(2,1)S(1)}, u32[]{:S(2)}, u32[]{:S(2)}) collective-permute-start(bf16[96,2048]{1,0:T(8,128)(2,1)S(1)} %collective-permute-done.1.refs_2_), channel_id=1, source_target_pairs={{8,0},{16,8},{24,16},{28,24},{20,28},{12,20},{4,12},{0,4},{9,1},{1... | collective-permute-start | bytes 1179656 | tf_op jit(solution)/shard_map/ppermute | solution.py:450
  28.2 9.7 %collective-permute-start.4 = (bf16[96,2048]{1,0:T(8,128)(2,1)S(1)}, bf16[96,2048]{1,0:T(8,128)(2,1)S(1)}, u32[]{:S(2)}, u32[]{:S(2)}) collective-permute-start(bf16[96,2048]{1,0:T(8,128)(2,1)S(1)} %collective-permute-done.2.refs_3_), channel_id=1, source_target_pairs={{0,8},{8,16},{16,24},{24,28},{28,20},{20,12},{12,4},{4,0},{1,9},{9... | collective-permute-start | bytes 1179656 | tf_op jit(solution)/shard_map/ppermute | solution.py:448
  37.4 9.2 %collective-permute-start.5 = (bf16[96,2048]{1,0:T(8,128)(2,1)S(1)}, bf16[96,2048]{1,0:T(8,128)(2,1)S(1)}, u32[]{:S(2)}, u32[]{:S(2)}) collective-permute-start(bf16[96,2048]{1,0:T(8,128)(2,1)S(1)} %collective-permute-done.3.refs_4_), channel_id=1, source_target_pairs={{8,0},{16,8},{24,16},{28,24},{20,28},{12,20},{4,12},{0,4},{9,1},{1... | collective-permute-start | bytes 1179656 | tf_op jit(solution)/shard_map/ppermute | solution.py:450
  37.9 9.0 %collective-permute-start.6 = (bf16[96,2048]{1,0:T(8,128)(2,1)S(1)}, bf16[96,2048]{1,0:T(8,128)(2,1)S(1)}, u32[]{:S(2)}, u32[]{:S(2)}) collective-permute-start(bf16[96,2048]{1,0:T(8,128)(2,1)S(1)} %collective-permute-done.4.refs_5_), channel_id=1, source_target_pairs={{0,8},{8,16},{16,24},{24,28},{28,20},{20,12},{12,4},{4,0},{1,9},{9... | collective-permute-start | bytes 1179656 | tf_op jit(solution)/shard_map/ppermute | solution.py:448
  61.0 5.9 %collective-permute-start.7 = (bf16[768,2048]{1,0:T(8,128)(2,1)}, bf16[768,2048]{1,0:T(8,128)(2,1)S(1)}, u32[]{:S(2)}, u32[]{:S(2)}) collective-permute-start(bf16[768,2048]{1,0:T(8,128)(2,1)} %get-tuple-element.67), channel_id=1, source_target_pairs={{0,1},{1,0},{2,3},{3,2},{4,5},{5,4},{6,7},{7,6},{8,9},{9,8},{10,11... | collective-permute-start | bytes 9437192 | tf_op jit(solution)/shard_map/ppermute | solution.py:421
  92.6 34.6 %collective-permute-start.10 = (bf16[768,1536]{1,0:T(8,128)(2,1)}, bf16[768,1536]{1,0:T(8,128)(2,1)}, u32[]{:S(2)}, u32[]{:S(2)}) collective-permute-start(bf16[768,1536]{1,0:T(8,128)(2,1)} %get-tuple-element.71), channel_id=1, source_target_pairs={{0,1},{1,0},{2,3},{3,2},{4,5},{5,4},{6,7},{7,6},{8,9},{9,8},{10,11... | collective-permute-start | bytes 7077896 | tf_op jit(solution)/shard_map/ppermute | solution.py:421
  92.8 11.4 %collective-permute-start.11 = (bf16[96,2048]{1,0:T(8,128)(2,1)S(1)}, bf16[96,2048]{1,0:T(8,128)(2,1)S(1)}, u32[]{:S(2)}, u32[]{:S(2)}) collective-permute-start(bf16[96,2048]{1,0:T(8,128)(2,1)S(1)} %copy-done.9), channel_id=1, source_target_pairs={{0,8},{8,16},{16,24},{24,28},{28,20},{20,12},{12,4},{4,0},{1,9},{9... | collective-permute-start | bytes 1179656 | tf_op jit(solution)/shard_map/ppermute | solution.py:448
  94.3 17.9 %collective-permute-start.12 = (bf16[96,2048]{1,0:T(8,128)(2,1)S(1)}, bf16[96,2048]{1,0:T(8,128)(2,1)S(1)}, u32[]{:S(2)}, u32[]{:S(2)}) collective-permute-start(bf16[96,2048]{1,0:T(8,128)(2,1)S(1)} %copy-done.9), channel_id=1, source_target_pairs={{8,0},{16,8},{24,16},{28,24},{20,28},{12,20},{4,12},{0,4},{9,1},{1... | collective-permute-start | bytes 1179656 | tf_op jit(solution)/shard_map/ppermute | solution.py:450
  104.2 10.5 %collective-permute-start.13 = (bf16[96,2048]{1,0:T(8,128)(2,1)S(1)}, bf16[96,2048]{1,0:T(8,128)(2,1)S(1)}, u32[]{:S(2)}, u32[]{:S(2)}) collective-permute-start(bf16[96,2048]{1,0:T(8,128)(2,1)S(1)} %collective-permute-done.11.refs_1_.refs_5_), channel_id=1, source_target_pairs={{0,8},{8,16},{16,24},{24,28},{28,20},{20,12},{12,4},{4,0},{1,9},{9... | collective-permute-start | bytes 1179656 | tf_op jit(solution)/shard_map/ppermute | solution.py:448
  105.9 1.2 collective-permute-start.8
  107.1 3.6 collective-permute-start.9
  110.7 69.6 %collective-permute-start.20 = (bf16[768,2048]{1,0:T(8,128)(2,1)}, bf16[768,2048]{1,0:T(8,128)(2,1)}, u32[]{:S(2)}, u32[]{:S(2)}) collective-permute-start(bf16[768,2048]{1,0:T(8,128)(2,1)} %get-tuple-element.87.refs_0_), channel_id=1, source_target_pairs={{0,2},{1,3},{2,0},{3,1},{4,6},{5,7},{6,4},{7,5},{8,10},{9,11},{10,... | collective-permute-start | bytes 9437192 | tf_op jit(solution)/shard_map/ppermute | solution.py:425
  112.2 12.9 %collective-permute-start.14 = (bf16[96,2048]{1,0:T(8,128)(2,1)S(1)}, bf16[96,2048]{1,0:T(8,128)(2,1)S(1)}, u32[]{:S(2)}, u32[]{:S(2)}) collective-permute-start(bf16[96,2048]{1,0:T(8,128)(2,1)S(1)} %collective-permute-done.12.refs_2_.refs_6_), channel_id=1, source_target_pairs={{8,0},{16,8},{24,16},{28,24},{20,28},{12,20},{4,12},{0,4},{9,1},{1... | collective-permute-start | bytes 1179656 | tf_op jit(solution)/shard_map/ppermute | solution.py:450
  114.8 11.0 %collective-permute-start.15 = (bf16[96,2048]{1,0:T(8,128)(2,1)S(1)}, bf16[96,2048]{1,0:T(8,128)(2,1)S(1)}, u32[]{:S(2)}, u32[]{:S(2)}) collective-permute-start(bf16[96,2048]{1,0:T(8,128)(2,1)S(1)} %collective-permute-done.13.refs_3_.refs_7_), channel_id=1, source_target_pairs={{0,8},{8,16},{16,24},{24,28},{28,20},{20,12},{12,4},{4,0},{1,9},{9... | collective-permute-start | bytes 1179656 | tf_op jit(solution)/shard_map/ppermute | solution.py:448
  125.1 13.5 %collective-permute-start.16 = (bf16[96,2048]{1,0:T(8,128)(2,1)S(1)}, bf16[96,2048]{1,0:T(8,128)(2,1)S(1)}, u32[]{:S(2)}, u32[]{:S(2)}) collective-permute-start(bf16[96,2048]{1,0:T(8,128)(2,1)S(1)} %collective-permute-done.14.refs_4_.refs_8_), channel_id=1, source_target_pairs={{8,0},{16,8},{24,16},{28,24},{20,28},{12,20},{4,12},{0,4},{9,1},{1... | collective-permute-start | bytes 1179656 | tf_op jit(solution)/shard_map/ppermute | solution.py:450
  125.8 12.9 %collective-permute-start.17 = (bf16[96,2048]{1,0:T(8,128)(2,1)S(1)}, bf16[96,2048]{1,0:T(8,128)(2,1)S(1)}, u32[]{:S(2)}, u32[]{:S(2)}) collective-permute-start(bf16[96,2048]{1,0:T(8,128)(2,1)S(1)} %collective-permute-done.15.refs_5_.refs_9_), channel_id=1, source_target_pairs={{0,8},{8,16},{16,24},{24,28},{28,20},{20,12},{12,4},{4,0},{1,9},{9... | collective-permute-start | bytes 1179656 | tf_op jit(solution)/shard_map/ppermute | solution.py:448
  148.5 7.2 %collective-permute-start.18 = (bf16[768,1024]{1,0:T(8,128)(2,1)}, bf16[768,1024]{1,0:T(8,128)(2,1)S(1)}, u32[]{:S(2)}, u32[]{:S(2)}) collective-permute-start(bf16[768,1024]{1,0:T(8,128)(2,1)} %shard_map.143), channel_id=1, source_target_pairs={{0,1},{1,0},{2,3},{3,2},{4,5},{5,4},{6,7},{7,6},{8,9},{9,8},{10,11... | collective-permute-start | bytes 4718600 | tf_op jit(solution)/shard_map/ppermute | solution.py:421
  180.3 35.0 %collective-permute-start.21 = (bf16[768,1024]{1,0:T(8,128)(2,1)}, bf16[768,1024]{1,0:T(8,128)(2,1)S(1)}, u32[]{:S(2)}, u32[]{:S(2)}) collective-permute-start(bf16[768,1024]{1,0:T(8,128)(2,1)} %shard_map.145.refs_2_), channel_id=1, source_target_pairs={{0,2},{1,3},{2,0},{3,1},{4,6},{5,7},{6,4},{7,5},{8,10},{9,11},{10,... | collective-permute-start | bytes 4718600 | tf_op jit(solution)/shard_map/ppermute | solution.py:425
  181.8 3.1 collective-permute-start.19
  193.4 32.1 %copy-start.11 = (bf16[768,1536]{1,0:T(8,128)(2,1)S(1)}, bf16[768,1536]{1,0:T(8,128)(2,1)}, u32[]{:S(2)}) copy-start(bf16[768,1536]{1,0:T(8,128)(2,1)} %get-tuple-element.96.refs_0_) | copy-start | bytes 7077892
  225.0 6.0 %collective-permute-start.23 = (bf16[768,2048]{1,0:T(8,128)(2,1)}, bf16[768,2048]{1,0:T(8,128)(2,1)}, u32[]{:S(2)}, u32[]{:S(2)}) collective-permute-start(bf16[768,2048]{1,0:T(8,128)(2,1)} %get-tuple-element.90.m_ref.refs_0_), channel_id=1, source_target_pairs={{0,1},{1,0},{2,3},{3,2},{4,5},{5,4},{6,7},{7,6},{8,9},{9,8},{10,11... | collective-permute-start | bytes 9437192 | tf_op jit(solution)/shard_map/ppermute | solution.py:421
  225.0 60.7 %collective-permute-start.22 = (bf16[768,1024]{1,0:T(8,128)(2,1)}, bf16[768,1024]{1,0:T(8,128)(2,1)}, u32[]{:S(2)}, u32[]{:S(2)}) collective-permute-start(bf16[768,1024]{1,0:T(8,128)(2,1)} %get-tuple-element.89.refs_0_), channel_id=1, source_target_pairs={{0,1},{1,0},{2,3},{3,2},{4,5},{5,4},{6,7},{7,6},{8,9},{9,8},{10,11... | collective-permute-start | bytes 4718600 | tf_op jit(solution)/shard_map/ppermute | solution.py:421
  225.5 53.3 %collective-permute-start.24 = (bf16[768,1536]{1,0:T(8,128)(2,1)S(1)}, bf16[768,1536]{1,0:T(8,128)(2,1)}, u32[]{:S(2)}, u32[]{:S(2)}) collective-permute-start(bf16[768,1536]{1,0:T(8,128)(2,1)S(1)} %copy-done.11), channel_id=1, source_target_pairs={{0,2},{1,3},{2,0},{3,1},{4,6},{5,7},{6,4},{7,5},{8,10},{9,11},{10,... | collective-permute-start | bytes 7077896 | tf_op jit(solution)/shard_map/ppermute | solution.py:425
  284.2 3.1 collective-permute-start.25
  284.2 28.4 %collective-permute-start.33 = (bf16[768,768]{1,0:T(8,128)(2,1)S(1)}, bf16[768,768]{1,0:T(8,128)(2,1)S(1)}, u32[]{:S(2)}, u32[]{:S(2)}) collective-permute-start(bf16[768,768]{1,0:T(8,128)(2,1)S(1)} %copy-done.19), channel_id=1, source_target_pairs={{0,2},{1,3},{2,0},{3,1},{4,6},{5,7},{6,4},{7,5},{8,10},{9,11},{10,... | collective-permute-start | bytes 3538952 | tf_op jit(solution)/shard_map/ppermute | solution.py:425
  321.0 4.7 %collective-permute-start.34 = (bf16[768,1536]{1,0:T(8,128)(2,1)}, bf16[768,1536]{1,0:T(8,128)(2,1)S(1)}, u32[]{:S(2)}, u32[]{:S(2)}) collective-permute-start(bf16[768,1536]{1,0:T(8,128)(2,1)} %shard_map.152.m_ref.refs_0_), channel_id=1, source_target_pairs={{0,1},{1,0},{2,3},{3,2},{4,5},{5,4},{6,7},{7,6},{8,9},{9,8},{10,11... | collective-permute-start | bytes 7077896 | tf_op jit(solution)/shard_map/ppermute | solution.py:421
  322.9 23.5 %collective-permute-start.26 = (bf16[96,2048]{1,0:T(8,128)(2,1)}, bf16[96,2048]{1,0:T(8,128)(2,1)}, u32[]{:S(2)}, u32[]{:S(2)}) collective-permute-start(bf16[96,2048]{1,0:T(8,128)(2,1)} %get-tuple-element.124), channel_id=1, source_target_pairs={{8,0},{16,8},{24,16},{28,24},{20,28},{12,20},{4,12},{0,4},{9,1},{1... | collective-permute-start | bytes 1179656 | tf_op jit(solution)/shard_map/ppermute | solution.py:516
  323.5 36.1 %collective-permute-start.30 = (bf16[96,2048]{1,0:T(8,128)(2,1)S(1)}, bf16[96,2048]{1,0:T(8,128)(2,1)S(1)}, u32[]{:S(2)}, u32[]{:S(2)}) collective-permute-start(bf16[96,2048]{1,0:T(8,128)(2,1)S(1)} %get-tuple-element.125), channel_id=1, source_target_pairs={{0,8},{8,16},{16,24},{24,28},{28,20},{20,12},{12,4},{4,0},{1,9},{9... | collective-permute-start | bytes 1179656 | tf_op jit(solution)/shard_map/ppermute | solution.py:520
  345.8 12.0 %collective-permute-start.35 = (bf16[96,2048]{1,0:T(8,128)(2,1)S(1)}, bf16[96,2048]{1,0:T(8,128)(2,1)S(1)}, u32[]{:S(2)}, u32[]{:S(2)}) collective-permute-start(bf16[96,2048]{1,0:T(8,128)(2,1)S(1)} %get-tuple-element.118), channel_id=1, source_target_pairs={{8,0},{16,8},{24,16},{28,24},{20,28},{12,20},{4,12},{0,4},{9,1},{1... | collective-permute-start | bytes 1179656 | tf_op jit(solution)/shard_map/ppermute | solution.py:516
  347.7 18.6 %collective-permute-start.27 = (bf16[96,2048]{1,0:T(8,128)(2,1)S(1)}, bf16[96,2048]{1,0:T(8,128)(2,1)S(1)}, u32[]{:S(2)}, u32[]{:S(2)}) collective-permute-start(bf16[96,2048]{1,0:T(8,128)(2,1)S(1)} %add_convert_fusion.9), channel_id=1, source_target_pairs={{8,0},{16,8},{24,16},{28,24},{20,28},{12,20},{4,12},{0,4},{9,1},{1... | collective-permute-start | bytes 1179656 | tf_op jit(solution)/shard_map/ppermute | solution.py:516
  349.1 20.6 %collective-permute-start.39 = (bf16[96,2048]{1,0:T(8,128)(2,1)S(1)}, bf16[96,2048]{1,0:T(8,128)(2,1)S(1)}, u32[]{:S(2)}, u32[]{:S(2)}) collective-permute-start(bf16[96,2048]{1,0:T(8,128)(2,1)S(1)} %get-tuple-element.119), channel_id=1, source_target_pairs={{0,8},{8,16},{16,24},{24,28},{28,20},{20,12},{12,4},{4,0},{1,9},{9... | collective-permute-start | bytes 1179656 | tf_op jit(solution)/shard_map/ppermute | solution.py:520
  359.0 15.8 %collective-permute-start.36 = (bf16[96,2048]{1,0:T(8,128)(2,1)S(1)}, bf16[96,2048]{1,0:T(8,128)(2,1)S(1)}, u32[]{:S(2)}, u32[]{:S(2)}) collective-permute-start(bf16[96,2048]{1,0:T(8,128)(2,1)S(1)} %add_convert_fusion.4), channel_id=1, source_target_pairs={{8,0},{16,8},{24,16},{28,24},{20,28},{12,20},{4,12},{0,4},{9,1},{1... | collective-permute-start | bytes 1179656 | tf_op jit(solution)/shard_map/ppermute | solution.py:516
  367.7 15.5 %collective-permute-start.28 = (bf16[96,2048]{1,0:T(8,128)(2,1)S(1)}, bf16[96,2048]{1,0:T(8,128)(2,1)S(1)}, u32[]{:S(2)}, u32[]{:S(2)}) collective-permute-start(bf16[96,2048]{1,0:T(8,128)(2,1)S(1)} %get-tuple-element.122), channel_id=1, source_target_pairs={{8,0},{16,8},{24,16},{28,24},{20,28},{12,20},{4,12},{0,4},{9,1},{1... | collective-permute-start | bytes 1179656 | tf_op jit(solution)/shard_map/ppermute | solution.py:516
  368.3 14.8 %collective-permute-start.31 = (bf16[96,2048]{1,0:T(8,128)(2,1)S(1)}, bf16[96,2048]{1,0:T(8,128)(2,1)S(1)}, u32[]{:S(2)}, u32[]{:S(2)}) collective-permute-start(bf16[96,2048]{1,0:T(8,128)(2,1)S(1)} %get-tuple-element.123), channel_id=1, source_target_pairs={{0,8},{8,16},{16,24},{24,28},{28,20},{20,12},{12,4},{4,0},{1,9},{9... | collective-permute-start | bytes 1179656 | tf_op jit(solution)/shard_map/ppermute | solution.py:520
  375.0 16.6 %collective-permute-start.37 = (bf16[96,2048]{1,0:T(8,128)(2,1)S(1)}, bf16[96,2048]{1,0:T(8,128)(2,1)S(1)}, u32[]{:S(2)}, u32[]{:S(2)}) collective-permute-start(bf16[96,2048]{1,0:T(8,128)(2,1)S(1)} %get-tuple-element.116), channel_id=1, source_target_pairs={{8,0},{16,8},{24,16},{28,24},{20,28},{12,20},{4,12},{0,4},{9,1},{1... | collective-permute-start | bytes 1179656 | tf_op jit(solution)/shard_map/ppermute | solution.py:516
  375.6 16.0 %collective-permute-start.40 = (bf16[96,2048]{1,0:T(8,128)(2,1)S(1)}, bf16[96,2048]{1,0:T(8,128)(2,1)S(1)}, u32[]{:S(2)}, u32[]{:S(2)}) collective-permute-start(bf16[96,2048]{1,0:T(8,128)(2,1)S(1)} %get-tuple-element.117), channel_id=1, source_target_pairs={{0,8},{8,16},{16,24},{24,28},{28,20},{20,12},{12,4},{4,0},{1,9},{9... | collective-permute-start | bytes 1179656 | tf_op jit(solution)/shard_map/ppermute | solution.py:520
  385.5 63.8 %collective-permute-start.32 = (bf16[96,2048]{1,0:T(8,128)(2,1)}, bf16[96,2048]{1,0:T(8,128)(2,1)}, u32[]{:S(2)}, u32[]{:S(2)}) collective-permute-start(bf16[96,2048]{1,0:T(8,128)(2,1)} %get-tuple-element.121), channel_id=1, source_target_pairs={{0,8},{8,16},{16,24},{24,28},{28,20},{20,12},{12,4},{4,0},{1,9},{9... | collective-permute-start | bytes 1179656 | tf_op jit(solution)/shard_map/ppermute | solution.py:520
  387.0 62.2 %collective-permute-start.29 = (bf16[96,2048]{1,0:T(8,128)(2,1)}, bf16[96,2048]{1,0:T(8,128)(2,1)}, u32[]{:S(2)}, u32[]{:S(2)}) collective-permute-start(bf16[96,2048]{1,0:T(8,128)(2,1)} %get-tuple-element.120), channel_id=1, source_target_pairs={{8,0},{16,8},{24,16},{28,24},{20,28},{12,20},{4,12},{0,4},{9,1},{1... | collective-permute-start | bytes 1179656 | tf_op jit(solution)/shard_map/ppermute | solution.py:516
  392.7 29.9 %collective-permute-start.41 = (bf16[96,2048]{1,0:T(8,128)(2,1)}, bf16[96,2048]{1,0:T(8,128)(2,1)S(1)}, u32[]{:S(2)}, u32[]{:S(2)}) collective-permute-start(bf16[96,2048]{1,0:T(8,128)(2,1)} %get-tuple-element.115), channel_id=1, source_target_pairs={{0,8},{8,16},{16,24},{24,28},{28,20},{20,12},{12,4},{4,0},{1,9},{9... | collective-permute-start | bytes 1179656 | tf_op jit(solution)/shard_map/ppermute | solution.py:520
  394.3 28.3 %collective-permute-start.38 = (bf16[96,2048]{1,0:T(8,128)(2,1)}, bf16[96,2048]{1,0:T(8,128)(2,1)}, u32[]{:S(2)}, u32[]{:S(2)}) collective-permute-start(bf16[96,2048]{1,0:T(8,128)(2,1)} %get-tuple-element.114), channel_id=1, source_target_pairs={{8,0},{16,8},{24,16},{28,24},{20,28},{12,20},{4,12},{0,4},{9,1},{1... | collective-permute-start | bytes 1179656 | tf_op jit(solution)/shard_map/ppermute | solution.py:516
  424.2 9.0 %collective-permute-start.42 = (f32[96]{0:T(128)S(1)}, f32[96]{0:T(128)S(1)}, u32[]{:S(2)}, u32[]{:S(2)}) collective-permute-start(f32[96]{0:T(128)S(1)} %get-tuple-element.113), channel_id=1, source_target_pairs={{0,1},{1,0},{2,3},{3,2},{4,5},{5,4},{6,7},{7,6},{8,9},{9,8},{10,11... | collective-permute-start | bytes 1160 | tf_op jit(solution)/shard_map/ppermute | solution.py:421
  432.6 10.4 %collective-permute-start.44 = (f32[2048]{0:T(1024)S(1)}, f32[2048]{0:T(1024)S(1)}, u32[]{:S(2)}, u32[]{:S(2)}) collective-permute-start(f32[2048]{0:T(1024)S(1)} %get-tuple-element.112), channel_id=1, source_target_pairs={{0,4},{4,0},{8,12},{12,8},{16,20},{20,16},{24,28},{28,24},{1,5},{5... | collective-permute-start | bytes 24584 | tf_op jit(solution)/shard_map/ppermute | solution.py:555
  433.2 11.3 %collective-permute-start.43 = (f32[96]{0:T(128)S(1)}, f32[96]{0:T(128)S(1)}, u32[]{:S(2)}, u32[]{:S(2)}) collective-permute-start(f32[96]{0:T(128)S(1)} %add.94), channel_id=1, source_target_pairs={{0,2},{1,3},{2,0},{3,1},{4,6},{5,7},{6,4},{7,5},{8,10},{9,11},{10,... | collective-permute-start | bytes 1160 | tf_op jit(solution)/shard_map/ppermute | solution.py:425
  443.0 3.7 collective-permute-start.45
  446.7 5.5 %collective-permute-start.46 = (f32[2048]{0:T(1024)S(1)}, f32[2048]{0:T(1024)S(1)}, u32[]{:S(2)}, u32[]{:S(2)}) collective-permute-start(f32[2048]{0:T(1024)S(1)} %add.98), channel_id=1, source_target_pairs={{0,16},{4,20},{8,24},{12,28},{16,0},{20,4},{24,8},{28,12},{1,17},{... | collective-permute-start | bytes 24584 | tf_op jit(solution)/shard_map/ppermute | solution.py:555
  (32 other events, 313.6 us)

commit v3 on v2

--- a/solution.py
+++ b/solution.py
@@ -78,24 +78,36 @@
             self.chunks.append((first, self.count - first))
 
 
-def mask_rows(plan, chunk, scalars, w_down, down_lanes):
+def chunk_tile(chunk):
     first, steps = chunk
+    return steps, lambda j: jnp.clip(j - first, 0, steps - 1)
+
+
+def mask_rows(plan, scalars, w_down, down_lanes):
     depth, tile = w_down.shape[1], plan.tile
 
-    def body(_, w_ref, k_ref, out_ref):
-        start = pl.program_id(0) * plan.count + first + pl.program_id(1)
-        for index in range(tile // BLOCK):
-            span = pl.ds(index * BLOCK, BLOCK)
-            keep = keep_rows(k_ref, start * (tile // BLOCK) + index, depth)
-            out_ref[span, :] = block_rows(w_ref[span, :], keep)
-
-    return call(
-        body, (CORES, steps), scalars, (w_down, down_lanes),
-        [pl.BlockSpec((tile, depth), lambda h, j, s: (h * plan.count + first + j, 0)),
+    def body(_, w_ref, k_ref, *outs):
+        half, step = pl.program_id(0), pl.program_id(1)
+        start = half * plan.count + step
+        for (first, steps), out_ref in zip(plan.chunks, outs):
+            @pl.when(jnp.logical_and(step >= first, step < first + steps))
+            def _(out_ref=out_ref):
+                for index in range(tile // BLOCK):
+                    span = pl.ds(index * BLOCK, BLOCK)
+                    keep = keep_rows(k_ref, start * (tile // BLOCK) + index, depth)
+                    out_ref[span, :] = block_rows(w_ref[span, :], keep)
+
+    out_specs, shapes = [], []
+    for chunk in plan.chunks:
+        steps, local = chunk_tile(chunk)
+        out_specs.append(pl.BlockSpec(
+            (tile, depth), lambda h, j, s, n=steps, f=local: (h * n + f(j), 0)))
+        shapes.append(jax.ShapeDtypeStruct((CORES * steps * tile, depth), bf16))
+    return call(
+        body, (CORES, plan.count), scalars, (w_down, down_lanes),
+        [pl.BlockSpec((tile, depth), lambda h, j, s: (h * plan.count + j, 0)),
          whole(down_lanes)],
-        pl.BlockSpec((tile, depth), lambda h, j, s: (h * steps + j, 0)),
-        jax.ShapeDtypeStruct((CORES * steps * tile, depth), bf16), [],
-        0, 4 * CORES * depth * steps * tile)
+        out_specs, shapes, [], 0, 4 * w_down.size)
 
 
 def gathered(shards, scratch):
@@ -160,30 +172,46 @@
         2 * rows * depth * width, 4 * depth * width + 2 * rows * depth + 4 * rows * width)
 
 
-def back_project(side, halves, tokens, weight, added=None):
+def back_project(side, plan, halves, tokens, weights, added=None):
     local, depth = tokens[0].shape
-    rows, count = local * len(tokens), len(tokens)
-    width = weight.shape[0] // CORES
-    tile = tile_of(width, 256)
-    steps = width // tile
+    rows, count, tile = local * len(tokens), len(tokens), plan.tile
+    parts = len(plan.chunks)
 
     def body(_, *refs):
-        scratch, out_ref, w_ref = refs[-1], refs[-2], refs[count]
+        scratch = refs[-1]
         gathered(refs[:count], scratch)
-        value = dot(scratch[...], w_ref[...], 1, 1)
-        if added is not None:
-            value += refs[count + 1][...].astype(f32)
-        out_ref[...] = value.astype(bf16)
-
-    out = pl.BlockSpec((rows, tile), lambda i, h: (0, i))
-    extra = () if added is None else (added,)
-    return call(
-        body, (steps,), halves, (*tokens, weight, *extra),
-        [whole(value) for value in tokens]
-        + [pl.BlockSpec((tile, depth), lambda i, h: (h[side] * steps + i, 0))]
-        + [out] * len(extra),
-        out, jax.ShapeDtypeStruct((rows, width), bf16), [pltpu.VMEM((rows, depth), bf16)],
-        2 * rows * depth * width, 2 * depth * width + 2 * rows * depth + 2 * rows * width)
+        w_refs = refs[count:count + parts]
+        rest = refs[count + parts:-1]
+        outs = rest if added is None else rest[1:]
+        step = pl.program_id(0)
+        for index, (first, steps) in enumerate(plan.chunks):
+            @pl.when(jnp.logical_and(step >= first, step < first + steps))
+            def _(w_ref=w_refs[index], out_ref=outs[index if len(outs) > 1 else 0]):
+                value = dot(scratch[...], w_ref[...], 1, 1)
+                if added is not None:
+                    value += rest[0][...].astype(f32)
+                out_ref[...] = value.astype(bf16)
+
+    in_specs = [whole(value) for value in tokens]
+    out = pl.BlockSpec((rows, tile), lambda j, h: (0, j))
+    out_specs, shapes = [], []
+    for chunk in plan.chunks:
+        steps, place = chunk_tile(chunk)
+        in_specs.append(pl.BlockSpec(
+            (tile, depth), lambda j, h, n=steps, f=place: (h[side] * n + f(j), 0)))
+        out_specs.append(pl.BlockSpec((rows, tile), lambda j, h, f=place: (0, f(j))))
+        shapes.append(jax.ShapeDtypeStruct((rows, steps * tile), bf16))
+    extra = ()
+    if added is None:
+        out_specs, shapes = [out], [jax.ShapeDtypeStruct((rows, plan.half), bf16)]
+    else:
+        extra = (added,)
+        in_specs.append(out)
+    return call(
+        body, (plan.count,), halves, (*tokens, *weights, *extra), in_specs,
+        out_specs, shapes, [pltpu.VMEM((rows, depth), bf16)],
+        2 * rows * depth * plan.half,
+        2 * depth * plan.half + 2 * rows * depth + 2 * rows * plan.half)
 
 
 def activate(plan, scalars, scale, pair, grads, with_hidden):
@@ -231,30 +259,26 @@
         out_specs, shapes, [], 0, 2 * sum(a.size for a in operands) + 3 * rows * width)
 
 
-def down_product(halves, hidden, weights):
-    rows, depth = hidden[0][0].shape[0], weights[0].shape[1]
+def down_product(halves, pair, weight, added, dtype):
+    rows, width = pair[0].shape
+    depth = weight.shape[1]
     tile = tile_of(depth, 256)
-    operands, in_specs = [], []
-    for pair, weight in zip(hidden, weights):
-        width = weight.shape[0] // CORES
-        for side, value in enumerate(pair):
-            operands += [value, weight]
-            in_specs += [whole(value), pl.BlockSpec(
-                (width, tile), lambda i, h, side=side: (h[side], i))]
-
-    def body(_, *refs):
-        value = None
-        for h_ref, w_ref in zip(refs[:-1:2], refs[1:-1:2]):
-            term = dot(h_ref[...], w_ref[...], 1, 0)
-            value = term if value is None else value + term
-        refs[-1][...] = value.astype(bf16)
-
-    total = sum(weight.size for weight in weights)
-    return call(
-        body, (depth // tile,), halves, operands, in_specs,
-        pl.BlockSpec((rows, tile), lambda i, h: (0, i)),
-        jax.ShapeDtypeStruct((rows, depth), bf16), [],
-        2 * rows * total, 2 * total + 2 * rows * (total // depth + depth))
+    out = pl.BlockSpec((rows, tile), lambda i, h: (0, i))
+    extra = () if added is None else (added,)
+
+    def body(_, m_ref, o_ref, wm_ref, wo_ref, *rest):
+        value = dot(m_ref[...], wm_ref[...], 1, 0) + dot(o_ref[...], wo_ref[...], 1, 0)
+        if added is not None:
+            value += rest[0][...]
+        rest[-1][...] = value.astype(dtype)
+
+    return call(
+        body, (depth // tile,), halves, (*pair, weight, weight, *extra),
+        [whole(pair[0]), whole(pair[1]),
+         pl.BlockSpec((width, tile), lambda i, h: (h[0], i)),
+         pl.BlockSpec((width, tile), lambda i, h: (h[1], i))] + [out] * len(extra),
+        out, jax.ShapeDtypeStruct((rows, depth), dtype), [],
+        2 * rows * weight.size, 2 * weight.size + 4 * rows * width + 4 * rows * depth)
 
 
 def input_cotangent(scalars, pair, weights, added, dtype):
@@ -353,51 +377,49 @@
         2 * rows * depth + 8 * rows * steps * tile + 8 * depth * steps * tile, aliases)
 
 
-def down_grads(plan, halves, hidden, grads, down_lanes):
-    rows, depth = hidden[0][0].shape[0], grads[0].shape[1]
-    tile = tile_of(depth, 256)
-    operands, places = [], []
-    for pair, (first, steps) in zip(hidden, plan.chunks):
-        for side, value in enumerate(pair):
-            operands.append(value)
-            places.append((side, first * plan.tile))
-    count = len(operands)
-    width = plan.half * CORES
+def down_grads(plan, chunk, halves, pair, grads, down_lanes, earlier):
+    first, steps = chunk
+    local, depth = grads[0].shape
+    count, tile = len(grads), plan.tile
+    rows = local * count
 
     def body(half_ref, *refs):
-        turned, right, out_ref = refs[-2], refs[-1], refs[-3]
+        right, left = refs[-2:]
+        gathered(refs[:count], right)
+        m_ref, o_ref, k_ref, out_ref = refs[count], refs[count + 1], refs[count + 2], refs[-3]
 
         @pl.when(pl.program_id(0) == 0)
         def _():
-            for ref, (side, first) in zip(refs[:count], places):
-                start = pl.multiple_of(half_ref[side] * plan.half + first, 128)
-                for lane in range(0, ref.shape[1], plan.tile):
-                    turned[pl.ds(start + lane, plan.tile), :] = ref[:, lane:lane + plan.tile].T
-
-        row = 0
-        for ref in refs[count:count + len(grads)]:
-            right[row:row + ref.shape[0], :] = ref[...]
-            row += ref.shape[0]
-        k_ref = refs[count + len(grads)]
-        piece = plan.tile
-        for part in range(width // piece):
-            value = dot(turned[part * piece:(part + 1) * piece, :], right[...], 1, 0).astype(bf16)
-            for block in range(piece // BLOCK):
-                low = part * piece + block * BLOCK
-                out_ref[low:low + BLOCK, :] = block_rows(
-                    value[block * BLOCK:(block + 1) * BLOCK, :],
-                    keep_rows(k_ref, low // BLOCK, tile))
-
-    column = lambda i, h: (0, i)
-    return call(
-        body, (depth // tile,), halves, (*operands, *grads, down_lanes),
-        [whole(value) for value in operands]
-        + [pl.BlockSpec((g.shape[0], tile), column) for g in grads]
-        + [pl.BlockSpec((down_lanes.shape[0], tile), column)],
-        pl.BlockSpec((width, tile), column),
-        jax.ShapeDtypeStruct((width, depth), bf16),
-        [pltpu.VMEM((width, rows), bf16), pltpu.VMEM((rows, tile), bf16)],
-        2 * rows * depth * width, 2 * depth * width + 2 * rows * width + 2 * rows * depth)
+            left[...] = m_ref[...].T
+
+        @pl.when(pl.program_id(0) == 1)
+        def _():
+            left[...] = o_ref[...].T
+
+        value = dot(left[...], right[...], 1, 0).astype(bf16)
+        start = half_ref[pl.program_id(0)] * plan.count + first + pl.program_id(1)
+        for block in range(tile // BLOCK):
+            span = slice(block * BLOCK, (block + 1) * BLOCK)
+            out_ref[span, :] = block_rows(
+                value[span, :], keep_rows(k_ref, start * (tile // BLOCK) + block, depth))
+
+    operands = [*grads, *pair, down_lanes]
+    in_specs = [whole(g) for g in grads] + [
+        pl.BlockSpec((rows, tile), lambda p, j, h: (0, jnp.where(p == 0, j, steps - 1))),
+        pl.BlockSpec((rows, tile), lambda p, j, h: (0, jnp.where(p == 0, 0, j))),
+        whole(down_lanes)]
+    aliases = None
+    if earlier is not None:
+        aliases = {len(operands) + 1: 0}
+        operands.append(earlier)
+        in_specs.append(pl.BlockSpec(memory_space=pl.ANY))
+    return call(
+        body, (CORES, steps), halves, operands, in_specs,
+        pl.BlockSpec((tile, depth), lambda p, j, h: (h[p] * plan.count + first + j, 0)),
+        jax.ShapeDtypeStruct((CORES * plan.half, depth), bf16),
+        [pltpu.VMEM((rows, depth), bf16), pltpu.VMEM((tile, rows), bf16)],
+        4 * rows * depth * steps * tile,
+        4 * depth * steps * tile + 4 * rows * steps * tile + 2 * rows * depth, aliases)
 
 
 def after(value, *others):
@@ -452,14 +474,13 @@
     shard = {0: scaled}
     ring_step(shard, 1)
     down_lanes = lanes(mask_down)
-    dn = [mask_rows(plan, chunks[0], halves, w_down, down_lanes)]
-    ring_step(shard, 2, dn[0])
-    dn.append(mask_rows(plan, chunks[1], after(halves, dn[0]), w_down, down_lanes))
-    ring_step(shard, 3, dn[1])
-    gate_lanes = lanes(after(mask_gate, dn[1]))
-    up_lanes = lanes(after(mask_up, dn[1]))
+    gate_lanes = lanes(mask_gate)
+    up_lanes = lanes(mask_up)
+    ring_step(shard, 2, gate_lanes, up_lanes)
+    dn = mask_rows(plan, after(halves, shard[-1]), w_down, down_lanes)
+    ring_step(shard, 3, dn[0])
     for k in range(4, n_ahead + 1):
-        ring_step(shard, k, gate_lanes, up_lanes)
+        ring_step(shard, k)
     tokens = [shard[offset] for offset in offsets]
     weights = (w_gate, w_up, gate_lanes, up_lanes)
 
@@ -488,17 +509,19 @@
     own1, kept1_m = project(
         0, plan, chunks[1], after(halves, turned), tokens, weights, to_partner(sent1))
     grads = [grad_shard[offset] for offset in offsets]
-    sent_b0 = back_project(1, after(halves, own1), grads, dn[0])
-    sent_b1 = back_project(1, after(halves, sent_b0), grads, dn[1])
-    got_b1 = to_partner(sent_b1)
-    own_b0 = back_project(0, after(halves, sent_b1), grads, dn[0], to_partner(sent_b0))
+    sent_b, = back_project(1, plan, after(halves, own1), grads, dn)
+    own_b0, own_b1 = back_project(
+        0, plan, halves, grads, dn, to_partner(sent_b))
     others_b0 = from_chips(after(own_b0, *others0))
-    own_b1 = back_project(0, after(halves, own_b0), grads, dn[1], got_b1)
     others1 = from_chips(after(own1, *others_b0))
-    cot0, hidden0 = activate(plan, after(halves, own_b1), scale, [own0, *others0],
-                             [own_b0, *others_b0], True)
+    hidden0, = activate(plan, after(halves, own_b1), scale, [own0, *others0], None, True)
+    hidden0 = (hidden0, to_partner(hidden0))
+    mixed = down_product(halves, hidden0, dn[0], None, f32)
+    grad_w_down = down_grads(plan, chunks[0], after(halves, mixed), hidden0, grads,
+                             down_lanes, None)
+    halves = after(halves, grad_w_down)
+    cot0, = activate(plan, halves, scale, [own0, *others0], [own_b0, *others_b0], False)
     cot0 = (cot0, to_partner(cot0))
-    hidden0 = (hidden0, to_partner(hidden0))
     partial = input_cotangent(halves, cot0, (kept0_m, kept0_o), None, f32)
     grad_gu = gate_up_grads(plan, chunks[0], after(halves, partial), turned,
                             cot0[:1], cot0[1:], gate_lanes, up_lanes, None)
@@ -507,7 +530,9 @@
     hidden1, = activate(plan, after(halves, grad_gu[0]), scale, [own1, *others1],
                         None, True)
     hidden1 = (hidden1, to_partner(hidden1))
-    mixed = down_product(halves, (hidden0, hidden1), dn)
+    mixed = down_product(halves, hidden1, dn[1], mixed, bf16)
+    grad_w_down = down_grads(plan, chunks[1], after(halves, mixed), hidden1, grads,
+                             down_lanes, grad_w_down)
 
     def scatter(parts):
         back = parts(-n_ahead)
@@ -528,14 +553,12 @@
         return lambda offset: parts[offset]
 
     output = (inputs_wide + scatter(part_of(mixed))).astype(bf16)
-    cot1, = activate(plan, after(halves, mixed), scale, [own1, *others1],
+    cot1, = activate(plan, after(halves, grad_w_down), scale, [own1, *others1],
                      [own_b1, *others_b1], False)
     cot1 = (cot1, to_partner(cot1))
     norm_all = input_cotangent(halves, cot1, (kept1_m, kept1_o), partial, bf16)
     d_norm_in = scatter(part_of(norm_all))
-    grad_w_down = down_grads(plan, after(halves, norm_all), (hidden0, hidden1),
-                             grads, down_lanes)
-    ready = grad_w_down
+    ready = norm_all
     for index in range(chunks[1][1]):
         grad_gu = gate_up_grads(
             plan, chunks[1], after(halves, ready), turned,

time: 455 us -> 507 us (1.11)
  waiting for transfers between devices: 126 us -> 166 us
  Pallas kernels: 247 us -> 259 us
    ppermute x8, waiting for transfers between devices: 12.8 us -> 38.2 us  [ring_step(): found[-k] = lax.ppermute(after(found[1 - k], *ready), 'row', ahead)]
    ppermute x6, waiting for transfers between devices: 53.1 us -> 66.6 us  [from_chips(): lax.ppermute(value, 'col', [(i, (i + CORES * k) % n_col) for i in range(n...]
    pallas_call x22, Pallas kernels: 247 us -> 259 us  [call(): pl.pallas_call(body, grid_spec=pltpu.PrefetchScalarGridSpec(num_scalar_pr...]
    ppermute x6, waiting for transfers between devices: 11.3 us -> 0.02 us  [ring_step(): found[k] = lax.ppermute(after(found[k - 1], *ready), 'row', behind)]
    ppermute x10 -> x9, waiting for transfers between devices: 16.3 us -> 23.5 us  [to_partner(): return lax.ppermute(value, 'col', swap)]
    ppermute x8, waiting for transfers between devices: 29.9 us -> 35 us  [scatter(): back = lax.ppermute(back, 'row', behind)]
    unnamed x66 -> x60, local copies, waits for them, and re-layouts: 10.7 us -> 9.42 us
  transfers between devices with their start and end apart: 47 -> 46, of which waited for: 24 -> 24; matrix products, arithmetic and copies ran while one was open for 5% -> 4% of each run, Pallas kernels for 43% -> 33%
where the time goes in v3:
time: 507 us; the launch traced here: 504 us
  Pallas kernels  259 us (51%)
  waiting for transfers between devices  166 us (33%)
  starting transfers between devices  44.5 us (9%)
  local copies, waits for them, and re-layouts  17 us (3%)
  other arithmetic  15.8 us (3%)
    pallas_call x22, Pallas kernels, call(): pl.pallas_call(body, grid_spec=pltpu.PrefetchScalarGridSpec(num_scalar_pr...  259 us
    ppermute x6, waiting for transfers between devices, from_chips(): lax.ppermute(value, 'col', [(i, (i + CORES * k) % n_col) for i in range(n...  66.6 us
    ppermute x8, waiting for transfers between devices, ring_step(): found[-k] = lax.ppermute(after(found[1 - k], *ready), 'row', ahead)  38.2 us
    ppermute x8, waiting for transfers between devices, scatter(): back = lax.ppermute(back, 'row', behind)  35 us
    ppermute x9, waiting for transfers between devices, to_partner(): return lax.ppermute(value, 'col', swap)  23.5 us
    ppermute x8, starting transfers between devices, ring_step(): found[-k] = lax.ppermute(after(found[1 - k], *ready), 'row', ahead)  13.2 us
  transfers between devices with their start and end apart: 46, of which 24 were waited for; matrix products, arithmetic and copies ran while one was open for 4% of the time, Pallas kernels for 33%

profile of v3, /device:TPU:0, one launch (start us, length us, event | category | flops | bytes accessed | tf_op | source)
XLA Modules:
  0.0 503.8 jit_solution(17058802584140118513)
XLA Ops:
  1.7 3.1 collective-permute-start
  8.2 5.7 %collective-permute-done.refs_1_ = bf16[96,2048]{1,0:T(8,128)(2,1)S(1)} collective-permute-done((bf16[96,2048]{1,0:T(8,128)(2,1)S(1)}, bf16[96,2048]{1,0:T(8,128)(2,1)S(1)}, u32[]{:S(2)}, u32[]{:S(2)}) %collective-permute-start) | collective-permute-done | bytes 393248 | tf_op jit(solution)/shard_map/ppermute | solution.py:470
  18.1 15.9 %shard_map.136 = (bf16[2048,2048]{1,0:T(8,128)(2,1)}, bf16[1536,2048]{1,0:T(8,128)(2,1)}) custom-call(s32[2]{0:T(128)} %pad_add_fusion._.half_ref, bf16[3584,2048]{1,0:T(8,128)(2,1)} %w_ref.1, f32[56,2048]{1,0:T(8,128)} %reshape.30.k_ref.refs_10_), custom_call_target="tpu_custom_call" | custom-call | bytes 29360128 | tf_op jit(solution)/shard_map/pallas_call | solution.py:53
  34.0 1.8 collective-permute-start.4
  36.1 7.7 %collective-permute-done.4.refs_5_ = bf16[96,2048]{1,0:T(8,128)(2,1)S(1)} collective-permute-done((bf16[96,2048]{1,0:T(8,128)(2,1)S(1)}, bf16[96,2048]{1,0:T(8,128)(2,1)S(1)}, u32[]{:S(2)}, u32[]{:S(2)}) %collective-permute-start.4) | collective-permute-done | bytes 393248 | tf_op jit(solution)/shard_map/ppermute | solution.py:470
  45.9 6.7 %collective-permute-done.6.refs_7_ = bf16[96,2048]{1,0:T(8,128)(2,1)S(1)} collective-permute-done((bf16[96,2048]{1,0:T(8,128)(2,1)S(1)}, bf16[96,2048]{1,0:T(8,128)(2,1)S(1)}, u32[]{:S(2)}, u32[]{:S(2)}) %collective-permute-start.6) | collective-permute-done | bytes 393248 | tf_op jit(solution)/shard_map/ppermute | solution.py:470
  53.4 13.4 %shard_map.137 = (bf16[768,2048]{1,0:T(8,128)(2,1)}, bf16[2048,2048]{1,0:T(8,128)(2,1)}, f32[768,1]{1,0:T(8,128)}) custom-call(s32[2]{0:T(128)} %pad_add_fusion._.half_ref, bf16[96,2048]{1,0:T(8,128)(2,1)} %copy-done.1, bf16[96,2048]{1,0:T(8,128)(2,1)} %copy-done.4, bf16[96,2048]{1,0:T(8,128)(2,1)} %copy-done.5, bf16[96,2048]{1,0:T(8,128)(2,1)} %copy-done.6, ...), custom_call_target="tpu_custom_call" | custom-call | flops 6442450944 | bytes 26214400 | tf_op jit(solution)/shard_map/pallas_call | solution.py:53
  66.8 5.9 %collective-permute-done.9.refs_12_ = bf16[768,2048]{1,0:T(8,128)(2,1)S(1)} collective-permute-done((bf16[768,2048]{1,0:T(8,128)(2,1)}, bf16[768,2048]{1,0:T(8,128)(2,1)S(1)}, u32[]{:S(2)}, u32[]{:S(2)}) %collective-permute-start.9) | collective-permute-done | bytes 3145760 | tf_op jit(solution)/shard_map/ppermute | solution.py:443
  74.3 13.3 %shard_map.138 = (bf16[768,2048]{1,0:T(8,128)(2,1)}, bf16[2048,2048]{1,0:T(8,128)(2,1)}) custom-call(s32[2]{0:T(128)} %pad_add_fusion._.half_ref, bf16[96,2048]{1,0:T(8,128)(2,1)} %copy-done.1, bf16[96,2048]{1,0:T(8,128)(2,1)} %copy-done.4, bf16[96,2048]{1,0:T(8,128)(2,1)} %copy-done.5, bf16[96,2048]{1,0:T(8,128)(2,1)} %copy-done.6, ...), custom_call_target="tpu_custom_call" | custom-call | flops 6442450944 | bytes 26214400 | tf_op jit(solution)/shard_map/pallas_call | solution.py:53
  87.6 10.8 %shard_map.139 = (bf16[768,1536]{1,0:T(8,128)(2,1)}, bf16[2048,1536]{1,0:T(8,128)(2,1)}) custom-call(s32[2]{0:T(128)} %pad_add_fusion._.half_ref, bf16[96,2048]{1,0:T(8,128)(2,1)} %copy-done.1, bf16[96,2048]{1,0:T(8,128)(2,1)} %copy-done.4, bf16[96,2048]{1,0:T(8,128)(2,1)} %copy-done.5, bf16[96,2048]{1,0:T(8,128)(2,1)} %copy-done.6, ...), custom_call_target="tpu_custom_call" | custom-call | flops 4831838208 | bytes 20447232 | tf_op jit(solution)/shard_map/pallas_call | solution.py:53
  100.7 9.4 %collective-permute-done.7.refs_1_ = bf16[96,2048]{1,0:T(8,128)(2,1)S(1)} collective-permute-done((bf16[96,2048]{1,0:T(8,128)(2,1)S(1)}, bf16[96,2048]{1,0:T(8,128)(2,1)S(1)}, u32[]{:S(2)}, u32[]{:S(2)}) %collective-permute-start.7) | collective-permute-done | bytes 393248 | tf_op jit(solution)/shard_map/ppermute | solution.py:470
  112.1 8.7 %collective-permute-done.10.refs_3_ = bf16[96,2048]{1,0:T(8,128)(2,1)} collective-permute-done((bf16[96,2048]{1,0:T(8,128)(2,1)S(1)}, bf16[96,2048]{1,0:T(8,128)(2,1)}, u32[]{:S(2)}, u32[]{:S(2)}) %collective-permute-start.10) | collective-permute-done | bytes 393248 | tf_op jit(solution)/shard_map/ppermute | solution.py:470
  125.9 2.1 collective-permute-done.15
  129.0 7.9 %shard_map.140.x_ref = bf16[2048,768]{1,0:T(8,128)(2,1)} custom-call(s32[2]{0:T(128)} %pad_add_fusion._.half_ref, f32[768,1]{1,0:T(8,128)} %broadcast_in_dim.15.s_ref, bf16[96,2048]{1,0:T(8,128)(2,1)} %copy-done.1, bf16[96,2048]{1,0:T(8,128)(2,1)} %copy-done.4, bf16[96,2048]{1,0:T(8,128)(2,1)} %copy-done.5, bf16[96,2048]{1,0:T(8,128)(2,1)} %copy-done.6, ...), custom_call_target="tpu_custom_call" | custom-call | bytes 6291456 | tf_op jit(solution)/shard_map/pallas_call | solution.py:53
  140.4 11.3 %shard_map.141 = (bf16[768,1536]{1,0:T(8,128)(2,1)}, bf16[2048,1536]{1,0:T(8,128)(2,1)}) custom-call(s32[2]{0:T(128)} %pad_add_fusion._.half_ref, bf16[96,2048]{1,0:T(8,128)(2,1)} %copy-done.1, bf16[96,2048]{1,0:T(8,128)(2,1)} %copy-done.4, bf16[96,2048]{1,0:T(8,128)(2,1)} %copy-done.5, bf16[96,2048]{1,0:T(8,128)(2,1)} %copy-done.6, ...), custom_call_target="tpu_custom_call" | custom-call | flops 4831838208 | bytes 20447232 | tf_op jit(solution)/shard_map/pallas_call | solution.py:53
  152.6 12.5 %shard_map.142 = bf16[768,1792]{1,0:T(8,128)(2,1)} custom-call(s32[2]{0:T(128)} %pad_add_fusion._.half_ref, bf16[96,2048]{1,0:T(8,128)(2,1)} %refs_0_.3, bf16[96,2048]{1,0:T(8,128)(2,1)} %copy-done.23, bf16[96,2048]{1,0:T(8,128)(2,1)} %collective-permute-done.8.refs_2_, bf16[96,2048]{1,0:T(8,128)(2,1)} %collective-permute-done.10.refs_3_, ...), custom_call_target="tpu_custom_call" | custom-call | flops 5637144576 | bytes 13238272 | tf_op jit(solution)/shard_map/pallas_call | solution.py:53
  166.7 3.9 collective-permute-done.18.refs_10_
  170.6 12.8 %shard_map.143 = (bf16[768,1024]{1,0:T(8,128)(2,1)}, bf16[768,768]{1,0:T(8,128)(2,1)}) custom-call(s32[2]{0:T(128)} %pad_add_fusion._.half_ref, bf16[96,2048]{1,0:T(8,128)(2,1)} %refs_0_.3, bf16[96,2048]{1,0:T(8,128)(2,1)} %copy-done.23, bf16[96,2048]{1,0:T(8,128)(2,1)} %collective-permute-done.8.refs_2_, bf16[96,2048]{1,0:T(8,128)(2,1)} %collective-permute-done.10.refs_3_, ...), custom_call_target="tpu_custom_call" | custom-call | flops 5637144576 | bytes 13238272 | tf_op jit(solution)/shard_map/pallas_call | solution.py:53
  183.4 52.4 %collective-permute-done.19.refs_1_ = bf16[768,2048]{1,0:T(8,128)(2,1)} collective-permute-done((bf16[768,2048]{1,0:T(8,128)(2,1)S(1)}, bf16[768,2048]{1,0:T(8,128)(2,1)}, u32[]{:S(2)}, u32[]{:S(2)}) %collective-permute-start.19) | collective-permute-done | bytes 3145760 | tf_op jit(solution)/shard_map/ppermute | solution.py:447
  235.8 6.0 %shard_map.144.m_ref.refs_8_ = bf16[768,1024]{1,0:T(8,128)(2,1)} custom-call(s32[2]{0:T(128)} %pad_add_fusion._.half_ref, f32[768,1]{1,0:T(8,128)} %broadcast_in_dim.15.s_ref, bf16[768,2048]{1,0:T(8,128)(2,1)} %get-tuple-element.82.refs_0_, bf16[768,2048]{1,0:T(8,128)(2,1)} %collective-permute-done.19.refs_1_), custom_call_target="tpu_custom_call" | custom-call | bytes 11011584 | tf_op jit(solution)/shard_map/pallas_call | solution.py:53
  243.4 2.1 collective-permute-done.20.o_ref.refs_9_
  246.6 13.6 %shard_map.145.rest_0_ = f32[768,2048]{1,0:T(8,128)} custom-call(s32[2]{0:T(128)} %pad_add_fusion._.half_ref, bf16[768,1024]{1,0:T(8,128)(2,1)} %shard_map.144.m_ref.refs_8_, bf16[768,1024]{1,0:T(8,128)(2,1)} %copy-done.19, bf16[2048,2048]{1,0:T(8,128)(2,1)} %get-tuple-element.60.refs_8_.wm_ref.wo_ref, bf16[2048,2048]{1,0:T(8,128)(2,1)} %get-tuple-element.60.refs_8_.wm_ref.wo_ref), custom_call_target="tpu_custom_call" | custom-call | flops 6442450944 | bytes 17825792 | tf_op jit(solution)/shard_map/pallas_call | solution.py:53
  260.2 14.3 %shard_map.146.refs_11_ = bf16[3584,2048]{1,0:T(8,128)(2,1)} custom-call(s32[2]{0:T(128)} %pad_add_fusion._.half_ref, bf16[96,2048]{1,0:T(8,128)(2,1)} %refs_0_.3, bf16[96,2048]{1,0:T(8,128)(2,1)} %copy-done.23, bf16[96,2048]{1,0:T(8,128)(2,1)} %collective-permute-done.8.refs_2_, bf16[96,2048]{1,0:T(8,128)(2,1)} %collective-permute-done.10.refs_3_, ...), custom_call_target="tpu_custom_call" | custom-call | flops 6442450944 | bytes 14680064 | tf_op jit(solution)/shard_map/pallas_call | solution.py:53
  274.5 4.2 collective-permute-done.21.refs_3_
  278.7 8.0 %shard_map.147.m_ref.refs_0_ = bf16[768,2048]{1,0:T(8,128)(2,1)} custom-call(s32[2]{0:T(128)} %pad_add_fusion._.half_ref, f32[768,1]{1,0:T(8,128)} %broadcast_in_dim.15.s_ref, bf16[768,2048]{1,0:T(8,128)(2,1)} %get-tuple-element.82.refs_0_, bf16[768,2048]{1,0:T(8,128)(2,1)} %collective-permute-done.19.refs_1_, bf16[768,1024]{1,0:T(8,128)(2,1)} %get-tuple-element.86.refs_2_, ...), custom_call_target="tpu_custom_call" | custom-call | bytes 14157312 | tf_op jit(solution)/shard_map/pallas_call | solution.py:53
  288.3 4.4 collective-permute-done.22.o_ref.refs_1_
  292.7 19.8 %shard_map.148.rest_0_ = f32[768,2048]{1,0:T(8,128)} custom-call(s32[2]{0:T(128)} %pad_add_fusion._.half_ref, bf16[768,2048]{1,0:T(8,128)(2,1)} %shard_map.147.m_ref.refs_0_, bf16[768,2048]{1,0:T(8,128)(2,1)} %collective-permute-done.22.o_ref.refs_1_, bf16[2048,2048]{1,0:T(8,128)(2,1)} %get-tuple-element.87.wm_ref, bf16[2048,2048]{1,0:T(8,128)(2,1)} %get-tuple-element.88.wo_ref), custom_call_target="tpu_custom_call" | custom-call | flops 12884901888 | bytes 29360128 | tf_op jit(solution)/shard_map/pallas_call | solution.py:53
  312.5 20.1 %shard_map.149 = (bf16[2048,3584]{1,0:T(8,128)(2,1)}, bf16[2048,3584]{1,0:T(8,128)(2,1)}) custom-call(s32[2]{0:T(128)} %pad_add_fusion._.half_ref, bf16[2048,768]{1,0:T(8,128)(2,1)} %shard_map.140.x_ref, bf16[768,2048]{1,0:T(8,128)(2,1)} %shard_map.147.m_ref.refs_0_, bf16[768,2048]{1,0:T(8,128)(2,1)} %collective-permute-done.22.o_ref.refs_1_, ...), custom_call_target="tpu_custom_call" | custom-call | flops 12884901888 | bytes 26214400 | tf_op jit(solution)/shard_map/pallas_call | solution.py:53
  332.6 7.8 %collective-permute-done.23.refs_1_ = bf16[768,1536]{1,0:T(8,128)(2,1)} collective-permute-done((bf16[768,1536]{1,0:T(8,128)(2,1)S(1)}, bf16[768,1536]{1,0:T(8,128)(2,1)}, u32[]{:S(2)}, u32[]{:S(2)}) %collective-permute-start.23) | collective-permute-done | bytes 2359328 | tf_op jit(solution)/shard_map/ppermute | solution.py:447
  340.5 5.5 %shard_map.150.m_ref.refs_8_ = bf16[768,768]{1,0:T(8,128)(2,1)} custom-call(s32[2]{0:T(128)} %pad_add_fusion._.half_ref, f32[768,1]{1,0:T(8,128)} %broadcast_in_dim.15.s_ref, bf16[768,1536]{1,0:T(8,128)(2,1)} %get-tuple-element.92.refs_0_, bf16[768,1536]{1,0:T(8,128)(2,1)} %collective-permute-done.23.refs_1_), custom_call_target="tpu_custom_call" | custom-call | bytes 8259072 | tf_op jit(solution)/shard_map/pallas_call | solution.py:53
  350.1 12.6 %shard_map.151 = bf16[768,2048]{1,0:T(8,128)(2,1)} custom-call(s32[2]{0:T(128)} %pad_add_fusion._.half_ref, bf16[768,768]{1,0:T(8,128)(2,1)} %shard_map.150.m_ref.refs_8_, bf16[768,768]{1,0:T(8,128)(2,1)} %copy-done.12, bf16[1536,2048]{1,0:T(8,128)(2,1)} %get-tuple-element.76.refs_9_.wm_ref.wo_ref, ...), custom_call_target="tpu_custom_call" | custom-call | flops 4831838208 | bytes 14942208 | tf_op jit(solution)/shard_map/pallas_call | solution.py:53
  362.7 11.7 %shard_map.152 = bf16[3584,2048]{1,0:T(8,128)(2,1)} custom-call(s32[2]{0:T(128)} %pad_add_fusion._.half_ref, bf16[96,2048]{1,0:T(8,128)(2,1)} %refs_0_.3, bf16[96,2048]{1,0:T(8,128)(2,1)} %copy-done.23, bf16[96,2048]{1,0:T(8,128)(2,1)} %collective-permute-done.8.refs_2_, ...), custom_call_target="tpu_custom_call", output_to_operand_aliasing={{}: (12, {})} | custom-call | flops 4831838208 | bytes 11796480 | tf_op jit(solution)/shard_map/pallas_call | solution.py:53
  375.5 7.2 %shard_map.153.m_ref.refs_0_ = bf16[768,1536]{1,0:T(8,128)(2,1)} custom-call(s32[2]{0:T(128)} %pad_add_fusion._.half_ref, f32[768,1]{1,0:T(8,128)} %broadcast_in_dim.15.s_ref, bf16[768,1536]{1,0:T(8,128)(2,1)} %get-tuple-element.92.refs_0_, bf16[768,1536]{1,0:T(8,128)(2,1)} %collective-permute-done.23.refs_1_, bf16[768,768]{1,0:T(8,128)(2,1)} %get-tuple-element.95.refs_2_, ...), custom_call_target="tpu_custom_call" | custom-call | bytes 10618368 | tf_op jit(solution)/shard_map/pallas_call | solution.py:53
  382.8 4.6 collective-permute-done.33.o_ref.refs_1_
  388.8 17.4 %shard_map.154 = bf16[768,2048]{1,0:T(8,128)(2,1)} custom-call(s32[2]{0:T(128)} %pad_add_fusion._.half_ref, bf16[768,1536]{1,0:T(8,128)(2,1)} %shard_map.153.m_ref.refs_0_, bf16[768,1536]{1,0:T(8,128)(2,1)} %copy-done, bf16[2048,1536]{1,0:T(8,128)(2,1)} %get-tuple-element.96.wm_ref, bf16[2048,1536]{1,0:T(8,128)(2,1)} %get-tuple-element.97.wo_ref, ...), custom_call_target="tpu_custom_call" | custom-call | flops 9663676416 | bytes 23592960 | tf_op jit(solution)/shard_map/pallas_call | solution.py:53
  412.8 6.7 %collective-permute-done.34 = bf16[96,2048]{1,0:T(8,128)(2,1)S(1)} collective-permute-done((bf16[96,2048]{1,0:T(8,128)(2,1)S(1)}, bf16[96,2048]{1,0:T(8,128)(2,1)S(1)}, u32[]{:S(2)}, u32[]{:S(2)}) %collective-permute-start.34) | collective-permute-done | bytes 393248 | tf_op jit(solution)/shard_map/ppermute | solution.py:541
  421.5 6.5 %collective-permute-done.25 = bf16[96,2048]{1,0:T(8,128)(2,1)S(1)} collective-permute-done((bf16[96,2048]{1,0:T(8,128)(2,1)S(1)}, bf16[96,2048]{1,0:T(8,128)(2,1)S(1)}, u32[]{:S(2)}, u32[]{:S(2)}) %collective-permute-start.25) | collective-permute-done | bytes 393248 | tf_op jit(solution)/shard_map/ppermute | solution.py:541
  429.8 6.6 %collective-permute-done.35 = bf16[96,2048]{1,0:T(8,128)(2,1)S(1)} collective-permute-done((bf16[96,2048]{1,0:T(8,128)(2,1)S(1)}, bf16[96,2048]{1,0:T(8,128)(2,1)S(1)}, u32[]{:S(2)}, u32[]{:S(2)}) %collective-permute-start.35) | collective-permute-done | bytes 393248 | tf_op jit(solution)/shard_map/ppermute | solution.py:541
  439.9 5.0 collective-permute-done.26
  447.2 6.1 %collective-permute-done.36 = bf16[96,2048]{1,0:T(8,128)(2,1)S(1)} collective-permute-done((bf16[96,2048]{1,0:T(8,128)(2,1)S(1)}, bf16[96,2048]{1,0:T(8,128)(2,1)S(1)}, u32[]{:S(2)}, u32[]{:S(2)}) %collective-permute-start.36) | collective-permute-done | bytes 393248 | tf_op jit(solution)/shard_map/ppermute | solution.py:541
  453.3 2.3 add_convert_fusion.2
  457.6 4.1 collective-permute-done.27
  464.9 8.6 %shard_map.155 = (bf16[2048,3584]{1,0:T(8,128)(2,1)}, bf16[2048,3584]{1,0:T(8,128)(2,1)}) custom-call(s32[2]{0:T(128)} %pad_add_fusion._.half_ref, bf16[2048,768]{1,0:T(8,128)(2,1)} %shard_map.140.x_ref, bf16[768,1536]{1,0:T(8,128)(2,1)} %shard_map.153.m_ref.refs_0_, bf16[768,1536]{1,0:T(8,128)(2,1)} %copy-done, ...), custom_call_target="tpu_custom_call", output_to_operand_aliasing={{0}: (6, {}), {1}: (7, {})} | custom-call | flops 3221225472 | bytes 8912896 | tf_op jit(solution)/shard_map/pallas_call | solution.py:53
  475.3 8.2 %shard_map.156 = (bf16[2048,3584]{1,0:T(8,128)(2,1)}, bf16[2048,3584]{1,0:T(8,128)(2,1)}) custom-call(s32[2]{0:T(128)} %pad_add_fusion._.half_ref, bf16[2048,768]{1,0:T(8,128)(2,1)} %shard_map.140.x_ref, bf16[768,1536]{1,0:T(8,128)(2,1)} %shard_map.153.m_ref.refs_0_, bf16[768,1536]{1,0:T(8,128)(2,1)} %copy-done, ...), custom_call_target="tpu_custom_call", output_to_operand_aliasing={{0}: (6, {}), {1}: (7, {})} | custom-call | flops 3221225472 | bytes 8912896 | tf_op jit(solution)/shard_map/pallas_call | solution.py:53
  485.6 8.4 %shard_map.157 = (bf16[2048,3584]{1,0:T(8,128)(2,1)}, bf16[2048,3584]{1,0:T(8,128)(2,1)}) custom-call(s32[2]{0:T(128)} %pad_add_fusion._.half_ref, bf16[2048,768]{1,0:T(8,128)(2,1)} %shard_map.140.x_ref, bf16[768,1536]{1,0:T(8,128)(2,1)} %shard_map.153.m_ref.refs_0_, bf16[768,1536]{1,0:T(8,128)(2,1)} %copy-done, ...), custom_call_target="tpu_custom_call", output_to_operand_aliasing={{0}: (6, {}), {1}: (7, {})} | custom-call | flops 3221225472 | bytes 8912896 | tf_op jit(solution)/shard_map/pallas_call | solution.py:53
  495.5 2.1 collective-permute-done.44
  497.7 2.5 collective-permute-start.45
  500.2 3.0 fusion.7
  (159 shorter events, 68.1 us)
Async XLA Ops:
  1.7 12.2 %collective-permute-start = (bf16[96,2048]{1,0:T(8,128)(2,1)S(1)}, bf16[96,2048]{1,0:T(8,128)(2,1)S(1)}, u32[]{:S(2)}, u32[]{:S(2)}) collective-permute-start(bf16[96,2048]{1,0:T(8,128)(2,1)S(1)} %fusion.9.refs_0_), channel_id=1, source_target_pairs={{0,8},{8,16},{16,24},{24,28},{28,20},{20,12},{12,4},{4,0},{1,9},{9... | collective-permute-start | bytes 1179656 | tf_op jit(solution)/shard_map/ppermute | solution.py:470
  4.9 13.0 %collective-permute-start.1 = (bf16[96,2048]{1,0:T(8,128)(2,1)S(1)}, bf16[96,2048]{1,0:T(8,128)(2,1)S(1)}, u32[]{:S(2)}, u32[]{:S(2)}) collective-permute-start(bf16[96,2048]{1,0:T(8,128)(2,1)S(1)} %fusion.9.refs_0_), channel_id=1, source_target_pairs={{8,0},{16,8},{24,16},{28,24},{20,28},{12,20},{4,12},{0,4},{9,1},{1... | collective-permute-start | bytes 1179656 | tf_op jit(solution)/shard_map/ppermute | solution.py:472
  13.9 20.1 %collective-permute-start.2 = (bf16[96,2048]{1,0:T(8,128)(2,1)S(1)}, bf16[96,2048]{1,0:T(8,128)(2,1)S(1)}, u32[]{:S(2)}, u32[]{:S(2)}) collective-permute-start(bf16[96,2048]{1,0:T(8,128)(2,1)S(1)} %collective-permute-done.refs_1_), channel_id=1, source_target_pairs={{0,8},{8,16},{16,24},{24,28},{28,20},{20,12},{12,4},{4,0},{1,9},{9... | collective-permute-start | bytes 1179656 | tf_op jit(solution)/shard_map/ppermute | solution.py:470
  17.9 27.5 %copy-start.27 = (f32[2048]{0:T(1024)S(1)}, f32[2048]{0:T(1024)}, u32[]{:S(2)}) copy-start(f32[2048]{0:T(1024)} %param.10) | copy-start | bytes 24580
  17.9 18.0 %collective-permute-start.3 = (bf16[96,2048]{1,0:T(8,128)(2,1)S(1)}, bf16[96,2048]{1,0:T(8,128)(2,1)S(1)}, u32[]{:S(2)}, u32[]{:S(2)}) collective-permute-start(bf16[96,2048]{1,0:T(8,128)(2,1)S(1)} %collective-permute-done.1.refs_2_), channel_id=1, source_target_pairs={{8,0},{16,8},{24,16},{28,24},{20,28},{12,20},{4,12},{0,4},{9,1},{1... | collective-permute-start | bytes 1179656 | tf_op jit(solution)/shard_map/ppermute | solution.py:472
  34.0 9.8 %collective-permute-start.4 = (bf16[96,2048]{1,0:T(8,128)(2,1)S(1)}, bf16[96,2048]{1,0:T(8,128)(2,1)S(1)}, u32[]{:S(2)}, u32[]{:S(2)}) collective-permute-start(bf16[96,2048]{1,0:T(8,128)(2,1)S(1)} %collective-permute-done.2.refs_3_), channel_id=1, source_target_pairs={{0,8},{8,16},{16,24},{24,28},{28,20},{20,12},{12,4},{4,0},{1,9},{9... | collective-permute-start | bytes 1179656 | tf_op jit(solution)/shard_map/ppermute | solution.py:470
  35.9 10.0 %collective-permute-start.5 = (bf16[96,2048]{1,0:T(8,128)(2,1)S(1)}, bf16[96,2048]{1,0:T(8,128)(2,1)S(1)}, u32[]{:S(2)}, u32[]{:S(2)}) collective-permute-start(bf16[96,2048]{1,0:T(8,128)(2,1)S(1)} %collective-permute-done.3.refs_4_), channel_id=1, source_target_pairs={{8,0},{16,8},{24,16},{28,24},{20,28},{12,20},{4,12},{0,4},{9,1},{1... | collective-permute-start | bytes 1179656 | tf_op jit(solution)/shard_map/ppermute | solution.py:472
  43.8 8.9 %collective-permute-start.6 = (bf16[96,2048]{1,0:T(8,128)(2,1)S(1)}, bf16[96,2048]{1,0:T(8,128)(2,1)S(1)}, u32[]{:S(2)}, u32[]{:S(2)}) collective-permute-start(bf16[96,2048]{1,0:T(8,128)(2,1)S(1)} %collective-permute-done.4.refs_5_), channel_id=1, source_target_pairs={{0,8},{8,16},{16,24},{24,28},{28,20},{20,12},{12,4},{4,0},{1,9},{9... | collective-permute-start | bytes 1179656 | tf_op jit(solution)/shard_map/ppermute | solution.py:470
  66.8 5.9 %collective-permute-start.9 = (bf16[768,2048]{1,0:T(8,128)(2,1)}, bf16[768,2048]{1,0:T(8,128)(2,1)S(1)}, u32[]{:S(2)}, u32[]{:S(2)}) collective-permute-start(bf16[768,2048]{1,0:T(8,128)(2,1)} %get-tuple-element.64), channel_id=1, source_target_pairs={{0,1},{1,0},{2,3},{3,2},{4,5},{5,4},{6,7},{7,6},{8,9},{9,8},{10,11... | collective-permute-start | bytes 9437192 | tf_op jit(solution)/shard_map/ppermute | solution.py:443
  98.4 40.6 %collective-permute-start.17 = (bf16[768,1536]{1,0:T(8,128)(2,1)}, bf16[768,1536]{1,0:T(8,128)(2,1)S(1)}, u32[]{:S(2)}, u32[]{:S(2)}) collective-permute-start(bf16[768,1536]{1,0:T(8,128)(2,1)} %get-tuple-element.70), channel_id=1, source_target_pairs={{0,1},{1,0},{2,3},{3,2},{4,5},{5,4},{6,7},{7,6},{8,9},{9,8},{10,11... | collective-permute-start | bytes 7077896 | tf_op jit(solution)/shard_map/ppermute | solution.py:443
  98.6 11.4 %collective-permute-start.7 = (bf16[96,2048]{1,0:T(8,128)(2,1)S(1)}, bf16[96,2048]{1,0:T(8,128)(2,1)S(1)}, u32[]{:S(2)}, u32[]{:S(2)}) collective-permute-start(bf16[96,2048]{1,0:T(8,128)(2,1)S(1)} %copy-done.16), channel_id=1, source_target_pairs={{0,8},{8,16},{16,24},{24,28},{28,20},{20,12},{12,4},{4,0},{1,9},{9... | collective-permute-start | bytes 1179656 | tf_op jit(solution)/shard_map/ppermute | solution.py:470
  99.9 11.4 %collective-permute-start.8 = (bf16[96,2048]{1,0:T(8,128)(2,1)S(1)}, bf16[96,2048]{1,0:T(8,128)(2,1)}, u32[]{:S(2)}, u32[]{:S(2)}) collective-permute-start(bf16[96,2048]{1,0:T(8,128)(2,1)S(1)} %copy-done.16), channel_id=1, source_target_pairs={{8,0},{16,8},{24,16},{28,24},{20,28},{12,20},{4,12},{0,4},{9,1},{1... | collective-permute-start | bytes 1179656 | tf_op jit(solution)/shard_map/ppermute | solution.py:472
  110.0 26.8 %copy-start.23 = (bf16[96,2048]{1,0:T(8,128)(2,1)}, bf16[96,2048]{1,0:T(8,128)(2,1)S(1)}, u32[]{:S(2)}) copy-start(bf16[96,2048]{1,0:T(8,128)(2,1)S(1)} %collective-permute-done.7.refs_1_) | copy-start | bytes 1179652
  110.0 10.7 %collective-permute-start.10 = (bf16[96,2048]{1,0:T(8,128)(2,1)S(1)}, bf16[96,2048]{1,0:T(8,128)(2,1)}, u32[]{:S(2)}, u32[]{:S(2)}) collective-permute-start(bf16[96,2048]{1,0:T(8,128)(2,1)S(1)} %collective-permute-done.7.refs_1_), channel_id=1, source_target_pairs={{0,8},{8,16},{16,24},{24,28},{28,20},{20,12},{12,4},{4,0},{1,9},{9... | collective-permute-start | bytes 1179656 | tf_op jit(solution)/shard_map/ppermute | solution.py:470
  111.3 25.6 %collective-permute-start.11 = (bf16[96,2048]{1,0:T(8,128)(2,1)}, bf16[96,2048]{1,0:T(8,128)(2,1)S(1)}, u32[]{:S(2)}, u32[]{:S(2)}) collective-permute-start(bf16[96,2048]{1,0:T(8,128)(2,1)} %collective-permute-done.8.refs_2_), channel_id=1, source_target_pairs={{8,0},{16,8},{24,16},{28,24},{20,28},{12,20},{4,12},{0,4},{9,1},{1... | collective-permute-start | bytes 1179656 | tf_op jit(solution)/shard_map/ppermute | solution.py:472
  120.8 17.0 %collective-permute-start.12 = (bf16[96,2048]{1,0:T(8,128)(2,1)}, bf16[96,2048]{1,0:T(8,128)(2,1)}, u32[]{:S(2)}, u32[]{:S(2)}) collective-permute-start(bf16[96,2048]{1,0:T(8,128)(2,1)} %collective-permute-done.10.refs_3_), channel_id=1, source_target_pairs={{0,8},{8,16},{16,24},{24,28},{28,20},{20,12},{12,4},{4,0},{1,9},{9... | collective-permute-start | bytes 1179656 | tf_op jit(solution)/shard_map/ppermute | solution.py:470
  123.2 1.2 collective-permute-start.14
  124.4 3.6 collective-permute-start.15
  136.9 14.8 %collective-permute-start.13 = (bf16[96,2048]{1,0:T(8,128)(2,1)S(1)}, bf16[96,2048]{1,0:T(8,128)(2,1)S(1)}, u32[]{:S(2)}, u32[]{:S(2)}) collective-permute-start(bf16[96,2048]{1,0:T(8,128)(2,1)S(1)} %collective-permute-done.11.refs_4_), channel_id=1, source_target_pairs={{8,0},{16,8},{24,16},{28,24},{20,28},{12,20},{4,12},{0,4},{9,1},{1... | collective-permute-start | bytes 1179656 | tf_op jit(solution)/shard_map/ppermute | solution.py:472
  137.7 14.0 %collective-permute-start.16 = (bf16[96,2048]{1,0:T(8,128)(2,1)}, bf16[96,2048]{1,0:T(8,128)(2,1)S(1)}, u32[]{:S(2)}, u32[]{:S(2)}) collective-permute-start(bf16[96,2048]{1,0:T(8,128)(2,1)} %collective-permute-done.12.refs_5_), channel_id=1, source_target_pairs={{0,8},{8,16},{16,24},{24,28},{28,20},{20,12},{12,4},{4,0},{1,9},{9... | collective-permute-start | bytes 1179656 | tf_op jit(solution)/shard_map/ppermute | solution.py:470
  165.2 5.4 %collective-permute-start.18 = (bf16[768,1792]{1,0:T(8,128)(2,1)}, bf16[768,1792]{1,0:T(8,128)(2,1)}, u32[]{:S(2)}, u32[]{:S(2)}) collective-permute-start(bf16[768,1792]{1,0:T(8,128)(2,1)} %shard_map.142), channel_id=1, source_target_pairs={{0,1},{1,0},{2,3},{3,2},{4,5},{5,4},{6,7},{7,6},{8,9},{9,8},{10,11... | collective-permute-start | bytes 8257544 | tf_op jit(solution)/shard_map/ppermute | solution.py:443
  165.2 70.6 %collective-permute-start.19 = (bf16[768,2048]{1,0:T(8,128)(2,1)S(1)}, bf16[768,2048]{1,0:T(8,128)(2,1)}, u32[]{:S(2)}, u32[]{:S(2)}) collective-permute-start(bf16[768,2048]{1,0:T(8,128)(2,1)S(1)} %copy-done.2), channel_id=1, source_target_pairs={{0,2},{1,3},{2,0},{3,1},{4,6},{5,7},{6,4},{7,5},{8,10},{9,11},{10,... | collective-permute-start | bytes 9437192 | tf_op jit(solution)/shard_map/ppermute | solution.py:447
  241.8 3.6 collective-permute-start.20
  241.8 36.9 %collective-permute-start.21 = (bf16[768,1024]{1,0:T(8,128)(2,1)S(1)}, bf16[768,1024]{1,0:T(8,128)(2,1)}, u32[]{:S(2)}, u32[]{:S(2)}) collective-permute-start(bf16[768,1024]{1,0:T(8,128)(2,1)S(1)} %copy-done.18), channel_id=1, source_target_pairs={{0,2},{1,3},{2,0},{3,1},{4,6},{5,7},{6,4},{7,5},{8,10},{9,11},{10,... | collective-permute-start | bytes 4718600 | tf_op jit(solution)/shard_map/ppermute | solution.py:447
  286.7 6.0 %collective-permute-start.22 = (bf16[768,2048]{1,0:T(8,128)(2,1)}, bf16[768,2048]{1,0:T(8,128)(2,1)}, u32[]{:S(2)}, u32[]{:S(2)}) collective-permute-start(bf16[768,2048]{1,0:T(8,128)(2,1)} %shard_map.147.m_ref.refs_0_), channel_id=1, source_target_pairs={{0,1},{1,0},{2,3},{3,2},{4,5},{5,4},{6,7},{7,6},{8,9},{9,8},{10,11... | collective-permute-start | bytes 9437192 | tf_op jit(solution)/shard_map/ppermute | solution.py:443
  286.7 53.8 %collective-permute-start.23 = (bf16[768,1536]{1,0:T(8,128)(2,1)S(1)}, bf16[768,1536]{1,0:T(8,128)(2,1)}, u32[]{:S(2)}, u32[]{:S(2)}) collective-permute-start(bf16[768,1536]{1,0:T(8,128)(2,1)S(1)} %copy-done.11), channel_id=1, source_target_pairs={{0,2},{1,3},{2,0},{3,1},{4,6},{5,7},{6,4},{7,5},{8,10},{9,11},{10,... | collective-permute-start | bytes 7077896 | tf_op jit(solution)/shard_map/ppermute | solution.py:447
  346.0 3.1 collective-permute-start.24
  346.0 28.4 %collective-permute-start.32 = (bf16[768,768]{1,0:T(8,128)(2,1)S(1)}, bf16[768,768]{1,0:T(8,128)(2,1)S(1)}, u32[]{:S(2)}, u32[]{:S(2)}) collective-permute-start(bf16[768,768]{1,0:T(8,128)(2,1)S(1)} %copy-done.21), channel_id=1, source_target_pairs={{0,2},{1,3},{2,0},{3,1},{4,6},{5,7},{6,4},{7,5},{8,10},{9,11},{10,... | collective-permute-start | bytes 3538952 | tf_op jit(solution)/shard_map/ppermute | solution.py:447
  382.7 4.7 collective-permute-start.33
  407.5 12.0 %collective-permute-start.34 = (bf16[96,2048]{1,0:T(8,128)(2,1)S(1)}, bf16[96,2048]{1,0:T(8,128)(2,1)S(1)}, u32[]{:S(2)}, u32[]{:S(2)}) collective-permute-start(bf16[96,2048]{1,0:T(8,128)(2,1)S(1)} %get-tuple-element.114), channel_id=1, source_target_pairs={{8,0},{16,8},{24,16},{28,24},{20,28},{12,20},{4,12},{0,4},{9,1},{1... | collective-permute-start | bytes 1179656 | tf_op jit(solution)/shard_map/ppermute | solution.py:541
  409.5 18.5 %collective-permute-start.25 = (bf16[96,2048]{1,0:T(8,128)(2,1)S(1)}, bf16[96,2048]{1,0:T(8,128)(2,1)S(1)}, u32[]{:S(2)}, u32[]{:S(2)}) collective-permute-start(bf16[96,2048]{1,0:T(8,128)(2,1)S(1)} %get-tuple-element.120), channel_id=1, source_target_pairs={{8,0},{16,8},{24,16},{28,24},{20,28},{12,20},{4,12},{0,4},{9,1},{1... | collective-permute-start | bytes 1179656 | tf_op jit(solution)/shard_map/ppermute | solution.py:541
  410.8 29.1 %collective-permute-start.29 = (bf16[96,2048]{1,0:T(8,128)(2,1)S(1)}, bf16[96,2048]{1,0:T(8,128)(2,1)S(1)}, u32[]{:S(2)}, u32[]{:S(2)}) collective-permute-start(bf16[96,2048]{1,0:T(8,128)(2,1)S(1)} %get-tuple-element.121), channel_id=1, source_target_pairs={{0,8},{8,16},{16,24},{24,28},{28,20},{20,12},{12,4},{4,0},{1,9},{9... | collective-permute-start | bytes 1179656 | tf_op jit(solution)/shard_map/ppermute | solution.py:545
  411.6 18.2 %collective-permute-start.38 = (bf16[96,2048]{1,0:T(8,128)(2,1)S(1)}, bf16[96,2048]{1,0:T(8,128)(2,1)S(1)}, u32[]{:S(2)}, u32[]{:S(2)}) collective-permute-start(bf16[96,2048]{1,0:T(8,128)(2,1)S(1)} %get-tuple-element.115), channel_id=1, source_target_pairs={{0,8},{8,16},{16,24},{24,28},{28,20},{20,12},{12,4},{4,0},{1,9},{9... | collective-permute-start | bytes 1179656 | tf_op jit(solution)/shard_map/ppermute | solution.py:545
  420.7 15.8 %collective-permute-start.35 = (bf16[96,2048]{1,0:T(8,128)(2,1)S(1)}, bf16[96,2048]{1,0:T(8,128)(2,1)S(1)}, u32[]{:S(2)}, u32[]{:S(2)}) collective-permute-start(bf16[96,2048]{1,0:T(8,128)(2,1)S(1)} %add_convert_fusion.4), channel_id=1, source_target_pairs={{8,0},{16,8},{24,16},{28,24},{20,28},{12,20},{4,12},{0,4},{9,1},{1... | collective-permute-start | bytes 1179656 | tf_op jit(solution)/shard_map/ppermute | solution.py:541
  428.1 16.7 %collective-permute-start.26 = (bf16[96,2048]{1,0:T(8,128)(2,1)S(1)}, bf16[96,2048]{1,0:T(8,128)(2,1)S(1)}, u32[]{:S(2)}, u32[]{:S(2)}) collective-permute-start(bf16[96,2048]{1,0:T(8,128)(2,1)S(1)} %add_convert_fusion.9), channel_id=1, source_target_pairs={{8,0},{16,8},{24,16},{28,24},{20,28},{12,20},{4,12},{0,4},{9,1},{1... | collective-permute-start | bytes 1179656 | tf_op jit(solution)/shard_map/ppermute | solution.py:541
  437.8 15.5 %collective-permute-start.36 = (bf16[96,2048]{1,0:T(8,128)(2,1)S(1)}, bf16[96,2048]{1,0:T(8,128)(2,1)S(1)}, u32[]{:S(2)}, u32[]{:S(2)}) collective-permute-start(bf16[96,2048]{1,0:T(8,128)(2,1)S(1)} %get-tuple-element.112), channel_id=1, source_target_pairs={{8,0},{16,8},{24,16},{28,24},{20,28},{12,20},{4,12},{0,4},{9,1},{1... | collective-permute-start | bytes 1179656 | tf_op jit(solution)/shard_map/ppermute | solution.py:541
  438.6 14.6 %collective-permute-start.39 = (bf16[96,2048]{1,0:T(8,128)(2,1)S(1)}, bf16[96,2048]{1,0:T(8,128)(2,1)S(1)}, u32[]{:S(2)}, u32[]{:S(2)}) collective-permute-start(bf16[96,2048]{1,0:T(8,128)(2,1)S(1)} %get-tuple-element.113), channel_id=1, source_target_pairs={{0,8},{8,16},{16,24},{24,28},{28,20},{20,12},{12,4},{4,0},{1,9},{9... | collective-permute-start | bytes 1179656 | tf_op jit(solution)/shard_map/ppermute | solution.py:545
  445.1 16.6 %collective-permute-start.27 = (bf16[96,2048]{1,0:T(8,128)(2,1)S(1)}, bf16[96,2048]{1,0:T(8,128)(2,1)S(1)}, u32[]{:S(2)}, u32[]{:S(2)}) collective-permute-start(bf16[96,2048]{1,0:T(8,128)(2,1)S(1)} %get-tuple-element.118), channel_id=1, source_target_pairs={{8,0},{16,8},{24,16},{28,24},{20,28},{12,20},{4,12},{0,4},{9,1},{1... | collective-permute-start | bytes 1179656 | tf_op jit(solution)/shard_map/ppermute | solution.py:541
  445.9 15.7 %collective-permute-start.30 = (bf16[96,2048]{1,0:T(8,128)(2,1)S(1)}, bf16[96,2048]{1,0:T(8,128)(2,1)S(1)}, u32[]{:S(2)}, u32[]{:S(2)}) collective-permute-start(bf16[96,2048]{1,0:T(8,128)(2,1)S(1)} %get-tuple-element.119), channel_id=1, source_target_pairs={{0,8},{8,16},{16,24},{24,28},{28,20},{20,12},{12,4},{4,0},{1,9},{9... | collective-permute-start | bytes 1179656 | tf_op jit(solution)/shard_map/ppermute | solution.py:545
  455.5 18.0 %collective-permute-start.40 = (bf16[96,2048]{1,0:T(8,128)(2,1)}, bf16[96,2048]{1,0:T(8,128)(2,1)S(1)}, u32[]{:S(2)}, u32[]{:S(2)}) collective-permute-start(bf16[96,2048]{1,0:T(8,128)(2,1)} %get-tuple-element.111), channel_id=1, source_target_pairs={{0,8},{8,16},{16,24},{24,28},{28,20},{20,12},{12,4},{4,0},{1,9},{9... | collective-permute-start | bytes 1179656 | tf_op jit(solution)/shard_map/ppermute | solution.py:545
  457.1 16.4 %collective-permute-start.37 = (bf16[96,2048]{1,0:T(8,128)(2,1)}, bf16[96,2048]{1,0:T(8,128)(2,1)}, u32[]{:S(2)}, u32[]{:S(2)}) collective-permute-start(bf16[96,2048]{1,0:T(8,128)(2,1)} %get-tuple-element.110), channel_id=1, source_target_pairs={{8,0},{16,8},{24,16},{28,24},{20,28},{12,20},{4,12},{0,4},{9,1},{1... | collective-permute-start | bytes 1179656 | tf_op jit(solution)/shard_map/ppermute | solution.py:541
  462.9 37.3 %collective-permute-start.31 = (bf16[96,2048]{1,0:T(8,128)(2,1)}, bf16[96,2048]{1,0:T(8,128)(2,1)}, u32[]{:S(2)}, u32[]{:S(2)}) collective-permute-start(bf16[96,2048]{1,0:T(8,128)(2,1)} %get-tuple-element.117), channel_id=1, source_target_pairs={{0,8},{8,16},{16,24},{24,28},{28,20},{20,12},{12,4},{4,0},{1,9},{9... | collective-permute-start | bytes 1179656 | tf_op jit(solution)/shard_map/ppermute | solution.py:545
  464.4 35.7 %collective-permute-start.28 = (bf16[96,2048]{1,0:T(8,128)(2,1)}, bf16[96,2048]{1,0:T(8,128)(2,1)}, u32[]{:S(2)}, u32[]{:S(2)}) collective-permute-start(bf16[96,2048]{1,0:T(8,128)(2,1)} %get-tuple-element.116), channel_id=1, source_target_pairs={{8,0},{16,8},{24,16},{28,24},{20,28},{12,20},{4,12},{0,4},{9,1},{1... | collective-permute-start | bytes 1179656 | tf_op jit(solution)/shard_map/ppermute | solution.py:541
  475.2 9.2 %collective-permute-start.41 = (f32[96]{0:T(128)S(1)}, f32[96]{0:T(128)S(1)}, u32[]{:S(2)}, u32[]{:S(2)}) collective-permute-start(f32[96]{0:T(128)S(1)} %get-tuple-element.109), channel_id=1, source_target_pairs={{0,1},{1,0},{2,3},{3,2},{4,5},{5,4},{6,7},{7,6},{8,9},{9,8},{10,11... | collective-permute-start | bytes 1160 | tf_op jit(solution)/shard_map/ppermute | solution.py:443
  483.6 10.4 %collective-permute-start.43 = (f32[2048]{0:T(1024)S(1)}, f32[2048]{0:T(1024)S(1)}, u32[]{:S(2)}, u32[]{:S(2)}) collective-permute-start(f32[2048]{0:T(1024)S(1)} %get-tuple-element.108), channel_id=1, source_target_pairs={{0,4},{4,0},{8,12},{12,8},{16,20},{20,16},{24,28},{28,24},{1,5},{5... | collective-permute-start | bytes 24584 | tf_op jit(solution)/shard_map/ppermute | solution.py:578
  484.4 11.1 %collective-permute-start.42 = (f32[96]{0:T(128)S(1)}, f32[96]{0:T(128)S(1)}, u32[]{:S(2)}, u32[]{:S(2)}) collective-permute-start(f32[96]{0:T(128)S(1)} %add.94), channel_id=1, source_target_pairs={{0,2},{1,3},{2,0},{3,1},{4,6},{5,7},{6,4},{7,5},{8,10},{9,11},{10,... | collective-permute-start | bytes 1160 | tf_op jit(solution)/shard_map/ppermute | solution.py:447
  493.9 3.7 collective-permute-start.44
  497.7 5.5 %collective-permute-start.45 = (f32[2048]{0:T(1024)S(1)}, f32[2048]{0:T(1024)S(1)}, u32[]{:S(2)}, u32[]{:S(2)}) collective-permute-start(f32[2048]{0:T(1024)S(1)} %add.98), channel_id=1, source_target_pairs={{0,16},{4,20},{8,24},{12,28},{16,0},{20,4},{24,8},{28,12},{1,17},{... | collective-permute-start | bytes 24584 | tf_op jit(solution)/shard_map/ppermute | solution.py:578
  (28 other events, 259.4 us)

commit v4 on v2

--- a/solution.py
+++ b/solution.py
@@ -107,18 +107,22 @@
             row += ref.shape[0]
 
 
-def project(side, plan, chunk, halves, tokens, weights, added=None, inverse_gain=None):
+def project(side, plan, chunk, halves, tokens, weights, added=None, inverse_gain=None,
+            keep=True):
     first, steps = chunk
     local, depth = tokens[0].shape
     rows, tile, count = local * len(tokens), plan.tile, len(tokens)
 
     def body(_, *refs):
-        scratch = refs[-1]
+        scratch = refs[-1] if keep else refs[-2]
         g_ref, u_ref, gm_ref, um_ref = refs[count:count + 4]
-        rest = refs[count + 4:-1]
+        rest = refs[count + 4:-1] if keep else refs[count + 4:-2]
+        kept_ref = rest[-1] if keep else refs[-1]
+        if keep:
+            rest = rest[:-1]
         gathered(refs[:count], scratch)
         if inverse_gain is not None:
-            gain_ref, out_ref, kept_ref, sum_ref = rest
+            gain_ref, out_ref, sum_ref = rest
 
             @pl.when(pl.program_id(0) == 0)
             def _():
@@ -126,7 +130,7 @@
                     value = scratch[row:row + local, :].astype(f32) * gain_ref[...]
                     sum_ref[row:row + local, :] = jnp.sum(value * value, axis=1, keepdims=True)
         else:
-            out_ref, kept_ref = rest[-2:]
+            out_ref = rest[-1]
         for w_ref, k_ref, lane in ((g_ref, gm_ref, 0), (u_ref, um_ref, tile)):
             for index in range(depth // BLOCK):
                 span = pl.ds(index * BLOCK, BLOCK)
@@ -144,19 +148,24 @@
     kept = pl.BlockSpec((depth, 2 * tile), lambda j, h: (0, j))
     width = 2 * steps * tile
     extra, extra_specs = [], []
-    out_specs = [out, kept]
-    shapes = [jax.ShapeDtypeStruct((rows, width), bf16),
-              jax.ShapeDtypeStruct((depth, width), bf16)]
+    out_specs = [out]
+    shapes = [jax.ShapeDtypeStruct((rows, width), bf16)]
+    scratch_shapes = [pltpu.VMEM((rows, depth), bf16)]
     if added is not None:
         extra, extra_specs = [added], [out]
     if inverse_gain is not None:
         extra, extra_specs = [inverse_gain], [whole(inverse_gain)]
         out_specs.append(pl.BlockSpec((rows, 1), lambda j, h: (0, 0)))
         shapes.append(jax.ShapeDtypeStruct((rows, 1), f32))
+    if keep:
+        out_specs.append(kept)
+        shapes.append(jax.ShapeDtypeStruct((depth, width), bf16))
+    else:
+        scratch_shapes.append(pltpu.VMEM((depth, 2 * tile), bf16))
     return call(
         body, (steps,), halves, (*tokens, *weights, *extra),
         [whole(value) for value in tokens] + [weight, weight, mask, mask] + extra_specs,
-        out_specs, shapes, [pltpu.VMEM((rows, depth), bf16)],
+        out_specs, shapes, scratch_shapes,
         2 * rows * depth * width, 4 * depth * width + 2 * rows * depth + 4 * rows * width)
 
 
@@ -187,12 +196,14 @@
 
 
 def activate(plan, scalars, scale, pair, grads, with_hidden):
-    rows, width = pair[0].shape
+    rows, width = scale.shape[0], pair[0][0].shape[1]
     tile = plan.tile
-    count = len(pair)
-    operands = [scale, *pair, *(grads or ())]
+    flat = [array for piece in pair for array in piece]
+    count = len(flat)
+    operands = [scale, *flat, *(grads or ())]
     in_specs = [whole(scale)]
-    in_specs += [pl.BlockSpec((rows, 2 * tile), lambda j, s: (0, j)) for _ in pair]
+    in_specs += [pl.BlockSpec((a.shape[0], 2 * tile), lambda j, s: (0, j)) for a in flat]
+    step = 96 if all(a.shape[0] % 96 == 0 for a in flat) else 16
     in_specs += [pl.BlockSpec((rows, tile), lambda j, s: (0, j)) for _ in grads or ()]
     out_specs, shapes = [], []
     if grads:
@@ -211,11 +222,17 @@
 
     def body(_, s_ref, *refs):
         outs = refs[len(operands) - 1:]
-        for low in range(0, rows, 96 if rows % 96 == 0 else 16):
-            high = low + (96 if rows % 96 == 0 else 16)
+        for low in range(0, rows, step):
+            high = low + step
             factor = s_ref[low:high, :]
-            gate = summed(refs[:count], low, high, 0) * factor
-            up = summed(refs[:count], low, high, tile) * factor
+            base, first = 0, 0
+            for piece in pair:
+                if low < base + piece[0].shape[0]:
+                    break
+                base, first = base + piece[0].shape[0], first + len(piece)
+            source = refs[first:first + len(piece)]
+            gate = summed(source, low - base, high - base, 0) * factor
+            up = summed(source, low - base, high - base, tile) * factor
             sigma = jax.nn.sigmoid(gate)
             silu = gate * sigma
             if grads:
@@ -451,51 +468,57 @@
 
     shard = {0: scaled}
     ring_step(shard, 1)
-    down_lanes = lanes(mask_down)
-    dn = [mask_rows(plan, chunks[0], halves, w_down, down_lanes)]
-    ring_step(shard, 2, dn[0])
-    dn.append(mask_rows(plan, chunks[1], after(halves, dn[0]), w_down, down_lanes))
-    ring_step(shard, 3, dn[1])
-    gate_lanes = lanes(after(mask_gate, dn[1]))
-    up_lanes = lanes(after(mask_up, dn[1]))
+    gate_lanes, up_lanes = lanes(mask_gate), lanes(mask_up)
+    weights = (w_gate, w_up, gate_lanes, up_lanes)
+    inverse_gain = (1.0 / norm_gain)[None]
+    ring_step(shard, 2, gate_lanes, up_lanes)
+    near = [shard[offset] for offset in offsets[:3]]
+    sent0n, squares_near = project(
+        1, plan, chunks[0], halves, near, weights,
+        inverse_gain=inverse_gain, keep=False)
+    ring_step(shard, 3, sent0n)
+    got0n = to_partner(sent0n)
+    down_lanes = lanes(after(mask_down, sent0n))
+    own0n, = project(
+        0, plan, chunks[0], after(halves, sent0n), near, weights, got0n, keep=False)
+    others0n = from_chips(own0n)
     for k in range(4, n_ahead + 1):
-        ring_step(shard, k, gate_lanes, up_lanes)
-    tokens = [shard[offset] for offset in offsets]
-    weights = (w_gate, w_up, gate_lanes, up_lanes)
-
-    sent0, kept0_o, squares = project(
-        1, plan, chunks[0], halves, tokens, weights,
-        inverse_gain=(1.0 / norm_gain)[None])
-    grad_shard = {0: after(grad_out, *tokens)}
+        ring_step(shard, k, own0n)
+    dn = [mask_rows(plan, chunks[0], after(halves, own0n), w_down, down_lanes)]
+    far = [shard[offset] for offset in offsets[3:]]
+    tokens = near + far
+    grad_shard = {0: after(grad_out, *far)}
     ring_step(grad_shard, 1)
-    squares = squares[:, 0]
+    sent0f, squares_far, kept0_o = project(
+        1, plan, chunks[0], after(halves, dn[0]), far, weights,
+        inverse_gain=inverse_gain)
+    ring_step(grad_shard, 2, sent0f)
+    got0f = to_partner(sent0f)
+    own0f, kept0_m = project(
+        0, plan, chunks[0], after(halves, sent0f), far, weights, got0f)
+    others0f = from_chips(after(own0f, *others0n))
+    squares = jnp.concatenate([squares_near[:, 0], squares_far[:, 0]])
     squares = squares + to_partner(squares)
-    got0 = to_partner(sent0)
-    own0, kept0_m = project(
-        0, plan, chunks[0], after(halves, sent0), tokens, weights, got0)
-    others = from_chips(squares)
-    for other in others:
+    for other in from_chips(squares):
         squares = squares + other
-    scale = lax.rsqrt(squares / features + epsilon)[:, None]
-    others0 = from_chips(after(own0, *others))
-
-    ring_step(grad_shard, 2, own0)
-    sent1, kept1_o = project(1, plan, chunks[1], after(halves, own0), tokens, weights)
-    ring_step(grad_shard, 3, sent1)
+    ring_step(grad_shard, 3, own0f)
+    sent1, kept1_o = project(1, plan, chunks[1], after(halves, own0f), tokens, weights)
+    scale = lax.rsqrt(after(squares, sent1) / features + epsilon)[:, None]
+    for k in range(4, n_ahead + 1):
+        ring_step(grad_shard, k, sent1)
     turned = turn(after(halves, sent1), scale, tokens)
-    for k in range(4, n_ahead + 1):
-        ring_step(grad_shard, k, turned)
+    grads = [grad_shard[offset] for offset in offsets]
+    sent_b0 = back_project(1, after(halves, turned), grads, dn[0])
+    own_b0 = back_project(0, halves, grads, dn[0], to_partner(sent_b0))
+    others_b0 = from_chips(after(own_b0, *others0f))
     own1, kept1_m = project(
-        0, plan, chunks[1], after(halves, turned), tokens, weights, to_partner(sent1))
-    grads = [grad_shard[offset] for offset in offsets]
-    sent_b0 = back_project(1, after(halves, own1), grads, dn[0])
-    sent_b1 = back_project(1, after(halves, sent_b0), grads, dn[1])
-    got_b1 = to_partner(sent_b1)
-    own_b0 = back_project(0, after(halves, sent_b1), grads, dn[0], to_partner(sent_b0))
-    others_b0 = from_chips(after(own_b0, *others0))
-    own_b1 = back_project(0, after(halves, own_b0), grads, dn[1], got_b1)
+        0, plan, chunks[1], after(halves, own_b0), tokens, weights, to_partner(sent1))
     others1 = from_chips(after(own1, *others_b0))
-    cot0, hidden0 = activate(plan, after(halves, own_b1), scale, [own0, *others0],
+    dn.append(mask_rows(plan, chunks[1], after(halves, own1), w_down, down_lanes))
+    sent_b1 = back_project(1, halves, grads, dn[1])
+    own_b1 = back_project(0, halves, grads, dn[1], to_partner(sent_b1))
+    cot0, hidden0 = activate(plan, after(halves, own_b1), scale,
+                             [[own0n, *others0n], [own0f, *others0f]],
                              [own_b0, *others_b0], True)
     cot0 = (cot0, to_partner(cot0))
     hidden0 = (hidden0, to_partner(hidden0))
@@ -504,7 +527,7 @@
                             cot0[:1], cot0[1:], gate_lanes, up_lanes, None)
 
     others_b1 = from_chips(after(own_b1, *others1))
-    hidden1, = activate(plan, after(halves, grad_gu[0]), scale, [own1, *others1],
+    hidden1, = activate(plan, after(halves, grad_gu[0]), scale, [[own1, *others1]],
                         None, True)
     hidden1 = (hidden1, to_partner(hidden1))
     mixed = down_product(halves, (hidden0, hidden1), dn)
@@ -528,7 +551,7 @@
         return lambda offset: parts[offset]
 
     output = (inputs_wide + scatter(part_of(mixed))).astype(bf16)
-    cot1, = activate(plan, after(halves, mixed), scale, [own1, *others1],
+    cot1, = activate(plan, after(halves, mixed), scale, [[own1, *others1]],
                      [own_b1, *others_b1], False)
     cot1 = (cot1, to_partner(cot1))
     norm_all = input_cotangent(halves, cot1, (kept1_m, kept1_o), partial, bf16)

time: 455 us -> 455 us (level)
  waiting for transfers between devices: 126 us -> 112 us
  Pallas kernels: 247 us -> 260 us
    pallas_call x22 -> x24, Pallas kernels: 247 us -> 260 us  [call(): pl.pallas_call(body, grid_spec=pltpu.PrefetchScalarGridSpec(num_scalar_pr...]
    ppermute x6, waiting for transfers between devices: 11.3 us -> 1.53 us  [ring_step(): found[k] = lax.ppermute(after(found[k - 1], *ready), 'row', behind)]
    ppermute x8, waiting for transfers between devices: 12.8 us -> 20.8 us  [ring_step(): found[-k] = lax.ppermute(after(found[1 - k], *ready), 'row', ahead)]
    ppermute x6 -> x7, waiting for transfers between devices: 53.1 us -> 45.1 us  [from_chips(): lax.ppermute(value, 'col', [(i, (i + CORES * k) % n_col) for i in range(n...]
    ppermute x10 -> x11, waiting for transfers between devices: 16.3 us -> 11.3 us  [to_partner(): return lax.ppermute(value, 'col', swap)]
    ppermute x6 -> x7, starting transfers between devices: 8.92 us -> 10.5 us  [from_chips(): lax.ppermute(value, 'col', [(i, (i + CORES * k) % n_col) for i in range(n...]
    unnamed x66 -> x70, local copies, waits for them, and re-layouts: 10.7 us -> 9.51 us
  transfers between devices with their start and end apart: 47 -> 49, of which waited for: 24 -> 21; matrix products, arithmetic and copies ran while one was open for 5% -> 5% of each run, Pallas kernels for 43% -> 50%
where the time goes in v4:
time: 455 us; the launch traced here: 452 us
  Pallas kernels  260 us (57%)
  waiting for transfers between devices  112 us (25%)
  starting transfers between devices  44.6 us (10%)
  local copies, waits for them, and re-layouts  17.8 us (4%)
  other arithmetic  16.9 us (4%)
    pallas_call x24, Pallas kernels, call(): pl.pallas_call(body, grid_spec=pltpu.PrefetchScalarGridSpec(num_scalar_pr...  260 us
    ppermute x7, waiting for transfers between devices, from_chips(): lax.ppermute(value, 'col', [(i, (i + CORES * k) % n_col) for i in range(n...  45.1 us
    ppermute x8, waiting for transfers between devices, scatter(): back = lax.ppermute(back, 'row', behind)  30.2 us
    ppermute x8, waiting for transfers between devices, ring_step(): found[-k] = lax.ppermute(after(found[1 - k], *ready), 'row', ahead)  20.8 us
    ppermute x8, starting transfers between devices, ring_step(): found[-k] = lax.ppermute(after(found[1 - k], *ready), 'row', ahead)  14.5 us
    ppermute x11, waiting for transfers between devices, to_partner(): return lax.ppermute(value, 'col', swap)  11.3 us
    ppermute x7, starting transfers between devices, from_chips(): lax.ppermute(value, 'col', [(i, (i + CORES * k) % n_col) for i in range(n...  10.5 us
    unnamed x70, local copies, waits for them, and re-layouts  9.51 us
  transfers between devices with their start and end apart: 49, of which 21 were waited for; matrix products, arithmetic and copies ran while one was open for 5% of the time, Pallas kernels for 50%

profile of v4, /device:TPU:0, one launch (start us, length us, event | category | flops | bytes accessed | tf_op | source)
XLA Modules:
  0.0 452.4 jit_solution(16082819643314286121)
XLA Ops:
  1.7 3.1 collective-permute-start
  9.4 4.5 collective-permute-done.refs_1_
  16.2 8.4 %shard_map.136 = (bf16[288,2048]{1,0:T(8,128)(2,1)}, f32[288,1]{1,0:T(8,128)}) custom-call(s32[2]{0:T(128)} %pad_add_fusion._.half_ref, bf16[96,2048]{1,0:T(8,128)(2,1)} %copy-done.1, bf16[96,2048]{1,0:T(8,128)(2,1)} %copy-done.2, bf16[96,2048]{1,0:T(8,128)(2,1)} %copy-done.3, bf16[2048,3584]{1,0:T(8,128)(2,1)} %refs_8_.3, bf16[2048,3584]{1,0:T(8,128)(2,1)} %refs_9_.3, ...), custom_call_target="tpu_custom_call" | custom-call | flops 2415919104 | bytes 20316160 | tf_op jit(solution)/shard_map/pallas_call | solution.py:53
  24.7 1.6 collective-permute-start.1
  26.7 9.6 %collective-permute-done.1.refs_0_.refs_3_ = bf16[96,2048]{1,0:T(8,128)(2,1)S(1)} collective-permute-done((bf16[96,2048]{1,0:T(8,128)(2,1)}, bf16[96,2048]{1,0:T(8,128)(2,1)S(1)}, u32[]{:S(2)}, u32[]{:S(2)}) %collective-permute-start.1) | collective-permute-done | bytes 393248 | tf_op jit(solution)/shard_map/ppermute | solution.py:465
  39.4 8.3 %shard_map.137.refs_0_ = bf16[288,2048]{1,0:T(8,128)(2,1)} custom-call(s32[2]{0:T(128)} %pad_add_fusion._.half_ref, bf16[96,2048]{1,0:T(8,128)(2,1)} %copy-done.1, bf16[96,2048]{1,0:T(8,128)(2,1)} %copy-done.2, bf16[96,2048]{1,0:T(8,128)(2,1)} %copy-done.3, bf16[2048,3584]{1,0:T(8,128)(2,1)} %refs_8_.3, bf16[2048,3584]{1,0:T(8,128)(2,1)} %refs_9_.3, ...), custom_call_target="tpu_custom_call" | custom-call | flops 2415919104 | bytes 20316160 | tf_op jit(solution)/shard_map/pallas_call | solution.py:53
  47.7 1.6 collective-permute-start.7
  50.9 9.9 %shard_map.138.refs_8_.refs_1_.refs_3_ = bf16[2048,2048]{1,0:T(8,128)(2,1)} custom-call(s32[2]{0:T(128)} %pad_add_fusion._.half_ref, bf16[3584,2048]{1,0:T(8,128)(2,1)} %w_ref.3, f32[56,2048]{1,0:T(8,128)} %reshape.30.k_ref.refs_12_), custom_call_target="tpu_custom_call" | custom-call | bytes 16777216 | tf_op jit(solution)/shard_map/pallas_call | solution.py:53
  62.4 11.6 %shard_map.139 = (bf16[480,2048]{1,0:T(8,128)(2,1)}, f32[480,1]{1,0:T(8,128)}, bf16[2048,2048]{1,0:T(8,128)(2,1)}) custom-call(s32[2]{0:T(128)} %pad_add_fusion._.half_ref, bf16[96,2048]{1,0:T(8,128)(2,1)} %copy-done.4, bf16[96,2048]{1,0:T(8,128)(2,1)} %copy-done.5, bf16[96,2048]{1,0:T(8,128)(2,1)} %copy-done.6, bf16[96,2048]{1,0:T(8,128)(2,1)} %copy-done.7, ...), custom_call_target="tpu_custom_call" | custom-call | flops 4026531840 | bytes 22675456 | tf_op jit(solution)/shard_map/pallas_call | solution.py:53
  78.9 6.6 %collective-permute-done.8.refs_1_.refs_5_ = bf16[96,2048]{1,0:T(8,128)(2,1)S(1)} collective-permute-done((bf16[96,2048]{1,0:T(8,128)(2,1)S(1)}, bf16[96,2048]{1,0:T(8,128)(2,1)S(1)}, u32[]{:S(2)}, u32[]{:S(2)}) %collective-permute-start.8) | collective-permute-done | bytes 393248 | tf_op jit(solution)/shard_map/ppermute | solution.py:465
  87.7 11.6 %shard_map.140 = (bf16[480,2048]{1,0:T(8,128)(2,1)}, bf16[2048,2048]{1,0:T(8,128)(2,1)}) custom-call(s32[2]{0:T(128)} %pad_add_fusion._.half_ref, bf16[96,2048]{1,0:T(8,128)(2,1)} %copy-done.4, bf16[96,2048]{1,0:T(8,128)(2,1)} %copy-done.5, bf16[96,2048]{1,0:T(8,128)(2,1)} %copy-done.6, bf16[96,2048]{1,0:T(8,128)(2,1)} %copy-done.7, ...), custom_call_target="tpu_custom_call" | custom-call | flops 4026531840 | bytes 22675456 | tf_op jit(solution)/shard_map/pallas_call | solution.py:53
  101.4 10.6 %shard_map.141 = (bf16[768,1536]{1,0:T(8,128)(2,1)}, bf16[2048,1536]{1,0:T(8,128)(2,1)}) custom-call(s32[2]{0:T(128)} %pad_add_fusion._.half_ref, bf16[96,2048]{1,0:T(8,128)(2,1)} %copy-done.1, bf16[96,2048]{1,0:T(8,128)(2,1)} %copy-done.2, bf16[96,2048]{1,0:T(8,128)(2,1)} %copy-done.3, bf16[96,2048]{1,0:T(8,128)(2,1)} %copy-done.4, ...), custom_call_target="tpu_custom_call" | custom-call | flops 4831838208 | bytes 20447232 | tf_op jit(solution)/shard_map/pallas_call | solution.py:53
  112.1 1.8 collective-permute-start.15
  115.4 2.1 collective-permute-done.17
  118.5 7.9 %shard_map.142.x_ref = bf16[2048,768]{1,0:T(8,128)(2,1)} custom-call(s32[2]{0:T(128)} %pad_add_fusion._.half_ref, f32[768,1]{1,0:T(8,128)} %broadcast_in_dim.15.s_ref, bf16[96,2048]{1,0:T(8,128)(2,1)} %copy-done.1, bf16[96,2048]{1,0:T(8,128)(2,1)} %copy-done.2, bf16[96,2048]{1,0:T(8,128)(2,1)} %copy-done.3, bf16[96,2048]{1,0:T(8,128)(2,1)} %copy-done.4, ...), custom_call_target="tpu_custom_call" | custom-call | bytes 6291456 | tf_op jit(solution)/shard_map/pallas_call | solution.py:53
  127.9 8.4 %shard_map.143 = bf16[768,1024]{1,0:T(8,128)(2,1)} custom-call(s32[2]{0:T(128)} %pad_add_fusion._.half_ref, bf16[96,2048]{1,0:T(8,128)(2,1)} %refs_4_.4, bf16[96,2048]{1,0:T(8,128)(2,1)} %copy-done.12, bf16[96,2048]{1,0:T(8,128)(2,1)} %copy-done.13, bf16[96,2048]{1,0:T(8,128)(2,1)} %copy-done.14, bf16[96,2048]{1,0:T(8,128)(2,1)} %copy-done.15, ...), custom_call_target="tpu_custom_call" | custom-call | flops 3221225472 | bytes 8912896 | tf_op jit(solution)/shard_map/pallas_call | solution.py:53
  138.3 1.8 collective-permute-done.18.refs_9_
  141.2 8.6 %shard_map.144.refs_4_ = bf16[768,1024]{1,0:T(8,128)(2,1)} custom-call(s32[2]{0:T(128)} %pad_add_fusion._.half_ref, bf16[96,2048]{1,0:T(8,128)(2,1)} %refs_4_.4, bf16[96,2048]{1,0:T(8,128)(2,1)} %copy-done.12, bf16[96,2048]{1,0:T(8,128)(2,1)} %copy-done.13, bf16[96,2048]{1,0:T(8,128)(2,1)} %copy-done.14, bf16[96,2048]{1,0:T(8,128)(2,1)} %copy-done.15, ...), custom_call_target="tpu_custom_call" | custom-call | flops 3221225472 | bytes 8912896 | tf_op jit(solution)/shard_map/pallas_call | solution.py:53
  149.8 11.3 %shard_map.145 = (bf16[768,1536]{1,0:T(8,128)(2,1)}, bf16[2048,1536]{1,0:T(8,128)(2,1)}) custom-call(s32[2]{0:T(128)} %pad_add_fusion._.half_ref, bf16[96,2048]{1,0:T(8,128)(2,1)} %copy-done.1, bf16[96,2048]{1,0:T(8,128)(2,1)} %copy-done.2, bf16[96,2048]{1,0:T(8,128)(2,1)} %copy-done.3, bf16[96,2048]{1,0:T(8,128)(2,1)} %copy-done.4, ...), custom_call_target="tpu_custom_call" | custom-call | flops 4831838208 | bytes 20447232 | tf_op jit(solution)/shard_map/pallas_call | solution.py:53
  161.2 7.8 %shard_map.146.refs_8_.refs_5_.refs_7_ = bf16[1536,2048]{1,0:T(8,128)(2,1)} custom-call(s32[2]{0:T(128)} %pad_add_fusion._.half_ref, bf16[3584,2048]{1,0:T(8,128)(2,1)} %w_ref.3, f32[56,2048]{1,0:T(8,128)} %reshape.30.k_ref.refs_12_), custom_call_target="tpu_custom_call" | custom-call | bytes 12582912 | tf_op jit(solution)/shard_map/pallas_call | solution.py:53
  169.0 12.8 %collective-permute-done.22.refs_3_ = bf16[480,2048]{1,0:T(8,128)(2,1)S(1)} collective-permute-done((bf16[480,2048]{1,0:T(8,128)(2,1)}, bf16[480,2048]{1,0:T(8,128)(2,1)S(1)}, u32[]{:S(2)}, u32[]{:S(2)}) %collective-permute-start.22) | collective-permute-done | bytes 1966112 | tf_op jit(solution)/shard_map/ppermute | solution.py:442
  183.3 7.3 %shard_map.147 = bf16[768,768]{1,0:T(8,128)(2,1)} custom-call(s32[2]{0:T(128)} %pad_add_fusion._.half_ref, bf16[96,2048]{1,0:T(8,128)(2,1)} %refs_4_.4, bf16[96,2048]{1,0:T(8,128)(2,1)} %copy-done.12, bf16[96,2048]{1,0:T(8,128)(2,1)} %copy-done.13, bf16[96,2048]{1,0:T(8,128)(2,1)} %copy-done.14, bf16[96,2048]{1,0:T(8,128)(2,1)} %copy-done.15, ...), custom_call_target="tpu_custom_call" | custom-call | flops 2415919104 | bytes 7471104 | tf_op jit(solution)/shard_map/pallas_call | solution.py:53
  190.6 3.2 collective-permute-done.20.refs_9_
  193.7 7.5 %shard_map.148.refs_2_ = bf16[768,768]{1,0:T(8,128)(2,1)} custom-call(s32[2]{0:T(128)} %pad_add_fusion._.half_ref, bf16[96,2048]{1,0:T(8,128)(2,1)} %refs_4_.4, bf16[96,2048]{1,0:T(8,128)(2,1)} %copy-done.12, bf16[96,2048]{1,0:T(8,128)(2,1)} %copy-done.13, bf16[96,2048]{1,0:T(8,128)(2,1)} %copy-done.14, bf16[96,2048]{1,0:T(8,128)(2,1)} %copy-done.15, ...), custom_call_target="tpu_custom_call" | custom-call | flops 2415919104 | bytes 7471104 | tf_op jit(solution)/shard_map/pallas_call | solution.py:53
  201.2 16.2 %collective-permute-done.23.refs_5_ = bf16[768,1024]{1,0:T(8,128)(2,1)} collective-permute-done((bf16[768,1024]{1,0:T(8,128)(2,1)S(1)}, bf16[768,1024]{1,0:T(8,128)(2,1)}, u32[]{:S(2)}, u32[]{:S(2)}) %collective-permute-start.23) | collective-permute-done | bytes 1572896 | tf_op jit(solution)/shard_map/ppermute | solution.py:442
  217.4 8.4 %shard_map.149 = (bf16[768,2048]{1,0:T(8,128)(2,1)}, bf16[768,1024]{1,0:T(8,128)(2,1)}) custom-call(s32[2]{0:T(128)} %pad_add_fusion._.half_ref, f32[768,1]{1,0:T(8,128)} %broadcast_in_dim.15.s_ref, bf16[288,2048]{1,0:T(8,128)(2,1)} %shard_map.137.refs_0_, bf16[288,2048]{1,0:T(8,128)(2,1)} %collective-permute-done.21.refs_1_, ...), custom_call_target="tpu_custom_call" | custom-call | bytes 14157312 | tf_op jit(solution)/shard_map/pallas_call | solution.py:53
  227.8 4.0 collective-permute-done.25.o_ref.refs_1_
  231.8 19.8 %shard_map.150.rest_0_ = f32[768,2048]{1,0:T(8,128)} custom-call(s32[2]{0:T(128)} %pad_add_fusion._.half_ref, bf16[768,2048]{1,0:T(8,128)(2,1)} %get-tuple-element.94.m_ref.refs_0_, bf16[768,2048]{1,0:T(8,128)(2,1)} %collective-permute-done.25.o_ref.refs_1_, bf16[2048,2048]{1,0:T(8,128)(2,1)} %get-tuple-element.95.wm_ref, ...), custom_call_target="tpu_custom_call" | custom-call | flops 12884901888 | bytes 29360128 | tf_op jit(solution)/shard_map/pallas_call | solution.py:53
  251.7 20.1 %shard_map.151 = (bf16[2048,3584]{1,0:T(8,128)(2,1)}, bf16[2048,3584]{1,0:T(8,128)(2,1)}) custom-call(s32[2]{0:T(128)} %pad_add_fusion._.half_ref, bf16[2048,768]{1,0:T(8,128)(2,1)} %shard_map.142.x_ref, bf16[768,2048]{1,0:T(8,128)(2,1)} %get-tuple-element.94.m_ref.refs_0_, bf16[768,2048]{1,0:T(8,128)(2,1)} %collective-permute-done.25.o_ref.refs_1_, ...), custom_call_target="tpu_custom_call" | custom-call | flops 12884901888 | bytes 26214400 | tf_op jit(solution)/shard_map/pallas_call | solution.py:53
  271.8 7.9 %collective-permute-done.26.refs_1_ = bf16[768,1536]{1,0:T(8,128)(2,1)} collective-permute-done((bf16[768,1536]{1,0:T(8,128)(2,1)S(1)}, bf16[768,1536]{1,0:T(8,128)(2,1)}, u32[]{:S(2)}, u32[]{:S(2)}) %collective-permute-start.26) | collective-permute-done | bytes 2359328 | tf_op jit(solution)/shard_map/ppermute | solution.py:442
  279.7 5.3 %shard_map.152.refs_4_.refs_2_ = bf16[768,768]{1,0:T(8,128)(2,1)} custom-call(s32[2]{0:T(128)} %pad_add_fusion._.half_ref, f32[768,1]{1,0:T(8,128)} %broadcast_in_dim.15.s_ref, bf16[768,1536]{1,0:T(8,128)(2,1)} %get-tuple-element.100.refs_0_, bf16[768,1536]{1,0:T(8,128)(2,1)} %collective-permute-done.26.refs_1_), custom_call_target="tpu_custom_call" | custom-call | bytes 8259072 | tf_op jit(solution)/shard_map/pallas_call | solution.py:53
  289.1 18.2 %shard_map.153 = bf16[768,2048]{1,0:T(8,128)(2,1)} custom-call(s32[2]{0:T(128)} %pad_add_fusion._.half_ref, bf16[768,1024]{1,0:T(8,128)(2,1)} %get-tuple-element.93.refs_0_, bf16[2048,2048]{1,0:T(8,128)(2,1)} %shard_map.138.refs_8_.refs_1_.refs_3_, bf16[768,1024]{1,0:T(8,128)(2,1)} %collective-permute-done.24.refs_2_.refs_1_, ...), custom_call_target="tpu_custom_call" | custom-call | flops 11274289152 | bytes 23330816 | tf_op jit(solution)/shard_map/pallas_call | solution.py:53
  307.3 6.0 %collective-permute-done.35.refs_3_ = bf16[768,768]{1,0:T(8,128)(2,1)S(1)} collective-permute-done((bf16[768,768]{1,0:T(8,128)(2,1)S(1)}, bf16[768,768]{1,0:T(8,128)(2,1)S(1)}, u32[]{:S(2)}, u32[]{:S(2)}) %collective-permute-start.35) | collective-permute-done | bytes 1179680 | tf_op jit(solution)/shard_map/ppermute | solution.py:442
  314.4 7.1 %shard_map.154.m_ref.refs_0_ = bf16[768,1536]{1,0:T(8,128)(2,1)} custom-call(s32[2]{0:T(128)} %pad_add_fusion._.half_ref, f32[768,1]{1,0:T(8,128)} %broadcast_in_dim.15.s_ref, bf16[768,1536]{1,0:T(8,128)(2,1)} %get-tuple-element.100.refs_0_, bf16[768,1536]{1,0:T(8,128)(2,1)} %collective-permute-done.26.refs_1_, bf16[768,768]{1,0:T(8,128)(2,1)} %shard_map.148.refs_2_, ...), custom_call_target="tpu_custom_call" | custom-call | bytes 10618368 | tf_op jit(solution)/shard_map/pallas_call | solution.py:53
  321.5 1.9 fusion.13
  327.7 17.3 %shard_map.155 = bf16[768,2048]{1,0:T(8,128)(2,1)} custom-call(s32[2]{0:T(128)} %pad_add_fusion._.half_ref, bf16[768,1536]{1,0:T(8,128)(2,1)} %shard_map.154.m_ref.refs_0_, bf16[768,1536]{1,0:T(8,128)(2,1)} %copy-done, bf16[2048,1536]{1,0:T(8,128)(2,1)} %get-tuple-element.103.wm_ref, bf16[2048,1536]{1,0:T(8,128)(2,1)} %get-tuple-element.104.wo_ref, ...), custom_call_target="tpu_custom_call" | custom-call | flops 9663676416 | bytes 23592960 | tf_op jit(solution)/shard_map/pallas_call | solution.py:53
  350.2 8.2 %collective-permute-done.37 = bf16[96,2048]{1,0:T(8,128)(2,1)S(1)} collective-permute-done((bf16[96,2048]{1,0:T(8,128)(2,1)S(1)}, bf16[96,2048]{1,0:T(8,128)(2,1)S(1)}, u32[]{:S(2)}, u32[]{:S(2)}) %collective-permute-start.37) | collective-permute-done | bytes 393248 | tf_op jit(solution)/shard_map/ppermute | solution.py:539
  360.0 6.8 %collective-permute-done.29 = bf16[96,2048]{1,0:T(8,128)(2,1)S(1)} collective-permute-done((bf16[96,2048]{1,0:T(8,128)(2,1)S(1)}, bf16[96,2048]{1,0:T(8,128)(2,1)S(1)}, u32[]{:S(2)}, u32[]{:S(2)}) %collective-permute-start.29) | collective-permute-done | bytes 393248 | tf_op jit(solution)/shard_map/ppermute | solution.py:539
  370.3 5.0 %collective-permute-done.38 = bf16[96,2048]{1,0:T(8,128)(2,1)S(1)} collective-permute-done((bf16[96,2048]{1,0:T(8,128)(2,1)S(1)}, bf16[96,2048]{1,0:T(8,128)(2,1)S(1)}, u32[]{:S(2)}, u32[]{:S(2)}) %collective-permute-start.38) | collective-permute-done | bytes 393248 | tf_op jit(solution)/shard_map/ppermute | solution.py:539
  377.6 6.1 %collective-permute-done.30 = bf16[96,2048]{1,0:T(8,128)(2,1)S(1)} collective-permute-done((bf16[96,2048]{1,0:T(8,128)(2,1)S(1)}, bf16[96,2048]{1,0:T(8,128)(2,1)S(1)}, u32[]{:S(2)}, u32[]{:S(2)}) %collective-permute-start.30) | collective-permute-done | bytes 393248 | tf_op jit(solution)/shard_map/ppermute | solution.py:539
  383.7 2.3 add_convert_fusion.7
  388.0 4.1 collective-permute-done.39
  395.3 19.5 %shard_map.156 = bf16[3584,2048]{1,0:T(8,128)(2,1)} custom-call(s32[2]{0:T(128)} %pad_add_fusion._.half_ref, bf16[768,1024]{1,0:T(8,128)(2,1)} %get-tuple-element.93.refs_0_, bf16[768,1024]{1,0:T(8,128)(2,1)} %collective-permute-done.24.refs_2_.refs_1_, bf16[768,768]{1,0:T(8,128)(2,1)} %shard_map.152.refs_4_.refs_2_, bf16[768,768]{1,0:T(8,128)(2,1)} %copy-done.34, ...), custom_call_target="tpu_custom_call" | custom-call | flops 11274289152 | bytes 23330816 | tf_op jit(solution)/shard_map/pallas_call | solution.py:53
  414.8 8.4 %shard_map.157 = (bf16[2048,3584]{1,0:T(8,128)(2,1)}, bf16[2048,3584]{1,0:T(8,128)(2,1)}) custom-call(s32[2]{0:T(128)} %pad_add_fusion._.half_ref, bf16[2048,768]{1,0:T(8,128)(2,1)} %shard_map.142.x_ref, bf16[768,1536]{1,0:T(8,128)(2,1)} %shard_map.154.m_ref.refs_0_, bf16[768,1536]{1,0:T(8,128)(2,1)} %copy-done, ...), custom_call_target="tpu_custom_call", output_to_operand_aliasing={{0}: (6, {}), {1}: (7, {})} | custom-call | flops 3221225472 | bytes 8912896 | tf_op jit(solution)/shard_map/pallas_call | solution.py:53
  424.8 8.2 %shard_map.158 = (bf16[2048,3584]{1,0:T(8,128)(2,1)}, bf16[2048,3584]{1,0:T(8,128)(2,1)}) custom-call(s32[2]{0:T(128)} %pad_add_fusion._.half_ref, bf16[2048,768]{1,0:T(8,128)(2,1)} %shard_map.142.x_ref, bf16[768,1536]{1,0:T(8,128)(2,1)} %shard_map.154.m_ref.refs_0_, bf16[768,1536]{1,0:T(8,128)(2,1)} %copy-done, ...), custom_call_target="tpu_custom_call", output_to_operand_aliasing={{0}: (6, {}), {1}: (7, {})} | custom-call | flops 3221225472 | bytes 8912896 | tf_op jit(solution)/shard_map/pallas_call | solution.py:53
  435.1 8.4 %shard_map.159 = (bf16[2048,3584]{1,0:T(8,128)(2,1)}, bf16[2048,3584]{1,0:T(8,128)(2,1)}) custom-call(s32[2]{0:T(128)} %pad_add_fusion._.half_ref, bf16[2048,768]{1,0:T(8,128)(2,1)} %shard_map.142.x_ref, bf16[768,1536]{1,0:T(8,128)(2,1)} %shard_map.154.m_ref.refs_0_, bf16[768,1536]{1,0:T(8,128)(2,1)} %copy-done, ...), custom_call_target="tpu_custom_call", output_to_operand_aliasing={{0}: (6, {}), {1}: (7, {})} | custom-call | flops 3221225472 | bytes 8912896 | tf_op jit(solution)/shard_map/pallas_call | solution.py:53
  444.7 2.5 collective-permute-done.47
  448.3 3.0 fusion.7
  (180 shorter events, 68.5 us)
Async XLA Ops:
  1.7 12.2 %collective-permute-start = (bf16[96,2048]{1,0:T(8,128)(2,1)S(1)}, bf16[96,2048]{1,0:T(8,128)(2,1)S(1)}, u32[]{:S(2)}, u32[]{:S(2)}) collective-permute-start(bf16[96,2048]{1,0:T(8,128)(2,1)S(1)} %fusion.9.refs_0_), channel_id=1, source_target_pairs={{0,8},{8,16},{16,24},{24,28},{28,20},{20,12},{12,4},{4,0},{1,9},{9... | collective-permute-start | bytes 1179656 | tf_op jit(solution)/shard_map/ppermute | solution.py:465
  4.9 10.6 %collective-permute-start.2 = (bf16[96,2048]{1,0:T(8,128)(2,1)S(1)}, bf16[96,2048]{1,0:T(8,128)(2,1)S(1)}, u32[]{:S(2)}, u32[]{:S(2)}) collective-permute-start(bf16[96,2048]{1,0:T(8,128)(2,1)S(1)} %fusion.9.refs_0_), channel_id=1, source_target_pairs={{8,0},{16,8},{24,16},{28,24},{20,28},{12,20},{4,12},{0,4},{9,1},{1... | collective-permute-start | bytes 1179656 | tf_op jit(solution)/shard_map/ppermute | solution.py:467
  24.6 13.8 %collective-permute-start.6 = (bf16[288,2048]{1,0:T(8,128)(2,1)}, bf16[288,2048]{1,0:T(8,128)(2,1)S(1)}, u32[]{:S(2)}, u32[]{:S(2)}) collective-permute-start(bf16[288,2048]{1,0:T(8,128)(2,1)} %get-tuple-element.63), channel_id=1, source_target_pairs={{0,1},{1,0},{2,3},{3,2},{4,5},{5,4},{6,7},{7,6},{8,9},{9,8},{10,11... | collective-permute-start | bytes 3538952 | tf_op jit(solution)/shard_map/ppermute | solution.py:438
  24.7 11.7 %collective-permute-start.1 = (bf16[96,2048]{1,0:T(8,128)(2,1)}, bf16[96,2048]{1,0:T(8,128)(2,1)S(1)}, u32[]{:S(2)}, u32[]{:S(2)}) collective-permute-start(bf16[96,2048]{1,0:T(8,128)(2,1)} %copy-done.2), channel_id=1, source_target_pairs={{0,8},{8,16},{16,24},{24,28},{28,20},{20,12},{12,4},{4,0},{1,9},{9... | collective-permute-start | bytes 1179656 | tf_op jit(solution)/shard_map/ppermute | solution.py:465
  26.3 11.7 %collective-permute-start.3 = (bf16[96,2048]{1,0:T(8,128)(2,1)}, bf16[96,2048]{1,0:T(8,128)(2,1)S(1)}, u32[]{:S(2)}, u32[]{:S(2)}) collective-permute-start(bf16[96,2048]{1,0:T(8,128)(2,1)} %copy-done.3), channel_id=1, source_target_pairs={{8,0},{16,8},{24,16},{28,24},{20,28},{12,20},{4,12},{0,4},{9,1},{1... | collective-permute-start | bytes 1179656 | tf_op jit(solution)/shard_map/ppermute | solution.py:467
  36.4 11.3 %collective-permute-start.4 = (bf16[96,2048]{1,0:T(8,128)(2,1)S(1)}, bf16[96,2048]{1,0:T(8,128)(2,1)S(1)}, u32[]{:S(2)}, u32[]{:S(2)}) collective-permute-start(bf16[96,2048]{1,0:T(8,128)(2,1)S(1)} %collective-permute-done.1.refs_0_.refs_3_), channel_id=1, source_target_pairs={{0,8},{8,16},{16,24},{24,28},{28,20},{20,12},{12,4},{4,0},{1,9},{9... | collective-permute-start | bytes 1179656 | tf_op jit(solution)/shard_map/ppermute | solution.py:465
  38.0 22.9 %collective-permute-start.5 = (bf16[96,2048]{1,0:T(8,128)(2,1)S(1)}, bf16[96,2048]{1,0:T(8,128)(2,1)S(1)}, u32[]{:S(2)}, u32[]{:S(2)}) collective-permute-start(bf16[96,2048]{1,0:T(8,128)(2,1)S(1)} %collective-permute-done.3.refs_1_.refs_4_), channel_id=1, source_target_pairs={{8,0},{16,8},{24,16},{28,24},{20,28},{12,20},{4,12},{0,4},{9,1},{1... | collective-permute-start | bytes 1179656 | tf_op jit(solution)/shard_map/ppermute | solution.py:467
  47.7 13.1 %collective-permute-start.7 = (bf16[96,2048]{1,0:T(8,128)(2,1)S(1)}, bf16[96,2048]{1,0:T(8,128)(2,1)S(1)}, u32[]{:S(2)}, u32[]{:S(2)}) collective-permute-start(bf16[96,2048]{1,0:T(8,128)(2,1)S(1)} %collective-permute-done.4.refs_2_.refs_5_), channel_id=1, source_target_pairs={{0,8},{8,16},{16,24},{24,28},{28,20},{20,12},{12,4},{4,0},{1,9},{9... | collective-permute-start | bytes 1179656 | tf_op jit(solution)/shard_map/ppermute | solution.py:465
  74.0 13.7 %collective-permute-start.12 = (bf16[480,2048]{1,0:T(8,128)(2,1)}, bf16[480,2048]{1,0:T(8,128)(2,1)}, u32[]{:S(2)}, u32[]{:S(2)}) collective-permute-start(bf16[480,2048]{1,0:T(8,128)(2,1)} %get-tuple-element.72), channel_id=1, source_target_pairs={{0,1},{1,0},{2,3},{3,2},{4,5},{5,4},{6,7},{7,6},{8,9},{9,8},{10,11... | collective-permute-start | bytes 5898248 | tf_op jit(solution)/shard_map/ppermute | solution.py:438
  74.0 11.5 %collective-permute-start.8 = (bf16[96,2048]{1,0:T(8,128)(2,1)S(1)}, bf16[96,2048]{1,0:T(8,128)(2,1)S(1)}, u32[]{:S(2)}, u32[]{:S(2)}) collective-permute-start(bf16[96,2048]{1,0:T(8,128)(2,1)S(1)} %copy-done.9), channel_id=1, source_target_pairs={{0,8},{8,16},{16,24},{24,28},{28,20},{20,12},{12,4},{4,0},{1,9},{9... | collective-permute-start | bytes 1179656 | tf_op jit(solution)/shard_map/ppermute | solution.py:465
  75.7 11.5 %collective-permute-start.9 = (bf16[96,2048]{1,0:T(8,128)(2,1)S(1)}, bf16[96,2048]{1,0:T(8,128)(2,1)S(1)}, u32[]{:S(2)}, u32[]{:S(2)}) collective-permute-start(bf16[96,2048]{1,0:T(8,128)(2,1)S(1)} %copy-done.9), channel_id=1, source_target_pairs={{8,0},{16,8},{24,16},{28,24},{20,28},{12,20},{4,12},{0,4},{9,1},{1... | collective-permute-start | bytes 1179656 | tf_op jit(solution)/shard_map/ppermute | solution.py:467
  76.3 60.5 %collective-permute-start.21 = (bf16[288,2048]{1,0:T(8,128)(2,1)S(1)}, bf16[288,2048]{1,0:T(8,128)(2,1)}, u32[]{:S(2)}, u32[]{:S(2)}) collective-permute-start(bf16[288,2048]{1,0:T(8,128)(2,1)S(1)} %copy-done.20), channel_id=1, source_target_pairs={{0,2},{1,3},{2,0},{3,1},{4,6},{5,7},{6,4},{7,5},{8,10},{9,11},{10,... | collective-permute-start | bytes 3538952 | tf_op jit(solution)/shard_map/ppermute | solution.py:442
  85.6 13.7 %collective-permute-start.10 = (bf16[96,2048]{1,0:T(8,128)(2,1)S(1)}, bf16[96,2048]{1,0:T(8,128)(2,1)S(1)}, u32[]{:S(2)}, u32[]{:S(2)}) collective-permute-start(bf16[96,2048]{1,0:T(8,128)(2,1)S(1)} %collective-permute-done.8.refs_1_.refs_5_), channel_id=1, source_target_pairs={{0,8},{8,16},{16,24},{24,28},{28,20},{20,12},{12,4},{4,0},{1,9},{9... | collective-permute-start | bytes 1179656 | tf_op jit(solution)/shard_map/ppermute | solution.py:465
  87.1 13.8 %collective-permute-start.11 = (bf16[96,2048]{1,0:T(8,128)(2,1)S(1)}, bf16[96,2048]{1,0:T(8,128)(2,1)S(1)}, u32[]{:S(2)}, u32[]{:S(2)}) collective-permute-start(bf16[96,2048]{1,0:T(8,128)(2,1)S(1)} %collective-permute-done.9.refs_2_.refs_6_), channel_id=1, source_target_pairs={{8,0},{16,8},{24,16},{28,24},{20,28},{12,20},{4,12},{0,4},{9,1},{1... | collective-permute-start | bytes 1179656 | tf_op jit(solution)/shard_map/ppermute | solution.py:467
  87.7 26.2 %collective-permute-start.16 = (f32[768]{0:T(1024)S(1)}, f32[768]{0:T(1024)S(1)}, u32[]{:S(2)}, u32[]{:S(2)}) collective-permute-start(f32[768]{0:T(1024)S(1)} %pad_maximum_fusion), channel_id=1, source_target_pairs={{0,1},{1,0},{2,3},{3,2},{4,5},{5,4},{6,7},{7,6},{8,9},{9,8},{10,11... | collective-permute-start | bytes 9224 | tf_op jit(solution)/shard_map/ppermute | solution.py:438
  99.3 12.7 %collective-permute-start.13 = (bf16[96,2048]{1,0:T(8,128)(2,1)S(1)}, bf16[96,2048]{1,0:T(8,128)(2,1)S(1)}, u32[]{:S(2)}, u32[]{:S(2)}) collective-permute-start(bf16[96,2048]{1,0:T(8,128)(2,1)S(1)} %collective-permute-done.10.refs_3_.refs_7_), channel_id=1, source_target_pairs={{0,8},{8,16},{16,24},{24,28},{28,20},{20,12},{12,4},{4,0},{1,9},{9... | collective-permute-start | bytes 1179656 | tf_op jit(solution)/shard_map/ppermute | solution.py:465
  100.9 25.5 %collective-permute-start.14 = (bf16[96,2048]{1,0:T(8,128)(2,1)S(1)}, bf16[96,2048]{1,0:T(8,128)(2,1)S(1)}, u32[]{:S(2)}, u32[]{:S(2)}) collective-permute-start(bf16[96,2048]{1,0:T(8,128)(2,1)S(1)} %collective-permute-done.11.refs_4_.refs_8_), channel_id=1, source_target_pairs={{8,0},{16,8},{24,16},{28,24},{20,28},{12,20},{4,12},{0,4},{9,1},{1... | collective-permute-start | bytes 1179656 | tf_op jit(solution)/shard_map/ppermute | solution.py:467
  112.1 14.4 %collective-permute-start.15 = (bf16[96,2048]{1,0:T(8,128)(2,1)S(1)}, bf16[96,2048]{1,0:T(8,128)(2,1)S(1)}, u32[]{:S(2)}, u32[]{:S(2)}) collective-permute-start(bf16[96,2048]{1,0:T(8,128)(2,1)S(1)} %collective-permute-done.13.refs_5_.refs_9_), channel_id=1, source_target_pairs={{0,8},{8,16},{16,24},{24,28},{28,20},{20,12},{12,4},{4,0},{1,9},{9... | collective-permute-start | bytes 1179656 | tf_op jit(solution)/shard_map/ppermute | solution.py:465
  114.0 3.6 collective-permute-start.17
  117.6 32.3 %collective-permute-start.19 = (bf16[768,1536]{1,0:T(8,128)(2,1)}, bf16[768,1536]{1,0:T(8,128)(2,1)}, u32[]{:S(2)}, u32[]{:S(2)}) collective-permute-start(bf16[768,1536]{1,0:T(8,128)(2,1)} %get-tuple-element.80), channel_id=1, source_target_pairs={{0,1},{1,0},{2,3},{3,2},{4,5},{5,4},{6,7},{7,6},{8,9},{9,8},{10,11... | collective-permute-start | bytes 7077896 | tf_op jit(solution)/shard_map/ppermute | solution.py:438
  136.3 3.8 collective-permute-start.18
  136.8 45.0 %collective-permute-start.22 = (bf16[480,2048]{1,0:T(8,128)(2,1)}, bf16[480,2048]{1,0:T(8,128)(2,1)S(1)}, u32[]{:S(2)}, u32[]{:S(2)}) collective-permute-start(bf16[480,2048]{1,0:T(8,128)(2,1)} %get-tuple-element.91.refs_2_), channel_id=1, source_target_pairs={{0,2},{1,3},{2,0},{3,1},{4,6},{5,7},{6,4},{7,5},{8,10},{9,11},{10,... | collective-permute-start | bytes 5898248 | tf_op jit(solution)/shard_map/ppermute | solution.py:442
  181.8 35.6 %collective-permute-start.23 = (bf16[768,1024]{1,0:T(8,128)(2,1)S(1)}, bf16[768,1024]{1,0:T(8,128)(2,1)}, u32[]{:S(2)}, u32[]{:S(2)}) collective-permute-start(bf16[768,1024]{1,0:T(8,128)(2,1)S(1)} %copy-done.19), channel_id=1, source_target_pairs={{0,2},{1,3},{2,0},{3,1},{4,6},{5,7},{6,4},{7,5},{8,10},{9,11},{10,... | collective-permute-start | bytes 4718600 | tf_op jit(solution)/shard_map/ppermute | solution.py:442
  190.5 3.2 collective-permute-start.20
  225.8 6.0 %collective-permute-start.25 = (bf16[768,2048]{1,0:T(8,128)(2,1)}, bf16[768,2048]{1,0:T(8,128)(2,1)}, u32[]{:S(2)}, u32[]{:S(2)}) collective-permute-start(bf16[768,2048]{1,0:T(8,128)(2,1)} %get-tuple-element.94.m_ref.refs_0_), channel_id=1, source_target_pairs={{0,1},{1,0},{2,3},{3,2},{4,5},{5,4},{6,7},{7,6},{8,9},{9,8},{10,11... | collective-permute-start | bytes 9437192 | tf_op jit(solution)/shard_map/ppermute | solution.py:438
  225.8 60.7 %collective-permute-start.24 = (bf16[768,1024]{1,0:T(8,128)(2,1)}, bf16[768,1024]{1,0:T(8,128)(2,1)}, u32[]{:S(2)}, u32[]{:S(2)}) collective-permute-start(bf16[768,1024]{1,0:T(8,128)(2,1)} %get-tuple-element.93.refs_0_), channel_id=1, source_target_pairs={{0,1},{1,0},{2,3},{3,2},{4,5},{5,4},{6,7},{7,6},{8,9},{9,8},{10,11... | collective-permute-start | bytes 4718600 | tf_op jit(solution)/shard_map/ppermute | solution.py:438
  226.3 53.3 %collective-permute-start.26 = (bf16[768,1536]{1,0:T(8,128)(2,1)S(1)}, bf16[768,1536]{1,0:T(8,128)(2,1)}, u32[]{:S(2)}, u32[]{:S(2)}) collective-permute-start(bf16[768,1536]{1,0:T(8,128)(2,1)S(1)} %copy-done.11), channel_id=1, source_target_pairs={{0,2},{1,3},{2,0},{3,1},{4,6},{5,7},{6,4},{7,5},{8,10},{9,11},{10,... | collective-permute-start | bytes 7077896 | tf_op jit(solution)/shard_map/ppermute | solution.py:442
  285.0 28.4 %collective-permute-start.35 = (bf16[768,768]{1,0:T(8,128)(2,1)S(1)}, bf16[768,768]{1,0:T(8,128)(2,1)S(1)}, u32[]{:S(2)}, u32[]{:S(2)}) collective-permute-start(bf16[768,768]{1,0:T(8,128)(2,1)S(1)} %copy-done.21), channel_id=1, source_target_pairs={{0,2},{1,3},{2,0},{3,1},{4,6},{5,7},{6,4},{7,5},{8,10},{9,11},{10,... | collective-permute-start | bytes 3538952 | tf_op jit(solution)/shard_map/ppermute | solution.py:442
  321.5 4.7 %collective-permute-start.36 = (bf16[768,1536]{1,0:T(8,128)(2,1)}, bf16[768,1536]{1,0:T(8,128)(2,1)S(1)}, u32[]{:S(2)}, u32[]{:S(2)}) collective-permute-start(bf16[768,1536]{1,0:T(8,128)(2,1)} %shard_map.154.m_ref.refs_0_), channel_id=1, source_target_pairs={{0,1},{1,0},{2,3},{3,2},{4,5},{5,4},{6,7},{7,6},{8,9},{9,8},{10,11... | collective-permute-start | bytes 7077896 | tf_op jit(solution)/shard_map/ppermute | solution.py:438
  323.5 23.4 %collective-permute-start.28 = (bf16[96,2048]{1,0:T(8,128)(2,1)}, bf16[96,2048]{1,0:T(8,128)(2,1)}, u32[]{:S(2)}, u32[]{:S(2)}) collective-permute-start(bf16[96,2048]{1,0:T(8,128)(2,1)} %get-tuple-element.128), channel_id=1, source_target_pairs={{8,0},{16,8},{24,16},{28,24},{20,28},{12,20},{4,12},{0,4},{9,1},{1... | collective-permute-start | bytes 1179656 | tf_op jit(solution)/shard_map/ppermute | solution.py:539
  323.9 36.1 %collective-permute-start.32 = (bf16[96,2048]{1,0:T(8,128)(2,1)S(1)}, bf16[96,2048]{1,0:T(8,128)(2,1)S(1)}, u32[]{:S(2)}, u32[]{:S(2)}) collective-permute-start(bf16[96,2048]{1,0:T(8,128)(2,1)S(1)} %get-tuple-element.129), channel_id=1, source_target_pairs={{0,8},{8,16},{16,24},{24,28},{28,20},{20,12},{12,4},{4,0},{1,9},{9... | collective-permute-start | bytes 1179656 | tf_op jit(solution)/shard_map/ppermute | solution.py:543
  346.3 12.0 %collective-permute-start.37 = (bf16[96,2048]{1,0:T(8,128)(2,1)S(1)}, bf16[96,2048]{1,0:T(8,128)(2,1)S(1)}, u32[]{:S(2)}, u32[]{:S(2)}) collective-permute-start(bf16[96,2048]{1,0:T(8,128)(2,1)S(1)} %get-tuple-element.122), channel_id=1, source_target_pairs={{8,0},{16,8},{24,16},{28,24},{20,28},{12,20},{4,12},{0,4},{9,1},{1... | collective-permute-start | bytes 1179656 | tf_op jit(solution)/shard_map/ppermute | solution.py:539
  348.1 18.7 %collective-permute-start.29 = (bf16[96,2048]{1,0:T(8,128)(2,1)S(1)}, bf16[96,2048]{1,0:T(8,128)(2,1)S(1)}, u32[]{:S(2)}, u32[]{:S(2)}) collective-permute-start(bf16[96,2048]{1,0:T(8,128)(2,1)S(1)} %add_convert_fusion.9), channel_id=1, source_target_pairs={{8,0},{16,8},{24,16},{28,24},{20,28},{12,20},{4,12},{0,4},{9,1},{1... | collective-permute-start | bytes 1179656 | tf_op jit(solution)/shard_map/ppermute | solution.py:539
  348.6 21.7 %collective-permute-start.41 = (bf16[96,2048]{1,0:T(8,128)(2,1)S(1)}, bf16[96,2048]{1,0:T(8,128)(2,1)S(1)}, u32[]{:S(2)}, u32[]{:S(2)}) collective-permute-start(bf16[96,2048]{1,0:T(8,128)(2,1)S(1)} %get-tuple-element.123), channel_id=1, source_target_pairs={{0,8},{8,16},{16,24},{24,28},{28,20},{20,12},{12,4},{4,0},{1,9},{9... | collective-permute-start | bytes 1179656 | tf_op jit(solution)/shard_map/ppermute | solution.py:543
  359.5 15.8 %collective-permute-start.38 = (bf16[96,2048]{1,0:T(8,128)(2,1)S(1)}, bf16[96,2048]{1,0:T(8,128)(2,1)S(1)}, u32[]{:S(2)}, u32[]{:S(2)}) collective-permute-start(bf16[96,2048]{1,0:T(8,128)(2,1)S(1)} %add_convert_fusion.4), channel_id=1, source_target_pairs={{8,0},{16,8},{24,16},{28,24},{20,28},{12,20},{4,12},{0,4},{9,1},{1... | collective-permute-start | bytes 1179656 | tf_op jit(solution)/shard_map/ppermute | solution.py:539
  368.2 15.5 %collective-permute-start.30 = (bf16[96,2048]{1,0:T(8,128)(2,1)S(1)}, bf16[96,2048]{1,0:T(8,128)(2,1)S(1)}, u32[]{:S(2)}, u32[]{:S(2)}) collective-permute-start(bf16[96,2048]{1,0:T(8,128)(2,1)S(1)} %get-tuple-element.126), channel_id=1, source_target_pairs={{8,0},{16,8},{24,16},{28,24},{20,28},{12,20},{4,12},{0,4},{9,1},{1... | collective-permute-start | bytes 1179656 | tf_op jit(solution)/shard_map/ppermute | solution.py:539
  368.7 15.0 %collective-permute-start.33 = (bf16[96,2048]{1,0:T(8,128)(2,1)S(1)}, bf16[96,2048]{1,0:T(8,128)(2,1)S(1)}, u32[]{:S(2)}, u32[]{:S(2)}) collective-permute-start(bf16[96,2048]{1,0:T(8,128)(2,1)S(1)} %get-tuple-element.127), channel_id=1, source_target_pairs={{0,8},{8,16},{16,24},{24,28},{28,20},{20,12},{12,4},{4,0},{1,9},{9... | collective-permute-start | bytes 1179656 | tf_op jit(solution)/shard_map/ppermute | solution.py:543
  375.5 16.6 %collective-permute-start.39 = (bf16[96,2048]{1,0:T(8,128)(2,1)S(1)}, bf16[96,2048]{1,0:T(8,128)(2,1)S(1)}, u32[]{:S(2)}, u32[]{:S(2)}) collective-permute-start(bf16[96,2048]{1,0:T(8,128)(2,1)S(1)} %get-tuple-element.120), channel_id=1, source_target_pairs={{8,0},{16,8},{24,16},{28,24},{20,28},{12,20},{4,12},{0,4},{9,1},{1... | collective-permute-start | bytes 1179656 | tf_op jit(solution)/shard_map/ppermute | solution.py:539
  376.0 16.1 %collective-permute-start.42 = (bf16[96,2048]{1,0:T(8,128)(2,1)S(1)}, bf16[96,2048]{1,0:T(8,128)(2,1)S(1)}, u32[]{:S(2)}, u32[]{:S(2)}) collective-permute-start(bf16[96,2048]{1,0:T(8,128)(2,1)S(1)} %get-tuple-element.121), channel_id=1, source_target_pairs={{0,8},{8,16},{16,24},{24,28},{28,20},{20,12},{12,4},{4,0},{1,9},{9... | collective-permute-start | bytes 1179656 | tf_op jit(solution)/shard_map/ppermute | solution.py:543
  386.0 62.3 %collective-permute-start.34 = (bf16[96,2048]{1,0:T(8,128)(2,1)}, bf16[96,2048]{1,0:T(8,128)(2,1)}, u32[]{:S(2)}, u32[]{:S(2)}) collective-permute-start(bf16[96,2048]{1,0:T(8,128)(2,1)} %get-tuple-element.125), channel_id=1, source_target_pairs={{0,8},{8,16},{16,24},{24,28},{28,20},{20,12},{12,4},{4,0},{1,9},{9... | collective-permute-start | bytes 1179656 | tf_op jit(solution)/shard_map/ppermute | solution.py:543
  387.5 60.8 %collective-permute-start.31 = (bf16[96,2048]{1,0:T(8,128)(2,1)}, bf16[96,2048]{1,0:T(8,128)(2,1)}, u32[]{:S(2)}, u32[]{:S(2)}) collective-permute-start(bf16[96,2048]{1,0:T(8,128)(2,1)} %get-tuple-element.124), channel_id=1, source_target_pairs={{8,0},{16,8},{24,16},{28,24},{20,28},{12,20},{4,12},{0,4},{9,1},{1... | collective-permute-start | bytes 1179656 | tf_op jit(solution)/shard_map/ppermute | solution.py:539
  393.2 29.9 %collective-permute-start.43 = (bf16[96,2048]{1,0:T(8,128)(2,1)}, bf16[96,2048]{1,0:T(8,128)(2,1)S(1)}, u32[]{:S(2)}, u32[]{:S(2)}) collective-permute-start(bf16[96,2048]{1,0:T(8,128)(2,1)} %get-tuple-element.119), channel_id=1, source_target_pairs={{0,8},{8,16},{16,24},{24,28},{28,20},{20,12},{12,4},{4,0},{1,9},{9... | collective-permute-start | bytes 1179656 | tf_op jit(solution)/shard_map/ppermute | solution.py:543
  394.8 28.4 %collective-permute-start.40 = (bf16[96,2048]{1,0:T(8,128)(2,1)}, bf16[96,2048]{1,0:T(8,128)(2,1)}, u32[]{:S(2)}, u32[]{:S(2)}) collective-permute-start(bf16[96,2048]{1,0:T(8,128)(2,1)} %get-tuple-element.118), channel_id=1, source_target_pairs={{8,0},{16,8},{24,16},{28,24},{20,28},{12,20},{4,12},{0,4},{9,1},{1... | collective-permute-start | bytes 1179656 | tf_op jit(solution)/shard_map/ppermute | solution.py:539
  424.8 8.8 %collective-permute-start.44 = (f32[96]{0:T(128)S(1)}, f32[96]{0:T(128)S(1)}, u32[]{:S(2)}, u32[]{:S(2)}) collective-permute-start(f32[96]{0:T(128)S(1)} %get-tuple-element.117), channel_id=1, source_target_pairs={{0,1},{1,0},{2,3},{3,2},{4,5},{5,4},{6,7},{7,6},{8,9},{9,8},{10,11... | collective-permute-start | bytes 1160 | tf_op jit(solution)/shard_map/ppermute | solution.py:438
  433.1 10.4 %collective-permute-start.46 = (f32[2048]{0:T(1024)S(1)}, f32[2048]{0:T(1024)S(1)}, u32[]{:S(2)}, u32[]{:S(2)}) collective-permute-start(f32[2048]{0:T(1024)S(1)} %get-tuple-element.116), channel_id=1, source_target_pairs={{0,4},{4,0},{8,12},{12,8},{16,20},{20,16},{24,28},{28,24},{1,5},{5... | collective-permute-start | bytes 24584 | tf_op jit(solution)/shard_map/ppermute | solution.py:578
  433.6 11.1 %collective-permute-start.45 = (f32[96]{0:T(128)S(1)}, f32[96]{0:T(128)S(1)}, u32[]{:S(2)}, u32[]{:S(2)}) collective-permute-start(f32[96]{0:T(128)S(1)} %add.94), channel_id=1, source_target_pairs={{0,2},{1,3},{2,0},{3,1},{4,6},{5,7},{6,4},{7,5},{8,10},{9,11},{10,... | collective-permute-start | bytes 1160 | tf_op jit(solution)/shard_map/ppermute | solution.py:442
  443.5 3.7 collective-permute-start.47
  447.2 4.5 %collective-permute-start.48 = (f32[2048]{0:T(1024)S(1)}, f32[2048]{0:T(1024)S(1)}, u32[]{:S(2)}, u32[]{:S(2)}) collective-permute-start(f32[2048]{0:T(1024)S(1)} %add.98), channel_id=1, source_target_pairs={{0,16},{4,20},{8,24},{12,28},{16,0},{20,4},{24,8},{28,12},{1,17},{... | collective-permute-start | bytes 24584 | tf_op jit(solution)/shard_map/ppermute | solution.py:578
  (36 other events, 347.1 us)
